TPU v7x, 32 devices: a whole 2x2x4 slice. The times are simulated.
32 devices in a mesh: rep: 8 (over y, x, core), zero: 4 (over z).
Axes of the slice: x: 2, y: 2, z: 4, core: 2. Of those that a mesh axis runs over, the one named last changes fastest.
Arguments:
- grads: bfloat16 [8, 4, 4194304], P('rep', 'zero'), may hold values from -6 to 6
- master: float32 [8, 4194304], P('rep', 'zero'), may hold values from -6 to 6
- moment_one: float32 [8, 4194304], P('rep', 'zero'), may hold values from -0.4375 to 0.4375
- moment_two: float32 [8, 4194304], P('rep', 'zero'), may hold values from 0.0001 to 0.01
- step_index: int32 [1], replicated, may hold values from 0 to 999
Outputs:
- master_out: float32 [8, 4194304], P('rep', 'zero')
- moment_one_out: float32 [8, 4194304], P('rep', 'zero')
- moment_two_out: float32 [8, 4194304], P('rep', 'zero')
- params_out: bfloat16 [8, 4194304], P('rep')
All inputs are finite; a program needn't handle non-finite values.
Results may differ from a plain program's by a relative error of at most 0.0075.
Values may be sent and summed in bfloat16 or wider, within the bound.
No kernel may reach another device: no remote copies, remote signals or barrier semaphores. Data moves between devices by JAX's collectives and lax.ppermute only.
A program may use at most 192 MiB of HBM per device.

v0:
```python
import jax
import jax.numpy as jnp
from jax import lax
from jax.sharding import PartitionSpec as P


def swapped(value, axis, apart):
    mask = 2**apart
    pairs = [(source, source ^ mask) for source in range(lax.axis_size(axis))]
    return lax.ppermute(value, axis, pairs)


def partner_values(values, tstep):
    nbits = lax.axis_size("rep").bit_length() - 1
    bit = tstep % nbits
    result = jnp.zeros_like(values)
    for level in range(nbits):
        other = swapped(values, "rep", level)
        result = jnp.where(bit == level, other, result)
    return result


def shards(grads, master, moment_one, moment_two, step_index):
    loop_size = lax.axis_size("zero")
    terms = grads[0, 0].astype(jnp.float32)
    g = (
        lax.psum_scatter(
            terms.astype(jnp.bfloat16), "zero", scatter_dimension=0, tiled=True
        ).astype(jnp.float32)
        / loop_size
    )
    g = g[None, :]
    tstep = step_index[0]
    count = (tstep + 1).astype(jnp.float32)
    m_new = 0.9 * moment_one + 0.1 * g
    v_new = 0.999 * moment_two + 0.001 * g * g
    corr_one = 1.0 - jnp.power(jnp.float32(0.9), count)
    corr_two = 1.0 - jnp.power(jnp.float32(0.999), count)
    fresh = master - 0.02 * (m_new / corr_one / (jnp.sqrt(v_new / corr_two) + 1e-08) + 0.1 * master)
    averaged = 0.5 * (fresh + partner_values(fresh, tstep))
    whole = lax.all_gather(averaged.astype(jnp.bfloat16), "zero", axis=1, tiled=True)
    return (averaged, m_new, v_new, whole)


def solution(mesh):
    return jax.shard_map(
        shards,
        mesh=mesh,
        in_specs=(
            P("rep", "zero", None),
            P("rep", "zero"),
            P("rep", "zero"),
            P("rep", "zero"),
            P(),
        ),
        out_specs=(P("rep", "zero"), P("rep", "zero"), P("rep", "zero"), P("rep", None)),
        check_vma=False,
    )
```

profile of v0, /device:TPU:0, one launch (start us, length us, event | category | flops | bytes accessed | tf_op | source)
XLA Modules:
  0.0 927.4 jit_solution(12522624360998154430)
XLA Ops:
  7.2 0.0 all-reduce.3.cloned.1.call-start
  7.2 178.5 %reduce = bf16[4194304]{0:T(1024)(128)(2,1)} reduce(bf16[1,1,4194304]{2,1,0:T(2,128)(2,1)} %param.5, bf16[]{:T(256)} %constant.59), dimensions={0,1}, to_apply=%param.5.reduce_sub_computation | reduce | bytes 16777218 | tf_op args[0]
  185.7 0.0 copy-start.2
  185.7 0.0 all-reduce.3.cloned.1.call-update
  185.7 0.2 all-gather.2.cloned.1.call-start
  186.7 0.0 copy-done.2
  186.7 0.6 dynamic-slice
  187.9 291.5 %all-reduce.3.cloned.1.call-done = bf16[4194304]{0:T(1024)(128)(2,1)} async-done(((bf16[4194304]{0:T(1024)(128)(2,1)}), bf16[4194304]{0:T(1024)(128)(2,1)}) %all-reduce.3.cloned.1.call-update) | async-done | bytes 8388624
  479.4 0.0 copy-start
  479.4 0.0 copy-start.1
  479.4 2.4 convert_multiply_fusion.2
  481.9 0.4 copy-done
  482.3 1.3 copy-done.1
  483.5 24.8 %multiply_subtract_fusion = (f32[1,1048576]{1,0:T(1,128)}, f32[1,1048576]{1,0:T(1,128)}, f32[1,1048576]{1,0:T(1,128)}) fusion(f32[1,1048576]{1,0:T(1,128)S(1)} %copy-done, f32[]{:T(128)} %bitcast.4, f32[]{:T(128)} %bitcast.2, f32[1,1048576]{1,0:T(1,128)S(1)} %bitcast.7, f32[1,1048576]{1,0:T(1,128)S(1)} %copy-done.1, f32[1,1048576]{1,0:T(1,128)S(1)} %bitcast.6, ...), kind=kLoop, calls=%fused_computation.9 | loop fusion | flops 12582912 | bytes 33554440 | tf_op jit(solution)/shard_map/sub | solution.py:39
  508.3 0.0 collective-permute-start.2
  508.3 1.5 collective-permute-start.1
  509.8 1.5 collective-permute-start
  511.3 4.6 collective-permute-done.2
  515.8 85.8 %collective-permute-done.1 = f32[1,1048576]{1,0:T(1,128)} collective-permute-done((f32[1,1048576]{1,0:T(1,128)}, f32[1,1048576]{1,0:T(1,128)}, u32[]{:S(2)}, u32[]{:S(2)}) %collective-permute-start.1) | collective-permute-done | bytes 4194336 | tf_op jit(solution)/shard_map/ppermute | solution.py:10
  601.6 1.2 collective-permute-done
  602.8 12.9 %fusion.3 = (bf16[1,1048576]{1,0:T(2,128)(2,1)}, f32[1,1048576]{1,0:T(1,128)}) fusion(f32[1,1048576]{1,0:T(1,128)} %get-tuple-element.6, f32[1,1048576]{1,0:T(1,128)} %collective-permute-done, f32[1,1048576]{1,0:T(1,128)} %collective-permute-done.1, f32[1,1048576]{1,0:T(1,128)} %collective-permute-done.2, pred[]{:T(512)S(6)} %eq.13, pred[]{:T(512)S(6)} %eq.12, ...), kind=kLoop, calls=%fused_computation.12 | loop fusion | flops 6291456 | bytes 23068676 | tf_op jit(solution)/shard_map/convert_element_type | solution.py:41
  615.7 0.0 all-gather.2.cloned.1.call-update
  615.7 285.0 %all-gather.2.cloned.1.call-done = bf16[1,4194304]{1,0:T(2,128)(2,1)} async-done(((bf16[1,1048576]{1,0:T(2,128)(2,1)}), bf16[1,4194304]{1,0:T(2,128)(2,1)}) %all-gather.2.cloned.1.call-update) | async-done | bytes 8388624 | tf_op jit(solution)/shard_map/all_gather | solution.py:41
  900.7 19.8 %copy.12 = bf16[1,4194304]{1,0:T(2,128)(2,1)} copy(bf16[1,4194304]{1,0:T(2,128)(2,1)} %all-gather.2.cloned.1.call-done) | data formatting | bytes 16777216
Async XLA Ops:
  7.2 472.3 %all-reduce.3.cloned.1.call-start = ((), (), s32[]{:S(2)}) async-start(), calls=%async_computation.1 | async-start | bytes 16777216
  185.7 1.0 copy-start.2
  185.7 715.0 %all-gather.2.cloned.1.call-start = ((), (), s32[]{:S(2)}) async-start(), calls=%async_computation | async-start | bytes 20971520 | tf_op jit(solution)/shard_map/all_gather | solution.py:41
  479.4 2.8 copy-start
  479.4 4.1 copy-start.1
  508.3 7.5 collective-permute-start.2
  508.3 93.3 %collective-permute-start.1 = (f32[1,1048576]{1,0:T(1,128)}, f32[1,1048576]{1,0:T(1,128)}, u32[]{:S(2)}, u32[]{:S(2)}) collective-permute-start(f32[1,1048576]{1,0:T(1,128)} %get-tuple-element.6), channel_id=1, source_target_pairs={{0,8},{4,12},{8,0},{12,4},{16,24},{20,28},{24,16},{28,20},{1,9},{5... | collective-permute-start | bytes 12582920 | tf_op jit(solution)/shard_map/ppermute | solution.py:10
  509.8 93.0 %collective-permute-start = (f32[1,1048576]{1,0:T(1,128)}, f32[1,1048576]{1,0:T(1,128)}, u32[]{:S(2)}, u32[]{:S(2)}) collective-permute-start(f32[1,1048576]{1,0:T(1,128)} %get-tuple-element.6), channel_id=1, source_target_pairs={{0,16},{4,20},{8,24},{12,28},{16,0},{20,4},{24,8},{28,12},{1,17},{... | collective-permute-start | bytes 12582920 | tf_op jit(solution)/shard_map/ppermute | solution.py:10
Sparse Core Ops, SparseCore 0:
  185.8 293.5 all-reduce.2
  615.8 284.8 all-gather.1
where the time goes:
time: 928 us; the launch traced here: 927 us
  waiting for transfers between devices  668 us (72%)
  other arithmetic  219 us (24%)
  local copies, waits for them, and re-layouts  22.1 us (2%)
  between operations  15.4 us (2%)
    unnamed x3, waiting for transfers between devices  292 us
    all_gather x1, waiting for transfers between devices, shards(): lax.all_gather(averaged.astype(jnp.bfloat16), 'zero', axis=1, tiled=True)  285 us
    unnamed x1, other arithmetic  178 us
    ppermute x3, waiting for transfers between devices, swapped(): return lax.ppermute(value, axis, pairs)  91.5 us
    sub x1, other arithmetic, shards(): master - 0.02 * (m_new / corr_one / (jnp.sqrt(v_new / corr_two) + 1e-08)...  24.8 us
    unnamed x8, local copies, waits for them, and re-layouts  22.1 us
  transfers between devices with their start and end apart: 5, of which 5 were waited for; matrix products, arithmetic and copies ran while one was open for 0% of the time, Pallas kernels for 0%

commit v1 on v0

v1 whole, which is shorter than its diff:
```python
import functools

import jax
import jax.numpy as jnp
from jax import lax
from jax.experimental import pallas as pl
from jax.experimental.pallas import tpu as pltpu
from jax.sharding import PartitionSpec as P

LANES = 128
CUTS = (3, 3, 2)
UNITS = 8
OUTER = ((0, 1), (3, 2))
MIDDLE = ((1, 2), (2, 1))
INNER = ((1, 0), (2, 3))
bf16 = jnp.bfloat16
f32 = jnp.float32
ANY = pl.BlockSpec(memory_space=pl.ANY)


def send(value, pairs):
    return lax.ppermute(value, "zero", list(pairs))


def swapped(value, apart):
    mask = 2**apart
    return lax.ppermute(value, "rep", [(r, r ^ mask) for r in range(lax.axis_size("rep"))])


def block_of(start, size):
    rows = 2048
    while start % rows or size % rows:
        rows //= 2
    return rows


def far(z, p):
    return jnp.where(z < 2, 3 - p, p)


def call(body, name, zero, grid, ins, specs, outs, out_specs, alias=(), after=(), cost=0):
    extra = [ANY] * len(after)
    count = len(specs)

    def kernel(zs, *refs):
        body(zs, *refs[:count], *refs[count + len(after) :])

    return pl.pallas_call(
        kernel,
        name=name,
        out_shape=outs,
        grid_spec=pltpu.PrefetchScalarGridSpec(
            num_scalar_prefetch=1,
            grid=grid,
            in_specs=list(specs) + extra,
            out_specs=out_specs,
        ),
        input_output_aliases={a + 1: b for a, b in alias},
        cost_estimate=pl.CostEstimate(flops=cost, bytes_accessed=cost, transcendentals=0),
    )(zero, *ins, *after)


def pack_outer(zs, g, o):
    o[0] = g[0].reshape(o.shape[1:])


def add_first(zs, r, g, o):
    own = g[0].astype(f32).reshape(o.shape[1:])
    o[0] = (r[0].astype(f32) + own).astype(bf16)


def adam_body(zs, g, re, rm, ri, m, v, w, sc, *rest):
    mo, vo, fr, fb = rest[-4:]
    shape = fr.shape
    total = g[0].astype(f32).reshape(shape)
    total = total + re[0].astype(f32) + rm[0].astype(f32) + ri[0].astype(f32)
    grad = total * 0.25
    m_new = 0.9 * m[...].reshape(shape) + 0.1 * grad
    v_new = 0.999 * v[...].reshape(shape) + 0.001 * grad * grad
    mo[...] = m_new.reshape(mo.shape)
    vo[...] = v_new.reshape(vo.shape)
    old = w[...].reshape(shape)
    root = jnp.sqrt(v_new * sc[1]) + 1e-08
    fresh = old - 0.02 * (m_new * sc[0] / root + 0.1 * old)
    fr[...] = fresh
    fb[...] = fresh.astype(bf16)


def mean_body(zs, fr, *rest):
    nbits = len(rest) - 2 if len(rest) < 6 else len(rest) - 3
    others = rest[:nbits]
    wo, ab = rest[-2:]
    bit = zs[1]
    for level in range(nbits):

        @pl.when(bit == level)
        def _(level=level):
            avg = 0.5 * (fr[...] + others[level][...].astype(f32))
            wo[...] = avg.reshape(wo.shape)
            ab[...] = avg.astype(bf16)


def spread_body(zs, own, *rest):
    near, ends, o = rest[:3], rest[3:6], rest[-1]
    slot = pl.program_id(0)
    z = zs[0]
    inner = (z == 1) | (z == 2)

    @pl.when(slot == 0)
    def _():
        o[...] = own[...].reshape(o.shape)

    for k in range(3):

        @pl.when((slot == k + 1) & inner)
        def _(k=k):
            o[...] = near[k][...].reshape(o.shape)

        @pl.when((slot == k + 1) & ~inner)
        def _(k=k):
            o[...] = ends[k][...].reshape(o.shape)


def slot_shard(z, slot):
    inner = jnp.where(
        z == 1,
        jnp.where(slot == 1, 0, slot),
        jnp.where(slot == 1, 3, 3 - slot),
    )
    end = jnp.where(z == 0, slot, 3 - slot)
    other = jnp.where((z == 1) | (z == 2), inner, end)
    return jnp.where(slot == 0, z, other)


def line_step(grads, master, moment_one, moment_two, step_index):
    size = master.shape[1]
    rows = size // LANES
    nbits = lax.axis_size("rep").bit_length() - 1
    z = lax.axis_index("zero").astype(jnp.int32)
    tstep = step_index[0]
    count = (tstep + 1).astype(f32)
    scale = jnp.stack(
        [
            1.0 / (1.0 - jnp.power(f32(0.9), count)),
            1.0 / (1.0 - jnp.power(f32(0.999), count)),
        ]
    )
    scalars = jnp.stack([z, tstep % nbits])
    unit = rows // UNITS
    m_all = v_all = w_all = p_all = None
    start = 0
    packs, parts = [], []
    for cut in CUTS:
        n = cut * unit
        R = block_of(start, n)
        parts.append((start, n, R))
        start += n

    def grad_spec(index, R):
        return pl.BlockSpec((1, 1, R * LANES), index)

    def chunk_kernels(start, n, R):
        nb, base, per = n // R, start // R, rows // R
        row = lambda f: pl.BlockSpec((R, LANES), f)
        lead = lambda f: pl.BlockSpec((1, R, LANES), f)
        flat = pl.BlockSpec((1, R * LANES), lambda i, zs: (0, base + i))
        return nb, base, per, row, lead, flat

    def outer(part, after):
        start, n, R = part
        nb, base, per, row, lead, flat = chunk_kernels(*part)
        packed = call(
            pack_outer, "pack_outer", scalars, (3, nb), (grads,),
            [grad_spec(lambda p, i, zs: (0, 0, far(zs[0], p) * per + base + i), R)],
            jax.ShapeDtypeStruct((3, n, LANES), bf16),
            lead(lambda p, i, zs: (p, i, 0)), after=after, cost=3 * n * LANES * 6,
        )
        return send(packed, OUTER)

    def reduce_rest(part, r_out):
        start, n, R = part
        nb, base, per, row, lead, flat = chunk_kernels(*part)
        summed = call(
            add_first, "sum_middle", scalars, (2, nb), (r_out, grads),
            [lead(lambda p, i, zs: (p, i, 0)),
             grad_spec(lambda p, i, zs: (0, 0, far(zs[0], p) * per + base + i), R)],
            jax.ShapeDtypeStruct((2, n, LANES), bf16),
            lead(lambda p, i, zs: (p, i, 0)), cost=2 * n * LANES * 8,
        )
        r_mid = send(summed, MIDDLE)
        last = call(
            add_first, "sum_inner", scalars, (1, nb), (r_mid, grads),
            [lead(lambda p, i, zs: (0, i, 0)),
             grad_spec(lambda p, i, zs: (0, 0, far(zs[0], 3) * per + base + i), R)],
            jax.ShapeDtypeStruct((1, n, LANES), bf16),
            lead(lambda p, i, zs: (0, i, 0)), cost=n * LANES * 8,
        )
        r_in = send(last, INNER)
        return r_mid, r_in

    def adam(part, r_out, r_mid, r_in):
        nonlocal m_all, v_all
        start, n, R = part
        nb, base, per, row, lead, flat = chunk_kernels(*part)
        whole = jax.ShapeDtypeStruct((1, size), f32)
        ins = [grads, r_out, r_mid, r_in, moment_one, moment_two, master, scale]
        specs = [
            grad_spec(lambda i, zs: (0, 0, zs[0] * per + base + i), R),
            lead(lambda i, zs: (2, i, 0)),
            lead(lambda i, zs: (1, i, 0)),
            lead(lambda i, zs: (0, i, 0)),
            flat, flat, flat,
            pl.BlockSpec(memory_space=pltpu.SMEM),
        ]
        alias = ()
        if m_all is not None:
            alias = ((len(ins), 0), (len(ins) + 1, 1))
            ins += [m_all, v_all]
            specs += [ANY, ANY]
        m_all, v_all, fresh, fresh16 = call(
            adam_body, "adam", scalars, (nb,), ins, specs,
            (whole, whole, jax.ShapeDtypeStruct((n, LANES), f32),
             jax.ShapeDtypeStruct((n, LANES), bf16)),
            (flat, flat, row(lambda i, zs: (i, 0)), row(lambda i, zs: (i, 0))),
            alias=alias, cost=n * LANES * 40,
        )
        return fresh, fresh16

    def mean(part, fresh, others):
        nonlocal w_all
        start, n, R = part
        nb, base, per, row, lead, flat = chunk_kernels(*part)
        ins = [fresh, *others]
        pick = lambda level: row(lambda i, zs: (jnp.where(zs[1] == level, i, 0), 0))
        specs = [row(lambda i, zs: (i, 0))] + [pick(k) for k in range(len(others))]
        alias = ()
        if w_all is not None:
            alias = ((len(ins), 0),)
            ins.append(w_all)
            specs.append(ANY)
        body = functools.partial(mean_wrap, len(others))
        w_all, avg = call(
            body, "mean", scalars, (nb,), ins, specs,
            (jax.ShapeDtypeStruct((1, size), f32), jax.ShapeDtypeStruct((n, LANES), bf16)),
            (flat, row(lambda i, zs: (i, 0))), alias=alias, cost=n * LANES * 14,
        )
        return avg

    def spread(part, avg):
        nonlocal p_all
        start, n, R = part
        nb, base, per, row, lead, flat = chunk_kernels(*part)
        c1 = send(avg, OUTER)
        m1 = send(avg, MIDDLE)
        a1 = send(avg, INNER)
        m2 = send(c1, MIDDLE)
        a2 = send(m1, INNER)
        a3 = send(m2, INNER)
        ins = [avg, c1, m1, m2, a1, a2, a3]
        inner = lambda zs: (zs[0] == 1) | (zs[0] == 2)
        specs = [row(lambda s, i, zs: (jnp.where(s == 0, i, 0), 0))]
        for k in range(3):
            specs.append(row(lambda s, i, zs, k=k: (jnp.where((s == k + 1) & inner(zs), i, 0), 0)))
        for k in range(3):
            specs.append(row(lambda s, i, zs, k=k: (jnp.where((s == k + 1) & ~inner(zs), i, 0), 0)))
        alias = ()
        if p_all is not None:
            alias = ((len(ins), 0),)
            ins.append(p_all)
            specs.append(ANY)
        per4 = per
        p_all = call(
            spread_body, "spread", scalars, (4, nb), ins, specs,
            jax.ShapeDtypeStruct((1, 4 * size), bf16),
            pl.BlockSpec((1, R * LANES), lambda s, i, zs: (0, slot_shard(zs[0], s) * per4 + base + i)),
            alias=alias, cost=4 * n * LANES * 6,
        )

    received = []
    after = ()
    for k, part in enumerate(parts):
        received.append(outer(part, after))
    for k, part in enumerate(parts):
        r_mid, r_in = reduce_rest(part, received[k])
        fresh, fresh16 = adam(part, received[k], r_mid, r_in)
        others = [swapped(fresh16, level) for level in range(nbits)]
        avg = mean(part, fresh, others)
        spread(part, avg)
    return (w_all, m_all, v_all, p_all)


def mean_wrap(nbits, zs, fr, *rest):
    others = rest[:nbits]
    wo, ab = rest[-2:]
    for level in range(nbits):

        @pl.when(zs[1] == level)
        def _(level=level):
            avg = 0.5 * (fr[...] + others[level][...].astype(f32))
            wo[...] = avg.reshape(wo.shape)
            ab[...] = avg.astype(bf16)


def plain_step(grads, master, moment_one, moment_two, step_index):
    loop_size = lax.axis_size("zero")
    nbits = lax.axis_size("rep").bit_length() - 1
    tstep = step_index[0]
    count = (tstep + 1).astype(f32)
    terms = grads.reshape(-1, LANES)
    g = lax.psum_scatter(terms, "zero", scatter_dimension=0, tiled=True).astype(f32)
    g = g.reshape(master.shape) / loop_size
    m_new = 0.9 * moment_one + 0.1 * g
    v_new = 0.999 * moment_two + 0.001 * g * g
    corr_one = 1.0 - jnp.power(f32(0.9), count)
    corr_two = 1.0 - jnp.power(f32(0.999), count)
    fresh = master - 0.02 * (m_new / corr_one / (jnp.sqrt(v_new / corr_two) + 1e-08) + 0.1 * master)
    other = jnp.zeros_like(fresh)
    for level in range(nbits):
        other = jnp.where(tstep % nbits == level, swapped(fresh, level), other)
    averaged = 0.5 * (fresh + other)
    whole = lax.all_gather(averaged.astype(bf16).reshape(-1, LANES), "zero", axis=0, tiled=True)
    return (averaged, m_new, v_new, whole.reshape(1, -1))


def shards(*args):
    if lax.axis_size("zero") == 4:
        return line_step(*args)
    return plain_step(*args)


def solution(mesh):
    return jax.shard_map(
        shards,
        mesh=mesh,
        in_specs=(
            P("rep", "zero", None),
            P("rep", "zero"),
            P("rep", "zero"),
            P("rep", "zero"),
            P(),
        ),
        out_specs=(P("rep", "zero"), P("rep", "zero"), P("rep", "zero"), P("rep", None)),
        check_vma=False,
    )
```

time: 928 us -> 415 us (0.45)
  waiting for transfers between devices: 668 us -> 238 us
  other arithmetic: 219 us -> 1.31 us
  Pallas kernels: 0 us -> 109 us
  starting transfers between devices: 3.21 us -> 55.9 us
  local copies, waits for them, and re-layouts: 22.1 us -> 7.08 us
  between operations: 15.4 us -> 1.88 us
    unnamed x3 -> x0, waiting for transfers between devices: 292 us -> none
    all_gather x1 -> x0, waiting for transfers between devices: 285 us -> none  [shards(): lax.all_gather(averaged.astype(jnp.bfloat16), 'zero', axis=1, tiled=True)]
    unnamed x1 -> x0, other arithmetic: 178 us -> none
    ppermute x3 -> x36, waiting for transfers between devices: 91.5 us -> 238 us  [the longest x27 229 us: send(): return lax.ppermute(value, 'zero', list(pairs))]
    pallas_call x0 -> x18, Pallas kernels: none -> 109 us  [call(): pl.pallas_call(kernel, name=name, out_shape=outs, grid_spec=pltpu.Prefetc...]
    ppermute x3 -> x36, starting transfers between devices: 2.95 us -> 55.9 us  [the longest x27 48.3 us: send(): return lax.ppermute(value, 'zero', list(pairs))]
    sub x1 -> x0, other arithmetic: 24.8 us -> none  [shards(): master - 0.02 * (m_new / corr_one / (jnp.sqrt(v_new / corr_two) + 1e-08)...]
    unnamed x8 -> x40, local copies, waits for them, and re-layouts: 22.1 us -> 7.08 us
  transfers between devices with their start and end apart: 5 -> 36, of which waited for: 5 -> 19; matrix products, arithmetic and copies ran while one was open for 0% -> 0% of each run, Pallas kernels for 0% -> 23%
where the time goes in v1:
time: 415 us; the launch traced here: 413 us
  waiting for transfers between devices  238 us (57%)
  Pallas kernels  109 us (26%)
  starting transfers between devices  55.9 us (13%)
  local copies, waits for them, and re-layouts  7.08 us (2%)
    ppermute x27, waiting for transfers between devices, send(): return lax.ppermute(value, 'zero', list(pairs))  229 us
    pallas_call x18, Pallas kernels, call(): pl.pallas_call(kernel, name=name, out_shape=outs, grid_spec=pltpu.Prefetc...  109 us
    ppermute x27, starting transfers between devices, send(): return lax.ppermute(value, 'zero', list(pairs))  48.3 us
    ppermute x9, waiting for transfers between devices, swapped(): lax.ppermute(value, 'rep', [(r, r ^ mask) for r in range(lax.axis_size('r...  9.08 us
  transfers between devices with their start and end apart: 36, of which 19 were waited for; matrix products, arithmetic and copies ran while one was open for 0% of the time, Pallas kernels for 23%

profile of v1, /device:TPU:0, one launch (start us, length us, event | category | flops | bytes accessed | tf_op | source)
XLA Modules:
  0.0 412.6 jit_solution(2229126374852698358)
XLA Ops:
  1.9 8.5 %pack_outer.5 = bf16[3,3072,128]{2,1,0:T(8,128)(2,1)} custom-call(s32[2]{0:T(128)} %pad_add_fusion.zs, bf16[1,1,4194304]{2,1,0:T(2,128)(2,1)} %refs_0_.11), custom_call_target="tpu_custom_call" | custom-call | flops 7077888 | bytes 7077888 | tf_op jit(solution)/shard_map/pack_outer/pallas_call | solution.py:48
  10.5 6.4 %collective-permute-start.6 = (bf16[3,3072,128]{2,1,0:T(8,128)(2,1)}, bf16[3,3072,128]{2,1,0:T(8,128)(2,1)}, u32[]{:S(2)}, u32[]{:S(2)}) collective-permute-start(bf16[3,3072,128]{2,1,0:T(8,128)(2,1)} %pack_outer.5), channel_id=1, source_target_pairs={{0,1},{3,2},{4,5},{7,6},{8,9},{11,10},{12,13},{15,14},{16,17},{19,... | collective-permute-start | bytes 7077896 | tf_op jit(solution)/shard_map/ppermute | solution.py:22
  16.8 8.5 %pack_outer.4 = bf16[3,3072,128]{2,1,0:T(8,128)(2,1)} custom-call(s32[2]{0:T(128)} %pad_add_fusion.zs, bf16[1,1,4194304]{2,1,0:T(2,128)(2,1)} %refs_0_.11), custom_call_target="tpu_custom_call" | custom-call | flops 7077888 | bytes 7077888 | tf_op jit(solution)/shard_map/pack_outer/pallas_call | solution.py:48
  26.8 5.2 %pack_outer.3 = bf16[3,2048,128]{2,1,0:T(8,128)(2,1)} custom-call(s32[2]{0:T(128)} %pad_add_fusion.zs, bf16[1,1,4194304]{2,1,0:T(2,128)(2,1)} %refs_0_.11), custom_call_target="tpu_custom_call" | custom-call | flops 4718592 | bytes 4718592 | tf_op jit(solution)/shard_map/pack_outer/pallas_call | solution.py:48
  32.0 2.5 collective-permute-start
  34.5 32.9 %collective-permute-done.6.refs_0_.refs_1_ = bf16[3,3072,128]{2,1,0:T(8,128)(2,1)} collective-permute-done((bf16[3,3072,128]{2,1,0:T(8,128)(2,1)}, bf16[3,3072,128]{2,1,0:T(8,128)(2,1)}, u32[]{:S(2)}, u32[]{:S(2)}) %collective-permute-start.6) | collective-permute-done | bytes 2359328 | tf_op jit(solution)/shard_map/ppermute | solution.py:22
  67.4 6.1 %sum_middle.5 = bf16[2,3072,128]{2,1,0:T(8,128)(2,1)} custom-call(s32[2]{0:T(128)} %pad_add_fusion.zs, bf16[3,3072,128]{2,1,0:T(8,128)(2,1)} %collective-permute-done.6.refs_0_.refs_1_, bf16[1,1,4194304]{2,1,0:T(2,128)(2,1)} %refs_0_.11), custom_call_target="tpu_custom_call" | custom-call | flops 6291456 | bytes 6291456 | tf_op jit(solution)/shard_map/sum_middle/pallas_call | solution.py:48
  73.5 1.8 collective-permute-start.7
  75.3 42.6 %collective-permute-done.3.refs_0_.refs_1_ = bf16[3,3072,128]{2,1,0:T(8,128)(2,1)S(1)} collective-permute-done((bf16[3,3072,128]{2,1,0:T(8,128)(2,1)}, bf16[3,3072,128]{2,1,0:T(8,128)(2,1)S(1)}, u32[]{:S(2)}, u32[]{:S(2)}) %collective-permute-start.3) | collective-permute-done | bytes 2359328 | tf_op jit(solution)/shard_map/ppermute | solution.py:22
  119.3 6.1 %sum_middle.4 = bf16[2,3072,128]{2,1,0:T(8,128)(2,1)} custom-call(s32[2]{0:T(128)} %pad_add_fusion.zs, bf16[3,3072,128]{2,1,0:T(8,128)(2,1)} %copy-done, bf16[1,1,4194304]{2,1,0:T(2,128)(2,1)} %refs_0_.11), custom_call_target="tpu_custom_call" | custom-call | flops 6291456 | bytes 6291456 | tf_op jit(solution)/shard_map/sum_middle/pallas_call | solution.py:48
  126.2 24.3 %collective-permute-done.refs_0_.refs_1_ = bf16[3,2048,128]{2,1,0:T(8,128)(2,1)} collective-permute-done((bf16[3,2048,128]{2,1,0:T(8,128)(2,1)}, bf16[3,2048,128]{2,1,0:T(8,128)(2,1)}, u32[]{:S(2)}, u32[]{:S(2)}) %collective-permute-start) | collective-permute-done | bytes 1572896 | tf_op jit(solution)/shard_map/ppermute | solution.py:22
  150.5 3.6 sum_middle.3
  154.9 4.1 sum_inner.5
  161.4 4.1 sum_inner.4
  167.6 16.4 %collective-permute-done.8.refs_3_ = bf16[1,3072,128]{2,1,0:T(8,128)(2,1)S(1)} collective-permute-done((bf16[1,3072,128]{2,1,0:T(8,128)(2,1)}, bf16[1,3072,128]{2,1,0:T(8,128)(2,1)S(1)}, u32[]{:S(2)}, u32[]{:S(2)}) %collective-permute-start.8) | collective-permute-done | bytes 786464 | tf_op jit(solution)/shard_map/ppermute | solution.py:22
  185.0 7.5 %adam.3 = (f32[1,1048576]{1,0:T(1,128)}, f32[1,1048576]{1,0:T(1,128)}, f32[3072,128]{1,0:T(8,128)}, bf16[3072,128]{1,0:T(8,128)(2,1)}) custom-call(s32[2]{0:T(128)} %pad_add_fusion.zs, bf16[1,1,4194304]{2,1,0:T(2,128)(2,1)} %refs_0_.11, bf16[3,3072,128]{2,1,0:T(8,128)(2,1)} %collective-permute-done.6.refs_0_.refs_1_, ...), custom_call_target="tpu_custom_call" | custom-call | flops 15728640 | bytes 15728640 | tf_op jit(solution)/shard_map/adam/pallas_call | solution.py:48
  193.6 3.1 sum_inner.3
  198.0 1.6 collective-permute-start.16
  199.5 1.5 collective-permute-start.17
  201.9 7.5 %adam.4 = (f32[1,1048576]{1,0:T(1,128)}, f32[1,1048576]{1,0:T(1,128)}, f32[3072,128]{1,0:T(8,128)}, bf16[3072,128]{1,0:T(8,128)(2,1)}) custom-call(s32[2]{0:T(128)} %pad_add_fusion.zs, bf16[1,1,4194304]{2,1,0:T(2,128)(2,1)} %refs_0_.11, bf16[3,3072,128]{2,1,0:T(8,128)(2,1)} %copy-done, ...), custom_call_target="tpu_custom_call", output_to_operand_aliasing={{0}: (9, {}), {1}: (10, {})} | custom-call | flops 15728640 | bytes 15728640 | tf_op jit(solution)/shard_map/adam/pallas_call | solution.py:48
  209.5 3.6 collective-permute-done.2.refs_3_
  213.1 1.5 collective-permute-start.13
  214.6 1.5 collective-permute-start.14
  216.1 5.9 %adam.5 = (f32[1,1048576]{1,0:T(1,128)}, f32[1,1048576]{1,0:T(1,128)}, f32[2048,128]{1,0:T(8,128)}, bf16[2048,128]{1,0:T(8,128)(2,1)}) custom-call(s32[2]{0:T(128)} %pad_add_fusion.zs, bf16[1,1,4194304]{2,1,0:T(2,128)(2,1)} %refs_0_.11, bf16[3,2048,128]{2,1,0:T(8,128)(2,1)} %collective-permute-done.refs_0_.refs_1_, ...), custom_call_target="tpu_custom_call", output_to_operand_aliasing={{0}: (9, {}), {1}: (10, {})} | custom-call | flops 10485760 | bytes 10485760 | tf_op jit(solution)/shard_map/adam/pallas_call | solution.py:48
  223.4 4.8 %mean.3 = (f32[1,1048576]{1,0:T(1,128)}, bf16[3072,128]{1,0:T(8,128)(2,1)}) custom-call(s32[2]{0:T(128)} %pad_add_fusion.zs, f32[3072,128]{1,0:T(8,128)} %get-tuple-element.30.refs_0_, bf16[3072,128]{1,0:T(8,128)(2,1)} %collective-permute-done.15.refs_1_, bf16[3072,128]{1,0:T(8,128)(2,1)} %copy-done.13, bf16[3072,128]{1,0:T(8,128)(2,1)} %collective-permute-done.17.refs_3_), custom_call_target="tpu_custom_call" | custom-call | flops 5505024 | bytes 5505024 | tf_op jit(solution)/shard_map/mean/pallas_call | solution.py:48
  228.2 7.3 %collective-permute-done.13.refs_2_ = bf16[3072,128]{1,0:T(8,128)(2,1)S(1)} collective-permute-done((bf16[3072,128]{1,0:T(8,128)(2,1)}, bf16[3072,128]{1,0:T(8,128)(2,1)S(1)}, u32[]{:S(2)}, u32[]{:S(2)}) %collective-permute-start.13) | collective-permute-done | bytes 786464 | tf_op jit(solution)/shard_map/ppermute | solution.py:27
  235.5 4.6 %collective-permute-start.30 = (bf16[3072,128]{1,0:T(8,128)(2,1)}, bf16[3072,128]{1,0:T(8,128)(2,1)S(1)}, u32[]{:S(2)}, u32[]{:S(2)}) collective-permute-start(bf16[3072,128]{1,0:T(8,128)(2,1)} %get-tuple-element.39.refs_0_), channel_id=1, source_target_pairs={{0,1},{3,2},{4,5},{7,6},{8,9},{11,10},{12,13},{15,14},{16,17},{19,... | collective-permute-start | bytes 2359304 | tf_op jit(solution)/shard_map/ppermute | solution.py:22
  241.0 4.8 %mean.4 = (f32[1,1048576]{1,0:T(1,128)}, bf16[3072,128]{1,0:T(8,128)(2,1)}) custom-call(s32[2]{0:T(128)} %pad_add_fusion.zs, f32[3072,128]{1,0:T(8,128)} %get-tuple-element.28.refs_0_, bf16[3072,128]{1,0:T(8,128)(2,1)} %copy-done.10, bf16[3072,128]{1,0:T(8,128)(2,1)} %copy-done.11, bf16[3072,128]{1,0:T(8,128)(2,1)} %copy-done.12, ...), custom_call_target="tpu_custom_call", output_to_operand_aliasing={{0}: (5, {})} | custom-call | flops 5505024 | bytes 5505024 | tf_op jit(solution)/shard_map/mean/pallas_call | solution.py:48
  247.6 3.6 mean.5
  251.2 4.3 %collective-permute-start.18 = (bf16[2048,128]{1,0:T(8,128)(2,1)}, bf16[2048,128]{1,0:T(8,128)(2,1)S(1)}, u32[]{:S(2)}, u32[]{:S(2)}) collective-permute-start(bf16[2048,128]{1,0:T(8,128)(2,1)} %get-tuple-element.37.refs_0_), channel_id=1, source_target_pairs={{0,1},{3,2},{4,5},{7,6},{8,9},{11,10},{12,13},{15,14},{16,17},{19,... | collective-permute-start | bytes 1572872 | tf_op jit(solution)/shard_map/ppermute | solution.py:22
  256.3 3.0 collective-permute-start.24
  259.2 1.5 collective-permute-start.19
  260.8 7.4 %collective-permute-done.18.refs_1_ = bf16[2048,128]{1,0:T(8,128)(2,1)S(1)} collective-permute-done((bf16[2048,128]{1,0:T(8,128)(2,1)}, bf16[2048,128]{1,0:T(8,128)(2,1)S(1)}, u32[]{:S(2)}, u32[]{:S(2)}) %collective-permute-start.18) | collective-permute-done | bytes 524320 | tf_op jit(solution)/shard_map/ppermute | solution.py:22
  270.2 1.6 collective-permute-start.25
  273.0 11.0 %collective-permute-done.24.refs_1_ = bf16[3072,128]{1,0:T(8,128)(2,1)S(1)} collective-permute-done((bf16[3072,128]{1,0:T(8,128)(2,1)}, bf16[3072,128]{1,0:T(8,128)(2,1)S(1)}, u32[]{:S(2)}, u32[]{:S(2)}) %collective-permute-start.24) | collective-permute-done | bytes 786464 | tf_op jit(solution)/shard_map/ppermute | solution.py:22
  284.0 1.5 collective-permute-start.26
  285.5 2.1 collective-permute-done.33.refs_4_
  290.3 1.5 collective-permute-start.20
  291.7 19.1 %collective-permute-done.27.refs_4_ = bf16[3072,128]{1,0:T(8,128)(2,1)S(1)} collective-permute-done((bf16[3072,128]{1,0:T(8,128)(2,1)}, bf16[3072,128]{1,0:T(8,128)(2,1)S(1)}, u32[]{:S(2)}, u32[]{:S(2)}) %collective-permute-start.27) | collective-permute-done | bytes 786464 | tf_op jit(solution)/shard_map/ppermute | solution.py:22
  314.7 12.9 %collective-permute-done.34.refs_5_ = bf16[3072,128]{1,0:T(8,128)(2,1)S(1)} collective-permute-done((bf16[3072,128]{1,0:T(8,128)(2,1)S(1)}, bf16[3072,128]{1,0:T(8,128)(2,1)S(1)}, u32[]{:S(2)}, u32[]{:S(2)}) %collective-permute-start.34) | collective-permute-done | bytes 786464 | tf_op jit(solution)/shard_map/ppermute | solution.py:22
  329.0 15.6 %collective-permute-done.35.refs_6_ = bf16[3072,128]{1,0:T(8,128)(2,1)S(1)} collective-permute-done((bf16[3072,128]{1,0:T(8,128)(2,1)S(1)}, bf16[3072,128]{1,0:T(8,128)(2,1)S(1)}, u32[]{:S(2)}, u32[]{:S(2)}) %collective-permute-start.35) | collective-permute-done | bytes 786464 | tf_op jit(solution)/shard_map/ppermute | solution.py:22
  346.7 9.9 %spread.3.refs_7_ = bf16[1,4194304]{1,0:T(2,128)(2,1)} custom-call(s32[2]{0:T(128)} %pad_add_fusion.zs, bf16[3072,128]{1,0:T(8,128)(2,1)} %get-tuple-element.39.refs_0_, bf16[3072,128]{1,0:T(8,128)(2,1)} %copy-done.4, bf16[3072,128]{1,0:T(8,128)(2,1)} %copy-done.5, bf16[3072,128]{1,0:T(8,128)(2,1)} %copy-done.7, bf16[3072,128]{1,0:T(8,128)(2,1)} %copy-done.6, ...), custom_call_target="tpu_custom_call" | custom-call | flops 9437184 | bytes 9437184 | tf_op jit(solution)/shard_map/spread/pallas_call | solution.py:48
  356.6 4.9 %collective-permute-done.28.refs_5_ = bf16[3072,128]{1,0:T(8,128)(2,1)} collective-permute-done((bf16[3072,128]{1,0:T(8,128)(2,1)}, bf16[3072,128]{1,0:T(8,128)(2,1)}, u32[]{:S(2)}, u32[]{:S(2)}) %collective-permute-start.28) | collective-permute-done | bytes 786464 | tf_op jit(solution)/shard_map/ppermute | solution.py:22
  361.5 16.9 %collective-permute-done.29.refs_6_ = bf16[3072,128]{1,0:T(8,128)(2,1)} collective-permute-done((bf16[3072,128]{1,0:T(8,128)(2,1)}, bf16[3072,128]{1,0:T(8,128)(2,1)}, u32[]{:S(2)}, u32[]{:S(2)}) %collective-permute-start.29) | collective-permute-done | bytes 786464 | tf_op jit(solution)/shard_map/ppermute | solution.py:22
  378.3 9.9 %spread.4.refs_7_ = bf16[1,4194304]{1,0:T(2,128)(2,1)} custom-call(s32[2]{0:T(128)} %pad_add_fusion.zs, bf16[3072,128]{1,0:T(8,128)(2,1)} %get-tuple-element.38.refs_0_, bf16[3072,128]{1,0:T(8,128)(2,1)} %copy-done.16, bf16[3072,128]{1,0:T(8,128)(2,1)} %collective-permute-done.25.refs_2_, ...), custom_call_target="tpu_custom_call", output_to_operand_aliasing={{}: (8, {})} | custom-call | flops 9437184 | bytes 9437184 | tf_op jit(solution)/shard_map/spread/pallas_call | solution.py:48
  389.6 11.2 %collective-permute-done.22.refs_5_ = bf16[2048,128]{1,0:T(8,128)(2,1)} collective-permute-done((bf16[2048,128]{1,0:T(8,128)(2,1)}, bf16[2048,128]{1,0:T(8,128)(2,1)}, u32[]{:S(2)}, u32[]{:S(2)}) %collective-permute-start.22) | collective-permute-done | bytes 524320 | tf_op jit(solution)/shard_map/ppermute | solution.py:22
  400.8 6.6 %collective-permute-done.23.refs_6_ = bf16[2048,128]{1,0:T(8,128)(2,1)} collective-permute-done((bf16[2048,128]{1,0:T(8,128)(2,1)}, bf16[2048,128]{1,0:T(8,128)(2,1)}, u32[]{:S(2)}, u32[]{:S(2)}) %collective-permute-start.23) | collective-permute-done | bytes 524320 | tf_op jit(solution)/shard_map/ppermute | solution.py:22
  407.4 5.2 %spread.5 = bf16[1,4194304]{1,0:T(2,128)(2,1)} custom-call(s32[2]{0:T(128)} %pad_add_fusion.zs, bf16[2048,128]{1,0:T(8,128)(2,1)} %get-tuple-element.37.refs_0_, bf16[2048,128]{1,0:T(8,128)(2,1)} %copy-done.18, bf16[2048,128]{1,0:T(8,128)(2,1)} %collective-permute-done.19.refs_2_, ...), custom_call_target="tpu_custom_call", output_to_operand_aliasing={{}: (8, {})} | custom-call | flops 6291456 | bytes 6291456 | tf_op jit(solution)/shard_map/spread/pallas_call | solution.py:48
  (84 shorter events, 32.8 us)
Async XLA Ops:
  10.5 56.9 %collective-permute-start.6 = (bf16[3,3072,128]{2,1,0:T(8,128)(2,1)}, bf16[3,3072,128]{2,1,0:T(8,128)(2,1)}, u32[]{:S(2)}, u32[]{:S(2)}) collective-permute-start(bf16[3,3072,128]{2,1,0:T(8,128)(2,1)} %pack_outer.5), channel_id=1, source_target_pairs={{0,1},{3,2},{4,5},{7,6},{8,9},{11,10},{12,13},{15,14},{16,17},{19,... | collective-permute-start | bytes 7077896 | tf_op jit(solution)/shard_map/ppermute | solution.py:22
  25.3 92.6 %collective-permute-start.3 = (bf16[3,3072,128]{2,1,0:T(8,128)(2,1)}, bf16[3,3072,128]{2,1,0:T(8,128)(2,1)S(1)}, u32[]{:S(2)}, u32[]{:S(2)}) collective-permute-start(bf16[3,3072,128]{2,1,0:T(8,128)(2,1)} %pack_outer.4), channel_id=1, source_target_pairs={{0,1},{3,2},{4,5},{7,6},{8,9},{11,10},{12,13},{15,14},{16,17},{19,... | collective-permute-start | bytes 7077896 | tf_op jit(solution)/shard_map/ppermute | solution.py:22
  32.0 118.5 %collective-permute-start = (bf16[3,2048,128]{2,1,0:T(8,128)(2,1)}, bf16[3,2048,128]{2,1,0:T(8,128)(2,1)}, u32[]{:S(2)}, u32[]{:S(2)}) collective-permute-start(bf16[3,2048,128]{2,1,0:T(8,128)(2,1)} %pack_outer.3), channel_id=1, source_target_pairs={{0,1},{3,2},{4,5},{7,6},{8,9},{11,10},{12,13},{15,14},{16,17},{19,... | collective-permute-start | bytes 4718600 | tf_op jit(solution)/shard_map/ppermute | solution.py:22
  73.5 81.4 %collective-permute-start.7 = (bf16[2,3072,128]{2,1,0:T(8,128)(2,1)}, bf16[2,3072,128]{2,1,0:T(8,128)(2,1)}, u32[]{:S(2)}, u32[]{:S(2)}) collective-permute-start(bf16[2,3072,128]{2,1,0:T(8,128)(2,1)} %sum_middle.5), channel_id=1, source_target_pairs={{1,2},{2,1},{5,6},{6,5},{9,10},{10,9},{13,14},{14,13},{17,18},{18,... | collective-permute-start | bytes 4718600 | tf_op jit(solution)/shard_map/ppermute | solution.py:22
  125.4 34.8 %collective-permute-start.4 = (bf16[2,3072,128]{2,1,0:T(8,128)(2,1)}, bf16[2,3072,128]{2,1,0:T(8,128)(2,1)S(1)}, u32[]{:S(2)}, u32[]{:S(2)}) collective-permute-start(bf16[2,3072,128]{2,1,0:T(8,128)(2,1)} %sum_middle.4), channel_id=1, source_target_pairs={{1,2},{2,1},{5,6},{6,5},{9,10},{10,9},{13,14},{14,13},{17,18},{18,... | collective-permute-start | bytes 4718600 | tf_op jit(solution)/shard_map/ppermute | solution.py:22
  154.1 38.4 %collective-permute-start.1 = (bf16[2,2048,128]{2,1,0:T(8,128)(2,1)}, bf16[2,2048,128]{2,1,0:T(8,128)(2,1)S(1)}, u32[]{:S(2)}, u32[]{:S(2)}) collective-permute-start(bf16[2,2048,128]{2,1,0:T(8,128)(2,1)} %sum_middle.3), channel_id=1, source_target_pairs={{1,2},{2,1},{5,6},{6,5},{9,10},{10,9},{13,14},{14,13},{17,18},{18,... | collective-permute-start | bytes 3145736 | tf_op jit(solution)/shard_map/ppermute | solution.py:22
  159.0 25.1 %collective-permute-start.8 = (bf16[1,3072,128]{2,1,0:T(8,128)(2,1)}, bf16[1,3072,128]{2,1,0:T(8,128)(2,1)S(1)}, u32[]{:S(2)}, u32[]{:S(2)}) collective-permute-start(bf16[1,3072,128]{2,1,0:T(8,128)(2,1)} %sum_inner.5), channel_id=1, source_target_pairs={{1,0},{2,3},{5,4},{6,7},{9,8},{10,11},{13,12},{14,15},{17,16},{18,... | collective-permute-start | bytes 2359304 | tf_op jit(solution)/shard_map/ppermute | solution.py:22
  165.5 35.5 %collective-permute-start.5 = (bf16[1,3072,128]{2,1,0:T(8,128)(2,1)}, bf16[1,3072,128]{2,1,0:T(8,128)(2,1)S(1)}, u32[]{:S(2)}, u32[]{:S(2)}) collective-permute-start(bf16[1,3072,128]{2,1,0:T(8,128)(2,1)} %sum_inner.4), channel_id=1, source_target_pairs={{1,0},{2,3},{5,4},{6,7},{9,8},{10,11},{13,12},{14,15},{17,16},{18,... | collective-permute-start | bytes 2359304 | tf_op jit(solution)/shard_map/ppermute | solution.py:22
  192.5 22.1 %collective-permute-start.15 = (bf16[3072,128]{1,0:T(8,128)(2,1)}, bf16[3072,128]{1,0:T(8,128)(2,1)}, u32[]{:S(2)}, u32[]{:S(2)}) collective-permute-start(bf16[3072,128]{1,0:T(8,128)(2,1)} %get-tuple-element.31), channel_id=1, source_target_pairs={{0,4},{4,0},{8,12},{12,8},{16,20},{20,16},{24,28},{28,24},{1,5},{5... | collective-permute-start | bytes 2359304 | tf_op jit(solution)/shard_map/ppermute | solution.py:27
  196.7 16.4 %collective-permute-start.2 = (bf16[1,2048,128]{2,1,0:T(8,128)(2,1)}, bf16[1,2048,128]{2,1,0:T(8,128)(2,1)S(1)}, u32[]{:S(2)}, u32[]{:S(2)}) collective-permute-start(bf16[1,2048,128]{2,1,0:T(8,128)(2,1)} %sum_inner.3), channel_id=1, source_target_pairs={{1,0},{2,3},{5,4},{6,7},{9,8},{10,11},{13,12},{14,15},{17,16},{18,... | collective-permute-start | bytes 1572872 | tf_op jit(solution)/shard_map/ppermute | solution.py:22
  198.0 24.1 %collective-permute-start.16 = (bf16[3072,128]{1,0:T(8,128)(2,1)}, bf16[3072,128]{1,0:T(8,128)(2,1)S(1)}, u32[]{:S(2)}, u32[]{:S(2)}) collective-permute-start(bf16[3072,128]{1,0:T(8,128)(2,1)} %get-tuple-element.31), channel_id=1, source_target_pairs={{0,8},{4,12},{8,0},{12,4},{16,24},{20,28},{24,16},{28,20},{1,9},{5... | collective-permute-start | bytes 2359304 | tf_op jit(solution)/shard_map/ppermute | solution.py:27
  199.5 23.4 %collective-permute-start.17 = (bf16[3072,128]{1,0:T(8,128)(2,1)}, bf16[3072,128]{1,0:T(8,128)(2,1)}, u32[]{:S(2)}, u32[]{:S(2)}) collective-permute-start(bf16[3072,128]{1,0:T(8,128)(2,1)} %get-tuple-element.31), channel_id=1, source_target_pairs={{0,16},{4,20},{8,24},{12,28},{16,0},{20,4},{24,8},{28,12},{1,17},{... | collective-permute-start | bytes 2359304 | tf_op jit(solution)/shard_map/ppermute | solution.py:27
  209.5 14.0 %collective-permute-start.12 = (bf16[3072,128]{1,0:T(8,128)(2,1)}, bf16[3072,128]{1,0:T(8,128)(2,1)S(1)}, u32[]{:S(2)}, u32[]{:S(2)}) collective-permute-start(bf16[3072,128]{1,0:T(8,128)(2,1)} %get-tuple-element.29), channel_id=1, source_target_pairs={{0,4},{4,0},{8,12},{12,8},{16,20},{20,16},{24,28},{28,24},{1,5},{5... | collective-permute-start | bytes 2359304 | tf_op jit(solution)/shard_map/ppermute | solution.py:27
  213.1 1.5 copy-start.19
  213.1 22.4 %collective-permute-start.13 = (bf16[3072,128]{1,0:T(8,128)(2,1)}, bf16[3072,128]{1,0:T(8,128)(2,1)S(1)}, u32[]{:S(2)}, u32[]{:S(2)}) collective-permute-start(bf16[3072,128]{1,0:T(8,128)(2,1)} %get-tuple-element.29), channel_id=1, source_target_pairs={{0,8},{4,12},{8,0},{12,4},{16,24},{20,28},{24,16},{28,20},{1,9},{5... | collective-permute-start | bytes 2359304 | tf_op jit(solution)/shard_map/ppermute | solution.py:27
  214.6 25.5 %collective-permute-start.14 = (bf16[3072,128]{1,0:T(8,128)(2,1)}, bf16[3072,128]{1,0:T(8,128)(2,1)S(1)}, u32[]{:S(2)}, u32[]{:S(2)}) collective-permute-start(bf16[3072,128]{1,0:T(8,128)(2,1)} %get-tuple-element.29), channel_id=1, source_target_pairs={{0,16},{4,20},{8,24},{12,28},{16,0},{20,4},{24,8},{28,12},{1,17},{... | collective-permute-start | bytes 2359304 | tf_op jit(solution)/shard_map/ppermute | solution.py:27
  222.0 24.3 %collective-permute-start.10 = (bf16[2048,128]{1,0:T(8,128)(2,1)}, bf16[2048,128]{1,0:T(8,128)(2,1)}, u32[]{:S(2)}, u32[]{:S(2)}) collective-permute-start(bf16[2048,128]{1,0:T(8,128)(2,1)} %get-tuple-element.27), channel_id=1, source_target_pairs={{0,8},{4,12},{8,0},{12,4},{16,24},{20,28},{24,16},{28,20},{1,9},{5... | collective-permute-start | bytes 1572872 | tf_op jit(solution)/shard_map/ppermute | solution.py:27
  222.9 24.7 %collective-permute-start.11 = (bf16[2048,128]{1,0:T(8,128)(2,1)}, bf16[2048,128]{1,0:T(8,128)(2,1)}, u32[]{:S(2)}, u32[]{:S(2)}) collective-permute-start(bf16[2048,128]{1,0:T(8,128)(2,1)} %get-tuple-element.27), channel_id=1, source_target_pairs={{0,16},{4,20},{8,24},{12,28},{16,0},{20,4},{24,8},{28,12},{1,17},{... | collective-permute-start | bytes 1572872 | tf_op jit(solution)/shard_map/ppermute | solution.py:27
  223.4 16.7 %copy-start.10 = (bf16[3072,128]{1,0:T(8,128)(2,1)}, bf16[3072,128]{1,0:T(8,128)(2,1)S(1)}, u32[]{:S(2)}) copy-start(bf16[3072,128]{1,0:T(8,128)(2,1)S(1)} %collective-permute-done.12.refs_1_) | copy-start | bytes 2359300
  223.4 24.2 %collective-permute-start.9 = (bf16[2048,128]{1,0:T(8,128)(2,1)}, bf16[2048,128]{1,0:T(8,128)(2,1)}, u32[]{:S(2)}, u32[]{:S(2)}) collective-permute-start(bf16[2048,128]{1,0:T(8,128)(2,1)} %get-tuple-element.27), channel_id=1, source_target_pairs={{0,4},{4,0},{8,12},{12,8},{16,20},{20,16},{24,28},{28,24},{1,5},{5... | collective-permute-start | bytes 1572872 | tf_op jit(solution)/shard_map/ppermute | solution.py:27
  235.5 4.7 %copy-start.11 = (bf16[3072,128]{1,0:T(8,128)(2,1)}, bf16[3072,128]{1,0:T(8,128)(2,1)S(1)}, u32[]{:S(2)}) copy-start(bf16[3072,128]{1,0:T(8,128)(2,1)S(1)} %collective-permute-done.13.refs_2_) | copy-start | bytes 2359300
  235.5 33.9 %collective-permute-start.30 = (bf16[3072,128]{1,0:T(8,128)(2,1)}, bf16[3072,128]{1,0:T(8,128)(2,1)S(1)}, u32[]{:S(2)}, u32[]{:S(2)}) collective-permute-start(bf16[3072,128]{1,0:T(8,128)(2,1)} %get-tuple-element.39.refs_0_), channel_id=1, source_target_pairs={{0,1},{3,2},{4,5},{7,6},{8,9},{11,10},{12,13},{15,14},{16,17},{19,... | collective-permute-start | bytes 2359304 | tf_op jit(solution)/shard_map/ppermute | solution.py:22
  245.8 9.8 %copy-start.3 = (bf16[3072,128]{1,0:T(8,128)(2,1)S(1)}, bf16[3072,128]{1,0:T(8,128)(2,1)}, u32[]{:S(2)}) copy-start(bf16[3072,128]{1,0:T(8,128)(2,1)} %get-tuple-element.39.refs_0_) | copy-start | bytes 2359300
  251.2 16.9 %collective-permute-start.18 = (bf16[2048,128]{1,0:T(8,128)(2,1)}, bf16[2048,128]{1,0:T(8,128)(2,1)S(1)}, u32[]{:S(2)}, u32[]{:S(2)}) collective-permute-start(bf16[2048,128]{1,0:T(8,128)(2,1)} %get-tuple-element.37.refs_0_), channel_id=1, source_target_pairs={{0,1},{3,2},{4,5},{7,6},{8,9},{11,10},{12,13},{15,14},{16,17},{19,... | collective-permute-start | bytes 1572872 | tf_op jit(solution)/shard_map/ppermute | solution.py:22
  255.6 16.2 %collective-permute-start.31 = (bf16[3072,128]{1,0:T(8,128)(2,1)S(1)}, bf16[3072,128]{1,0:T(8,128)(2,1)S(1)}, u32[]{:S(2)}, u32[]{:S(2)}) collective-permute-start(bf16[3072,128]{1,0:T(8,128)(2,1)S(1)} %copy-done.3), channel_id=1, source_target_pairs={{1,2},{2,1},{5,6},{6,5},{9,10},{10,9},{13,14},{14,13},{17,18},{18,... | collective-permute-start | bytes 2359304 | tf_op jit(solution)/shard_map/ppermute | solution.py:22
  256.3 27.7 %collective-permute-start.24 = (bf16[3072,128]{1,0:T(8,128)(2,1)}, bf16[3072,128]{1,0:T(8,128)(2,1)S(1)}, u32[]{:S(2)}, u32[]{:S(2)}) collective-permute-start(bf16[3072,128]{1,0:T(8,128)(2,1)} %get-tuple-element.38.refs_0_), channel_id=1, source_target_pairs={{0,1},{3,2},{4,5},{7,6},{8,9},{11,10},{12,13},{15,14},{16,17},{19,... | collective-permute-start | bytes 2359304 | tf_op jit(solution)/shard_map/ppermute | solution.py:22
  259.2 10.9 %collective-permute-start.19 = (bf16[2048,128]{1,0:T(8,128)(2,1)}, bf16[2048,128]{1,0:T(8,128)(2,1)}, u32[]{:S(2)}, u32[]{:S(2)}) collective-permute-start(bf16[2048,128]{1,0:T(8,128)(2,1)} %get-tuple-element.37.refs_0_), channel_id=1, source_target_pairs={{1,2},{2,1},{5,6},{6,5},{9,10},{10,9},{13,14},{14,13},{17,18},{18,... | collective-permute-start | bytes 1572872 | tf_op jit(solution)/shard_map/ppermute | solution.py:22
  268.1 76.4 %copy-start.18 = (bf16[2048,128]{1,0:T(8,128)(2,1)}, bf16[2048,128]{1,0:T(8,128)(2,1)S(1)}, u32[]{:S(2)}) copy-start(bf16[2048,128]{1,0:T(8,128)(2,1)S(1)} %collective-permute-done.18.refs_1_) | copy-start | bytes 1572868
  268.1 19.5 %collective-permute-start.33 = (bf16[3072,128]{1,0:T(8,128)(2,1)S(1)}, bf16[3072,128]{1,0:T(8,128)(2,1)S(1)}, u32[]{:S(2)}, u32[]{:S(2)}) collective-permute-start(bf16[3072,128]{1,0:T(8,128)(2,1)S(1)} %copy-done.3), channel_id=1, source_target_pairs={{1,0},{2,3},{5,4},{6,7},{9,8},{10,11},{13,12},{14,15},{17,16},{18,... | collective-permute-start | bytes 2359304 | tf_op jit(solution)/shard_map/ppermute | solution.py:22
  269.4 77.3 %copy-start.4 = (bf16[3072,128]{1,0:T(8,128)(2,1)}, bf16[3072,128]{1,0:T(8,128)(2,1)S(1)}, u32[]{:S(2)}) copy-start(bf16[3072,128]{1,0:T(8,128)(2,1)S(1)} %collective-permute-done.30.refs_1_) | copy-start | bytes 2359300
  269.4 19.5 %collective-permute-start.32 = (bf16[3072,128]{1,0:T(8,128)(2,1)S(1)}, bf16[3072,128]{1,0:T(8,128)(2,1)S(1)}, u32[]{:S(2)}, u32[]{:S(2)}) collective-permute-start(bf16[3072,128]{1,0:T(8,128)(2,1)S(1)} %collective-permute-done.30.refs_1_), channel_id=1, source_target_pairs={{1,2},{2,1},{5,6},{6,5},{9,10},{10,9},{13,14},{14,13},{17,18},{18,... | collective-permute-start | bytes 2359304 | tf_op jit(solution)/shard_map/ppermute | solution.py:22
  270.2 20.1 %collective-permute-start.25 = (bf16[3072,128]{1,0:T(8,128)(2,1)}, bf16[3072,128]{1,0:T(8,128)(2,1)}, u32[]{:S(2)}, u32[]{:S(2)}) collective-permute-start(bf16[3072,128]{1,0:T(8,128)(2,1)} %get-tuple-element.38.refs_0_), channel_id=1, source_target_pairs={{1,2},{2,1},{5,6},{6,5},{9,10},{10,9},{13,14},{14,13},{17,18},{18,... | collective-permute-start | bytes 2359304 | tf_op jit(solution)/shard_map/ppermute | solution.py:22
  271.8 74.9 %copy-start.5 = (bf16[3072,128]{1,0:T(8,128)(2,1)}, bf16[3072,128]{1,0:T(8,128)(2,1)S(1)}, u32[]{:S(2)}) copy-start(bf16[3072,128]{1,0:T(8,128)(2,1)S(1)} %collective-permute-done.31.refs_2_) | copy-start | bytes 2359300
  271.8 39.1 %collective-permute-start.27 = (bf16[3072,128]{1,0:T(8,128)(2,1)}, bf16[3072,128]{1,0:T(8,128)(2,1)S(1)}, u32[]{:S(2)}, u32[]{:S(2)}) collective-permute-start(bf16[3072,128]{1,0:T(8,128)(2,1)} %get-tuple-element.38.refs_0_), channel_id=1, source_target_pairs={{1,0},{2,3},{5,4},{6,7},{9,8},{10,11},{13,12},{14,15},{17,16},{18,... | collective-permute-start | bytes 2359304 | tf_op jit(solution)/shard_map/ppermute | solution.py:22
  284.0 60.5 %copy-start.16 = (bf16[3072,128]{1,0:T(8,128)(2,1)}, bf16[3072,128]{1,0:T(8,128)(2,1)S(1)}, u32[]{:S(2)}) copy-start(bf16[3072,128]{1,0:T(8,128)(2,1)S(1)} %collective-permute-done.24.refs_1_) | copy-start | bytes 2359300
  284.0 28.1 %collective-permute-start.26 = (bf16[3072,128]{1,0:T(8,128)(2,1)S(1)}, bf16[3072,128]{1,0:T(8,128)(2,1)}, u32[]{:S(2)}, u32[]{:S(2)}) collective-permute-start(bf16[3072,128]{1,0:T(8,128)(2,1)S(1)} %collective-permute-done.24.refs_1_), channel_id=1, source_target_pairs={{1,2},{2,1},{5,6},{6,5},{9,10},{10,9},{13,14},{14,13},{17,18},{18,... | collective-permute-start | bytes 2359304 | tf_op jit(solution)/shard_map/ppermute | solution.py:22
  287.7 59.0 %copy-start.6 = (bf16[3072,128]{1,0:T(8,128)(2,1)}, bf16[3072,128]{1,0:T(8,128)(2,1)S(1)}, u32[]{:S(2)}) copy-start(bf16[3072,128]{1,0:T(8,128)(2,1)S(1)} %collective-permute-done.33.refs_4_) | copy-start | bytes 2359300
  287.7 40.0 %collective-permute-start.34 = (bf16[3072,128]{1,0:T(8,128)(2,1)S(1)}, bf16[3072,128]{1,0:T(8,128)(2,1)S(1)}, u32[]{:S(2)}, u32[]{:S(2)}) collective-permute-start(bf16[3072,128]{1,0:T(8,128)(2,1)S(1)} %collective-permute-done.31.refs_2_), channel_id=1, source_target_pairs={{1,0},{2,3},{5,4},{6,7},{9,8},{10,11},{13,12},{14,15},{17,16},{18,... | collective-permute-start | bytes 2359304 | tf_op jit(solution)/shard_map/ppermute | solution.py:22
  289.0 38.7 %copy-start.7 = (bf16[3072,128]{1,0:T(8,128)(2,1)}, bf16[3072,128]{1,0:T(8,128)(2,1)S(1)}, u32[]{:S(2)}) copy-start(bf16[3072,128]{1,0:T(8,128)(2,1)S(1)} %collective-permute-done.32.refs_3_) | copy-start | bytes 2359300
  289.0 55.6 %collective-permute-start.35 = (bf16[3072,128]{1,0:T(8,128)(2,1)S(1)}, bf16[3072,128]{1,0:T(8,128)(2,1)S(1)}, u32[]{:S(2)}, u32[]{:S(2)}) collective-permute-start(bf16[3072,128]{1,0:T(8,128)(2,1)S(1)} %collective-permute-done.32.refs_3_), channel_id=1, source_target_pairs={{1,0},{2,3},{5,4},{6,7},{9,8},{10,11},{13,12},{14,15},{17,16},{18,... | collective-permute-start | bytes 2359304 | tf_op jit(solution)/shard_map/ppermute | solution.py:22
  290.3 23.1 %collective-permute-start.20 = (bf16[2048,128]{1,0:T(8,128)(2,1)S(1)}, bf16[2048,128]{1,0:T(8,128)(2,1)}, u32[]{:S(2)}, u32[]{:S(2)}) collective-permute-start(bf16[2048,128]{1,0:T(8,128)(2,1)S(1)} %collective-permute-done.18.refs_1_), channel_id=1, source_target_pairs={{1,2},{2,1},{5,6},{6,5},{9,10},{10,9},{13,14},{14,13},{17,18},{18,... | collective-permute-start | bytes 1572872 | tf_op jit(solution)/shard_map/ppermute | solution.py:22
  310.8 33.7 %copy-start.17 = (bf16[3072,128]{1,0:T(8,128)(2,1)}, bf16[3072,128]{1,0:T(8,128)(2,1)S(1)}, u32[]{:S(2)}) copy-start(bf16[3072,128]{1,0:T(8,128)(2,1)S(1)} %collective-permute-done.27.refs_4_) | copy-start | bytes 2359300
  310.8 50.7 %collective-permute-start.28 = (bf16[3072,128]{1,0:T(8,128)(2,1)}, bf16[3072,128]{1,0:T(8,128)(2,1)}, u32[]{:S(2)}, u32[]{:S(2)}) collective-permute-start(bf16[3072,128]{1,0:T(8,128)(2,1)} %collective-permute-done.25.refs_2_), channel_id=1, source_target_pairs={{1,0},{2,3},{5,4},{6,7},{9,8},{10,11},{13,12},{14,15},{17,16},{18,... | collective-permute-start | bytes 2359304 | tf_op jit(solution)/shard_map/ppermute | solution.py:22
  312.1 66.2 %collective-permute-start.29 = (bf16[3072,128]{1,0:T(8,128)(2,1)}, bf16[3072,128]{1,0:T(8,128)(2,1)}, u32[]{:S(2)}, u32[]{:S(2)}) collective-permute-start(bf16[3072,128]{1,0:T(8,128)(2,1)} %collective-permute-done.26.refs_3_), channel_id=1, source_target_pairs={{1,0},{2,3},{5,4},{6,7},{9,8},{10,11},{13,12},{14,15},{17,16},{18,... | collective-permute-start | bytes 2359304 | tf_op jit(solution)/shard_map/ppermute | solution.py:22
  313.4 76.1 %collective-permute-start.21 = (bf16[2048,128]{1,0:T(8,128)(2,1)}, bf16[2048,128]{1,0:T(8,128)(2,1)}, u32[]{:S(2)}, u32[]{:S(2)}) collective-permute-start(bf16[2048,128]{1,0:T(8,128)(2,1)} %get-tuple-element.37.refs_0_), channel_id=1, source_target_pairs={{1,0},{2,3},{5,4},{6,7},{9,8},{10,11},{13,12},{14,15},{17,16},{18,... | collective-permute-start | bytes 1572872 | tf_op jit(solution)/shard_map/ppermute | solution.py:22
  327.7 19.0 %copy-start.8 = (bf16[3072,128]{1,0:T(8,128)(2,1)}, bf16[3072,128]{1,0:T(8,128)(2,1)S(1)}, u32[]{:S(2)}) copy-start(bf16[3072,128]{1,0:T(8,128)(2,1)S(1)} %collective-permute-done.34.refs_5_) | copy-start | bytes 2359300
  327.7 73.1 %collective-permute-start.22 = (bf16[2048,128]{1,0:T(8,128)(2,1)}, bf16[2048,128]{1,0:T(8,128)(2,1)}, u32[]{:S(2)}, u32[]{:S(2)}) collective-permute-start(bf16[2048,128]{1,0:T(8,128)(2,1)} %collective-permute-done.19.refs_2_), channel_id=1, source_target_pairs={{1,0},{2,3},{5,4},{6,7},{9,8},{10,11},{13,12},{14,15},{17,16},{18,... | collective-permute-start | bytes 1572872 | tf_op jit(solution)/shard_map/ppermute | solution.py:22
  345.4 62.0 %collective-permute-start.23 = (bf16[2048,128]{1,0:T(8,128)(2,1)}, bf16[2048,128]{1,0:T(8,128)(2,1)}, u32[]{:S(2)}, u32[]{:S(2)}) collective-permute-start(bf16[2048,128]{1,0:T(8,128)(2,1)} %collective-permute-done.20.refs_3_), channel_id=1, source_target_pairs={{1,0},{2,3},{5,4},{6,7},{9,8},{10,11},{13,12},{14,15},{17,16},{18,... | collective-permute-start | bytes 1572872 | tf_op jit(solution)/shard_map/ppermute | solution.py:22
  (8 other events, 8.5 us)

commit v2 on v0

v2 whole, which is shorter than its diff:
```python
import functools

import jax
import jax.numpy as jnp
from jax import lax
from jax.experimental import pallas as pl
from jax.experimental.pallas import tpu as pltpu
from jax.sharding import PartitionSpec as P


LANES = 128
VMEM = 67043328
CUTS = (3, 3, 2)
UNITS = 8
OUTER = ((0, 1), (3, 2))
MIDDLE = ((1, 2), (2, 1))
INNER = ((1, 0), (2, 3))
bf16 = jnp.bfloat16
f32 = jnp.float32
ANY = pl.BlockSpec(memory_space=pl.ANY)


def swapped(value, level):
    pairs = [(r, r ^ 2**level) for r in range(lax.axis_size("rep"))]
    return lax.ppermute(value, "rep", pairs)


def crossed(value, mask):
    return lax.ppermute(value, "zero", [(i, i ^ mask) for i in range(lax.axis_size("zero"))])


def block_of(start, size, most):
    rows = 1
    while rows < most and not (start % (2 * rows) or size % (2 * rows)):
        rows *= 2
    return rows


def far(z, p):
    return jnp.where(z < 2, 3 - p, p)


def pieces(rows, most):
    step = block_of(0, rows, most)

    def run(body):
        def one(i, carry):
            at = pl.multiple_of(i * step, step)
            flat = pl.ds(pl.multiple_of(i * (step * LANES), step * LANES), step * LANES)
            body(pl.ds(at, step), flat, step)
            return carry

        lax.fori_loop(0, rows // step, one, 0)

    return run


def call(body, scalars, grid, ins, specs, outs, out_specs, alias=(), cost=0):
    return pl.pallas_call(
        body,
        out_shape=outs,
        grid_spec=pltpu.PrefetchScalarGridSpec(
            num_scalar_prefetch=1, grid=grid, in_specs=list(specs), out_specs=out_specs
        ),
        input_output_aliases={a + 1: b for a, b in alias},
        cost_estimate=pl.CostEstimate(flops=cost, bytes_accessed=cost, transcendentals=0),
        compiler_params=pltpu.CompilerParams(vmem_limit_bytes=VMEM),
    )(scalars, *ins)


def pack_body(zs, *refs):
    half = len(refs) // 2
    rows = refs[half].shape[0]

    @pieces(rows, 256)
    def _(row, flat, step):
        for g, o in zip(refs[:half], refs[half:]):
            o[row, :] = g[0, :, flat].reshape(step, LANES)


def sum_body(zs, *refs):
    count = len(refs) // 3
    rows = refs[-1].shape[0]

    @pieces(rows, 128)
    def _(row, flat, step):
        for k in range(count):
            r, g, o = refs[2 * k], refs[2 * k + 1], refs[2 * count + k]
            own = g[0, :, flat].astype(f32).reshape(step, LANES)
            o[row, :] = (r[row, :].astype(f32) + own).astype(bf16)


def adam_body(zs, g, ra, rb, rc, m, v, w, sc, *rest):
    mo, vo, fr, fb = rest[-4:]
    one, two = sc[0], sc[1]

    @pieces(fr.shape[0], 64)
    def _(row, flat, step):
        shape = (step, LANES)
        total = g[0, :, flat].astype(f32).reshape(shape)
        total = total + ra[row, :].astype(f32) + rb[row, :].astype(f32) + rc[row, :].astype(f32)
        grad = total * 0.25
        m_new = 0.9 * m[:, flat].reshape(shape) + 0.1 * grad
        v_new = 0.999 * v[:, flat].reshape(shape) + 0.001 * grad * grad
        mo[:, flat] = m_new.reshape(1, step * LANES)
        vo[:, flat] = v_new.reshape(1, step * LANES)
        old = w[:, flat].reshape(shape)
        root = jnp.sqrt(v_new * two) + 1e-08
        fresh = old - 0.02 * (m_new * one / root + 0.1 * old)
        fr[row, :] = fresh
        fb[row, :] = fresh.astype(bf16)


def mean_body(zs, fr, other, *rest):
    wo, mine, yours = rest[-3:]

    def write(to):
        @pieces(fr.shape[0], 64)
        def _(row, flat, step):
            avg = 0.5 * (fr[row, :] + other[row, :].astype(f32))
            wo[:, flat] = avg.reshape(1, step * LANES)
            to[row, :] = avg.astype(bf16)

    pl.when(pl.program_id(0) == 0)(lambda: write(mine))
    pl.when(pl.program_id(0) == 1)(lambda: write(yours))


def spread_body(zs, *refs):
    o = refs[-1]
    place = pl.program_id(0)

    for k in range(8):

        @pl.when(place == k)
        def _(src=refs[k]):
            @pieces(src.shape[0], 256)
            def _(row, flat, step):
                o[:, flat] = src[row, :].reshape(1, step * LANES)


def line_branch(level, grads, master, moment_one, moment_two, step_index):
    size = master.shape[1]
    rows = size // LANES
    z = lax.axis_index("zero").astype(jnp.int32)
    half = (lax.axis_index("rep").astype(jnp.int32) // 2**level) % 2
    count = (step_index[0] + 1).astype(f32)
    scale = jnp.stack(
        [1.0 / (1.0 - jnp.power(f32(0.9), count)), 1.0 / (1.0 - jnp.power(f32(0.999), count))]
    )
    scalars = jnp.stack([z, half])
    unit = rows // UNITS
    kept = {}
    whole = jax.ShapeDtypeStruct((1, size), f32)
    compact = lambda n: jax.ShapeDtypeStruct((n, LANES), bf16)

    def plan(part, most=2048):
        _, start, n = part
        R = block_of(start, n, most)
        return R, n // R, start // R, rows // R

    row_of = lambda R, f: pl.BlockSpec((R, LANES), f)
    grad_of = lambda R, f: pl.BlockSpec((1, 1, R * LANES), f)
    flat_of = lambda R, f: pl.BlockSpec((1, R * LANES), f)

    def own_grad(R, per, base, p):
        return grad_of(R, lambda i, zs: (0, 0, far(zs[0], p) * per + base + i))

    def pack(part, places):
        _, _, n = part
        R, nb, base, per = plan(part, 1024)
        return call(
            pack_body, scalars, (nb,), [grads] * len(places),
            [own_grad(R, per, base, p) for p in places],
            [compact(n)] * len(places),
            [row_of(R, lambda i, zs: (i, 0))] * len(places),
            cost=n * LANES * 6 * len(places),
        )

    def add(part, received, places):
        _, _, n = part
        R, nb, base, per = plan(part, 1024)
        ins, specs = [], []
        for r, p in zip(received, places):
            ins += [r, grads]
            specs += [row_of(R, lambda i, zs: (i, 0)), own_grad(R, per, base, p)]
        return call(
            sum_body, scalars, (nb,), ins, specs,
            [compact(n)] * len(places),
            [row_of(R, lambda i, zs: (i, 0))] * len(places),
            cost=n * LANES * 8 * len(places),
        )

    def send(value, pairs):
        return lax.ppermute(value, "zero", list(pairs))

    def keep(names, ins, specs, first):
        if names[0] not in kept:
            return ()
        alias = tuple((len(ins) + i, first + i) for i in range(len(names)))
        ins += [kept[name] for name in names]
        specs += [ANY] * len(names)
        return alias

    def adam(part, received):
        _, _, n = part
        R, nb, base, per = plan(part, 1024)
        row = row_of(R, lambda i, zs: (i, 0))
        flat = flat_of(R, lambda i, zs: (0, base + i))
        ins = [grads, *received, moment_one, moment_two, master, scale]
        specs = [grad_of(R, lambda i, zs: (0, 0, zs[0] * per + base + i)), row, row, row]
        specs += [flat, flat, flat, pl.BlockSpec(memory_space=pltpu.SMEM)]
        alias = keep(("m", "v"), ins, specs, 0)
        kept["m"], kept["v"], fresh, fresh16 = call(
            adam_body, scalars, (nb,), ins, specs,
            (whole, whole, jax.ShapeDtypeStruct((n, LANES), f32), compact(n)),
            (flat, flat, row, row), alias, cost=n * LANES * 40,
        )
        return fresh, fresh16

    def mean(part, fresh, other):
        _, start, n = part
        R = block_of(start, n // 2, 1024)
        nh, base = n // 2 // R, start // R
        at = lambda p, i, zs: jnp.where(p == 0, zs[1], 1 - zs[1]) * nh + i
        row = row_of(R, lambda p, i, zs: (at(p, i, zs), 0))
        ins, specs = [fresh, other], [row, row]
        alias = keep(("w",), ins, specs, 0)
        hold = lambda first: row_of(
            R, lambda p, i, zs: (jnp.clip((p - first) * nh + i, 0, nh - 1), 0)
        )
        kept["w"], mine, yours = call(
            mean_body, scalars, (2, nh), ins, specs,
            (whole, compact(n // 2), compact(n // 2)),
            (flat_of(R, lambda p, i, zs: (0, base + at(p, i, zs))), hold(0), hold(1)),
            alias, cost=n * LANES * 14,
        )
        return mine, yours

    def spread(part, mine, yours):
        _, start, n = part
        R = block_of(start, n // 2, 1024)
        nh, base, per = n // 2 // R, start // R, rows // R
        ins = [mine, yours]
        for mask in (1, 2, 3):
            got = crossed(mine, mask)
            ins += [got, swapped(got, level)]
        specs = [
            row_of(R, lambda q, i, zs, at=at: (jnp.clip((q - at) * nh + i, 0, nh - 1), 0))
            for at in range(8)
        ]
        alias = keep(("p",), ins, specs, 0)

        def out(q, i, zs):
            shard = jnp.bitwise_xor(zs[0], q // 2)
            side = jnp.where(q % 2 == 0, zs[1], 1 - zs[1])
            return (0, shard * per + base + side * nh + i)

        kept["p"] = call(
            spread_body, scalars, (8, nh), ins, specs,
            jax.ShapeDtypeStruct((1, 4 * size), bf16), flat_of(R, out),
            alias, cost=n * LANES * 24,
        )

    parts, start = [], 0
    for k, cut in enumerate(CUTS):
        parts.append((k, start, cut * unit))
        start += cut * unit
    for part in parts:
        k = part[0]
        (e,) = pack(part, (0,))
        f, g = pack(part, (1, 2))
        re = send(e, OUTER)
        rf = send(f, OUTER)
        rg = send(g, OUTER)
        (sm,) = add(part, (re,), (0,))
        rm = send(sm, MIDDLE)
        sn, si = add(part, (rf, rm), (1, 3))
        rn = send(sn, MIDDLE)
        ri = send(si, INNER)
        fresh, fresh16 = adam(part, (rg, rn, ri))
        other = swapped(fresh16, level)
        mine, yours = mean(part, fresh, other)
        spread(part, mine, yours)
    return kept["w"], kept["m"], kept["v"], kept["p"]


def line_step(*args):
    nbits = lax.axis_size("rep").bit_length() - 1

    def branch(level, *args):
        return line_branch(level, *args)

    bit = args[-1][0] % nbits
    return lax.switch(bit, [functools.partial(branch, b) for b in range(nbits)], *args)


def plain_step(grads, master, moment_one, moment_two, step_index):
    loop_size = lax.axis_size("zero")
    nbits = lax.axis_size("rep").bit_length() - 1
    tstep = step_index[0]
    count = (tstep + 1).astype(f32)
    terms = grads.reshape(-1, LANES)
    g = lax.psum_scatter(terms, "zero", scatter_dimension=0, tiled=True).astype(f32)
    g = g.reshape(master.shape) / loop_size
    m_new = 0.9 * moment_one + 0.1 * g
    v_new = 0.999 * moment_two + 0.001 * g * g
    corr_one = 1.0 - jnp.power(f32(0.9), count)
    corr_two = 1.0 - jnp.power(f32(0.999), count)
    fresh = master - 0.02 * (m_new / corr_one / (jnp.sqrt(v_new / corr_two) + 1e-08) + 0.1 * master)
    other = jnp.zeros_like(fresh)
    for level in range(nbits):
        other = jnp.where(tstep % nbits == level, swapped(fresh, level), other)
    averaged = 0.5 * (fresh + other)
    whole = lax.all_gather(averaged.astype(bf16).reshape(-1, LANES), "zero", axis=0, tiled=True)
    return (averaged, m_new, v_new, whole.reshape(1, -1))


def shards(*args):
    if lax.axis_size("zero") == 4:
        return line_step(*args)
    return plain_step(*args)


def solution(mesh):
    return jax.shard_map(
        shards,
        mesh=mesh,
        in_specs=(
            P("rep", "zero", None),
            P("rep", "zero"),
            P("rep", "zero"),
            P("rep", "zero"),
            P(),
        ),
        out_specs=(P("rep", "zero"), P("rep", "zero"), P("rep", "zero"), P("rep", None)),
        check_vma=False,
    )
```

time: 928 us -> 328 us (0.35)
  waiting for transfers between devices: 668 us -> 117 us
  other arithmetic: 219 us -> 1.19 us
  Pallas kernels: 0 us -> 122 us
  starting transfers between devices: 3.21 us -> 82.6 us
  local copies, waits for them, and re-layouts: 22.1 us -> 1.53 us
  between operations: 15.4 us -> 1.29 us
    unnamed x3 -> x0, waiting for transfers between devices: 292 us -> none
    all_gather x1 -> x0, waiting for transfers between devices: 285 us -> none  [shards(): lax.all_gather(averaged.astype(jnp.bfloat16), 'zero', axis=1, tiled=True)]
    unnamed x1 -> x0, other arithmetic: 178 us -> none
    pallas_call x0 -> x21, Pallas kernels: none -> 122 us  [call(): pl.pallas_call(body, out_shape=outs, grid_spec=pltpu.PrefetchScalarGridSp...]
    ppermute x3 -> x39, starting transfers between devices: 2.95 us -> 82.6 us  [the longest x18 53.5 us: send(): return lax.ppermute(value, 'zero', list(pairs))]
    ppermute x3 -> x39, waiting for transfers between devices: 91.5 us -> 117 us  [the longest x9 64.9 us: crossed(): lax.ppermute(value, 'zero', [(i, i ^ mask) for i in range(lax.axis_size('...]
    sub x1 -> x0, other arithmetic: 24.8 us -> none  [shards(): master - 0.02 * (m_new / corr_one / (jnp.sqrt(v_new / corr_two) + 1e-08)...]
    unnamed x8 -> x0, local copies, waits for them, and re-layouts: 22.1 us -> none
  transfers between devices with their start and end apart: 5 -> 39, of which waited for: 5 -> 9; matrix products, arithmetic and copies ran while one was open for 0% -> 0% of each run, Pallas kernels for 0% -> 33%
where the time goes in v2:
time: 328 us; the launch traced here: 326 us
  Pallas kernels  122 us (37%)
  waiting for transfers between devices  117 us (36%)
  starting transfers between devices  82.6 us (25%)
    pallas_call x21, Pallas kernels, call(): pl.pallas_call(body, out_shape=outs, grid_spec=pltpu.PrefetchScalarGridSp...  122 us
    ppermute x9, waiting for transfers between devices, crossed(): lax.ppermute(value, 'zero', [(i, i ^ mask) for i in range(lax.axis_size('...  64.9 us
    ppermute x18, starting transfers between devices, send(): return lax.ppermute(value, 'zero', list(pairs))  53.5 us
    ppermute x18, waiting for transfers between devices, send(): return lax.ppermute(value, 'zero', list(pairs))  51.6 us
    ppermute x9, starting transfers between devices, crossed(): lax.ppermute(value, 'zero', [(i, i ^ mask) for i in range(lax.axis_size('...  26.7 us
  transfers between devices with their start and end apart: 39, of which 9 were waited for; matrix products, arithmetic and copies ran while one was open for 0% of the time, Pallas kernels for 33%

profile of v2, /device:TPU:0, one launch (start us, length us, event | category | flops | bytes accessed | tf_op | source)
XLA Modules:
  0.0 325.9 jit_solution(12024797865638198938)
XLA Ops:
  1.3 324.7 %conditional.1 = (f32[1,1048576]{1,0:T(1,128)}, f32[1,1048576]{1,0:T(1,128)}, f32[1,1048576]{1,0:T(1,128)}, bf16[1,4194304]{1,0:T(2,128)(2,1)}) conditional(s32[]{:T(128)} %clamp.3, (bf16[1,1,4194304]{2,1,0:T(2,128)(2,1)}, s32[1]{0:T(128)}, f32[1,1048576]{1,0:T(1,128)}, f32[1,1048576]{1,0:T(1,128)}, ...), branch_computations={%region_0.1_spmd, %region_1.2_spmd, %region_2.3_spmd} | conditional | flops 125829160 | bytes 222300224 | solution.py:294
  1.9 3.8 %branch_0_fun.30 = bf16[3072,128]{1,0:T(8,128)(2,1)} custom-call(s32[2]{0:T(128)} %pad_add_fusion.zs, bf16[1,1,4194304]{2,1,0:T(2,128)(2,1)} %get-tuple-element.161.refs_0_.refs_1_.refs_3_.g), custom_call_target="tpu_custom_call" | custom-call | flops 2359296 | bytes 2359296 | tf_op jit(solution)/shard_map/cond/branch_0_fun/pallas_call | solution.py:59
  5.7 5.8 %collective-permute-start.14 = (bf16[3072,128]{1,0:T(8,128)(2,1)}, bf16[3072,128]{1,0:T(8,128)(2,1)}, u32[]{:S(2)}, u32[]{:S(2)}) collective-permute-start(bf16[3072,128]{1,0:T(8,128)(2,1)} %branch_0_fun.30), channel_id=1, source_target_pairs={{0,1},{3,2},{4,5},{7,6},{8,9},{11,10},{12,13},{15,14},{16,17},{19,... | collective-permute-start | bytes 2359304 | tf_op jit(solution)/shard_map/cond/branch_0_fun/ppermute | solution.py:194
  11.5 3.8 %branch_0_fun.26 = bf16[3072,128]{1,0:T(8,128)(2,1)} custom-call(s32[2]{0:T(128)} %pad_add_fusion.zs, bf16[1,1,4194304]{2,1,0:T(2,128)(2,1)} %get-tuple-element.161.refs_0_.refs_1_.refs_3_.g), custom_call_target="tpu_custom_call" | custom-call | flops 2359296 | bytes 2359296 | tf_op jit(solution)/shard_map/cond/branch_0_fun/pallas_call | solution.py:59
  15.3 2.2 collective-permute-start.8
  17.5 4.5 %branch_0_fun.29 = (bf16[3072,128]{1,0:T(8,128)(2,1)}, bf16[3072,128]{1,0:T(8,128)(2,1)}) custom-call(s32[2]{0:T(128)} %pad_add_fusion.zs, bf16[1,1,4194304]{2,1,0:T(2,128)(2,1)} %get-tuple-element.161.refs_0_.refs_1_.refs_3_.g, bf16[1,1,4194304]{2,1,0:T(2,128)(2,1)} %get-tuple-element.161.refs_0_.refs_1_.refs_3_.g), custom_call_target="tpu_custom_call" | custom-call | flops 4718592 | bytes 4718592 | tf_op jit(solution)/shard_map/cond/branch_0_fun/pallas_call | solution.py:59
  22.0 2.2 collective-permute-start.13
  24.3 2.7 branch_0_fun.22
  26.9 2.1 collective-permute-start.2
  29.0 4.2 %branch_0_fun.31 = bf16[3072,128]{1,0:T(8,128)(2,1)} custom-call(s32[2]{0:T(128)} %pad_add_fusion.zs, bf16[3072,128]{1,0:T(8,128)(2,1)} %collective-permute-done.14.refs_0_, bf16[1,1,4194304]{2,1,0:T(2,128)(2,1)} %get-tuple-element.161.refs_0_.refs_1_.refs_3_.g), custom_call_target="tpu_custom_call" | custom-call | flops 3145728 | bytes 3145728 | tf_op jit(solution)/shard_map/cond/branch_0_fun/pallas_call | solution.py:59
  33.2 1.5 collective-permute-start.15
  34.8 4.5 %branch_0_fun.25 = (bf16[3072,128]{1,0:T(8,128)(2,1)}, bf16[3072,128]{1,0:T(8,128)(2,1)}) custom-call(s32[2]{0:T(128)} %pad_add_fusion.zs, bf16[1,1,4194304]{2,1,0:T(2,128)(2,1)} %get-tuple-element.161.refs_0_.refs_1_.refs_3_.g, bf16[1,1,4194304]{2,1,0:T(2,128)(2,1)} %get-tuple-element.161.refs_0_.refs_1_.refs_3_.g), custom_call_target="tpu_custom_call" | custom-call | flops 4718592 | bytes 4718592 | tf_op jit(solution)/shard_map/cond/branch_0_fun/pallas_call | solution.py:59
  39.2 7.1 %collective-permute-start.7 = (bf16[3072,128]{1,0:T(8,128)(2,1)}, bf16[3072,128]{1,0:T(8,128)(2,1)}, u32[]{:S(2)}, u32[]{:S(2)}) collective-permute-start(bf16[3072,128]{1,0:T(8,128)(2,1)} %get-tuple-element.40), channel_id=1, source_target_pairs={{0,1},{3,2},{4,5},{7,6},{8,9},{11,10},{12,13},{15,14},{16,17},{19,... | collective-permute-start | bytes 2359304 | tf_op jit(solution)/shard_map/cond/branch_0_fun/ppermute | solution.py:194
  46.4 4.2 %branch_0_fun.27 = bf16[3072,128]{1,0:T(8,128)(2,1)} custom-call(s32[2]{0:T(128)} %pad_add_fusion.zs, bf16[3072,128]{1,0:T(8,128)(2,1)} %collective-permute-done.8.refs_0_, bf16[1,1,4194304]{2,1,0:T(2,128)(2,1)} %get-tuple-element.161.refs_0_.refs_1_.refs_3_.g), custom_call_target="tpu_custom_call" | custom-call | flops 3145728 | bytes 3145728 | tf_op jit(solution)/shard_map/cond/branch_0_fun/pallas_call | solution.py:59
  50.6 1.5 collective-permute-start.9
  52.1 21.7 %collective-permute-done.2.refs_0_ = bf16[2048,128]{1,0:T(8,128)(2,1)} collective-permute-done((bf16[2048,128]{1,0:T(8,128)(2,1)}, bf16[2048,128]{1,0:T(8,128)(2,1)}, u32[]{:S(2)}, u32[]{:S(2)}) %collective-permute-start.2) | collective-permute-done | bytes 524320 | tf_op jit(solution)/shard_map/cond/branch_0_fun/ppermute | solution.py:194
  73.8 5.3 %collective-permute-start.12 = (bf16[3072,128]{1,0:T(8,128)(2,1)}, bf16[3072,128]{1,0:T(8,128)(2,1)}, u32[]{:S(2)}, u32[]{:S(2)}) collective-permute-start(bf16[3072,128]{1,0:T(8,128)(2,1)} %get-tuple-element.43), channel_id=1, source_target_pairs={{0,1},{3,2},{4,5},{7,6},{8,9},{11,10},{12,13},{15,14},{16,17},{19,... | collective-permute-start | bytes 2359304 | tf_op jit(solution)/shard_map/cond/branch_0_fun/ppermute | solution.py:194
  79.1 3.1 branch_0_fun.21
  82.2 2.1 collective-permute-start.1
  84.4 2.9 branch_0_fun.23
  88.7 5.2 %branch_0_fun.32 = (bf16[3072,128]{1,0:T(8,128)(2,1)}, bf16[3072,128]{1,0:T(8,128)(2,1)}) custom-call(s32[2]{0:T(128)} %pad_add_fusion.zs, bf16[3072,128]{1,0:T(8,128)(2,1)} %collective-permute-done.13.refs_0_, bf16[1,1,4194304]{2,1,0:T(2,128)(2,1)} %get-tuple-element.161.refs_0_.refs_1_.refs_3_.g, bf16[3072,128]{1,0:T(8,128)(2,1)} %collective-permute-done.15.refs_2_, ...), custom_call_target="tpu_custom_call" | custom-call | flops 6291456 | bytes 6291456 | tf_op jit(solution)/shard_map/cond/branch_0_fun/pallas_call | solution.py:59
  94.0 23.7 %collective-permute-done.1.refs_0_ = bf16[2048,128]{1,0:T(8,128)(2,1)} collective-permute-done((bf16[2048,128]{1,0:T(8,128)(2,1)}, bf16[2048,128]{1,0:T(8,128)(2,1)}, u32[]{:S(2)}, u32[]{:S(2)}) %collective-permute-start.1) | collective-permute-done | bytes 524320 | tf_op jit(solution)/shard_map/cond/branch_0_fun/ppermute | solution.py:194
  117.6 5.3 %collective-permute-start.6 = (bf16[3072,128]{1,0:T(8,128)(2,1)}, bf16[3072,128]{1,0:T(8,128)(2,1)}, u32[]{:S(2)}, u32[]{:S(2)}) collective-permute-start(bf16[3072,128]{1,0:T(8,128)(2,1)} %get-tuple-element.39), channel_id=1, source_target_pairs={{0,1},{3,2},{4,5},{7,6},{8,9},{11,10},{12,13},{15,14},{16,17},{19,... | collective-permute-start | bytes 2359304 | tf_op jit(solution)/shard_map/cond/branch_0_fun/ppermute | solution.py:194
  122.9 1.6 collective-permute-start.16
  125.8 5.2 %branch_0_fun.28 = (bf16[3072,128]{1,0:T(8,128)(2,1)}, bf16[3072,128]{1,0:T(8,128)(2,1)}) custom-call(s32[2]{0:T(128)} %pad_add_fusion.zs, bf16[3072,128]{1,0:T(8,128)(2,1)} %collective-permute-done.7.refs_0_, bf16[1,1,4194304]{2,1,0:T(2,128)(2,1)} %get-tuple-element.161.refs_0_.refs_1_.refs_3_.g, bf16[3072,128]{1,0:T(8,128)(2,1)} %collective-permute-done.9.refs_2_, ...), custom_call_target="tpu_custom_call" | custom-call | flops 6291456 | bytes 6291456 | tf_op jit(solution)/shard_map/cond/branch_0_fun/pallas_call | solution.py:59
  131.0 1.5 collective-permute-start.10
  133.9 3.6 %branch_0_fun.24 = (bf16[2048,128]{1,0:T(8,128)(2,1)}, bf16[2048,128]{1,0:T(8,128)(2,1)}) custom-call(s32[2]{0:T(128)} %pad_add_fusion.zs, bf16[2048,128]{1,0:T(8,128)(2,1)} %collective-permute-done.1.refs_0_, bf16[1,1,4194304]{2,1,0:T(2,128)(2,1)} %get-tuple-element.161.refs_0_.refs_1_.refs_3_.g, bf16[2048,128]{1,0:T(8,128)(2,1)} %collective-permute-done.3.refs_2_, ...), custom_call_target="tpu_custom_call" | custom-call | flops 4194304 | bytes 4194304 | tf_op jit(solution)/shard_map/cond/branch_0_fun/pallas_call | solution.py:59
  138.3 8.3 %collective-permute-start = (bf16[2048,128]{1,0:T(8,128)(2,1)}, bf16[2048,128]{1,0:T(8,128)(2,1)}, u32[]{:S(2)}, u32[]{:S(2)}) collective-permute-start(bf16[2048,128]{1,0:T(8,128)(2,1)} %get-tuple-element.31), channel_id=1, source_target_pairs={{0,1},{3,2},{4,5},{7,6},{8,9},{11,10},{12,13},{15,14},{16,17},{19,... | collective-permute-start | bytes 1572872 | tf_op jit(solution)/shard_map/cond/branch_0_fun/ppermute | solution.py:194
  150.8 8.3 %branch_0_fun.33 = (f32[1,1048576]{1,0:T(1,128)}, f32[1,1048576]{1,0:T(1,128)}, f32[3072,128]{1,0:T(8,128)}, bf16[3072,128]{1,0:T(8,128)(2,1)}) custom-call(s32[2]{0:T(128)} %pad_add_fusion.zs, bf16[1,1,4194304]{2,1,0:T(2,128)(2,1)} %get-tuple-element.161.refs_0_.refs_1_.refs_3_.g, bf16[3072,128]{1,0:T(8,128)(2,1)} %collective-permute-done.12.ra, ...), custom_call_target="tpu_custom_call" | custom-call | flops 15728640 | bytes 15728640 | tf_op jit(solution)/shard_map/cond/branch_0_fun/pallas_call | solution.py:59
  159.2 4.8 %collective-permute-done.11.rc = bf16[3072,128]{1,0:T(8,128)(2,1)} collective-permute-done((bf16[3072,128]{1,0:T(8,128)(2,1)}, bf16[3072,128]{1,0:T(8,128)(2,1)}, u32[]{:S(2)}, u32[]{:S(2)}) %collective-permute-start.11) | collective-permute-done | bytes 786464 | tf_op jit(solution)/shard_map/cond/branch_0_fun/ppermute | solution.py:194
  164.0 8.3 %branch_0_fun.34 = (f32[1,1048576]{1,0:T(1,128)}, f32[1,1048576]{1,0:T(1,128)}, f32[3072,128]{1,0:T(8,128)}, bf16[3072,128]{1,0:T(8,128)(2,1)}) custom-call(s32[2]{0:T(128)} %pad_add_fusion.zs, bf16[1,1,4194304]{2,1,0:T(2,128)(2,1)} %get-tuple-element.161.refs_0_.refs_1_.refs_3_.g, ...), custom_call_target="tpu_custom_call", output_to_operand_aliasing={{0}: (9, {}), {1}: (10, {})} | custom-call | flops 15728640 | bytes 15728640 | tf_op jit(solution)/shard_map/cond/branch_0_fun/pallas_call | solution.py:59
  172.9 5.4 %branch_0_fun.35 = (f32[1,1048576]{1,0:T(1,128)}, f32[1,1048576]{1,0:T(1,128)}, f32[2048,128]{1,0:T(8,128)}, bf16[2048,128]{1,0:T(8,128)(2,1)}) custom-call(s32[2]{0:T(128)} %pad_add_fusion.zs, bf16[1,1,4194304]{2,1,0:T(2,128)(2,1)} %get-tuple-element.161.refs_0_.refs_1_.refs_3_.g, ...), custom_call_target="tpu_custom_call", output_to_operand_aliasing={{0}: (9, {}), {1}: (10, {})} | custom-call | flops 10485760 | bytes 10485760 | tf_op jit(solution)/shard_map/cond/branch_0_fun/pallas_call | solution.py:59
  178.4 5.7 %branch_0_fun.36 = (f32[1,1048576]{1,0:T(1,128)}, bf16[1536,128]{1,0:T(8,128)(2,1)}, bf16[1536,128]{1,0:T(8,128)(2,1)}) custom-call(s32[2]{0:T(128)} %pad_add_fusion.zs, f32[3072,128]{1,0:T(8,128)} %get-tuple-element.55.fr, bf16[3072,128]{1,0:T(8,128)(2,1)} %collective-permute-done.20.other), custom_call_target="tpu_custom_call" | custom-call | flops 5505024 | bytes 5505024 | tf_op jit(solution)/shard_map/cond/branch_0_fun/pallas_call | solution.py:59
  184.1 5.7 %branch_0_fun.37 = (f32[1,1048576]{1,0:T(1,128)}, bf16[1536,128]{1,0:T(8,128)(2,1)}, bf16[1536,128]{1,0:T(8,128)(2,1)}) custom-call(s32[2]{0:T(128)} %pad_add_fusion.zs, f32[3072,128]{1,0:T(8,128)} %get-tuple-element.53.fr, bf16[3072,128]{1,0:T(8,128)(2,1)} %collective-permute-done.19.other, ...), custom_call_target="tpu_custom_call", output_to_operand_aliasing={{0}: (3, {})} | custom-call | flops 5505024 | bytes 5505024 | tf_op jit(solution)/shard_map/cond/branch_0_fun/pallas_call | solution.py:59
  189.8 3.1 branch_0_fun.38
  192.9 2.5 collective-permute-start.25
  195.4 1.9 collective-permute-start.21
  197.3 2.5 collective-permute-start.31
  199.8 4.6 %collective-permute-done.25.refs_6_ = bf16[1024,128]{1,0:T(8,128)(2,1)} collective-permute-done((bf16[1024,128]{1,0:T(8,128)(2,1)}, bf16[1024,128]{1,0:T(8,128)(2,1)}, u32[]{:S(2)}, u32[]{:S(2)}) %collective-permute-start.25) | collective-permute-done | bytes 262176 | tf_op jit(solution)/shard_map/cond/branch_0_fun/ppermute | solution.py:29
  204.4 2.5 collective-permute-start.37
  206.9 36.6 %collective-permute-done.23.refs_4_ = bf16[1024,128]{1,0:T(8,128)(2,1)} collective-permute-done((bf16[1024,128]{1,0:T(8,128)(2,1)}, bf16[1024,128]{1,0:T(8,128)(2,1)}, u32[]{:S(2)}, u32[]{:S(2)}) %collective-permute-start.23) | collective-permute-done | bytes 262176 | tf_op jit(solution)/shard_map/cond/branch_0_fun/ppermute | solution.py:29
  243.5 3.0 collective-permute-start.33
  246.5 14.3 %collective-permute-start.27 = (bf16[1536,128]{1,0:T(8,128)(2,1)}, bf16[1536,128]{1,0:T(8,128)(2,1)}, u32[]{:S(2)}, u32[]{:S(2)}) collective-permute-start(bf16[1536,128]{1,0:T(8,128)(2,1)} %get-tuple-element.64.refs_0_), channel_id=1, source_target_pairs={{0,1},{1,0},{2,3},{3,2},{4,5},{5,4},{6,7},{7,6},{8,9},{9,8},{10,11... | collective-permute-start | bytes 1179656 | tf_op jit(solution)/shard_map/cond/branch_0_fun/ppermute | solution.py:29
  260.8 8.0 %collective-permute-done.29.refs_4_ = bf16[1536,128]{1,0:T(8,128)(2,1)} collective-permute-done((bf16[1536,128]{1,0:T(8,128)(2,1)}, bf16[1536,128]{1,0:T(8,128)(2,1)}, u32[]{:S(2)}, u32[]{:S(2)}) %collective-permute-start.29) | collective-permute-done | bytes 393248 | tf_op jit(solution)/shard_map/cond/branch_0_fun/ppermute | solution.py:29
  269.3 15.7 %collective-permute-done.35.refs_4_ = bf16[1536,128]{1,0:T(8,128)(2,1)S(1)} collective-permute-done((bf16[1536,128]{1,0:T(8,128)(2,1)}, bf16[1536,128]{1,0:T(8,128)(2,1)S(1)}, u32[]{:S(2)}, u32[]{:S(2)}) %collective-permute-start.35) | collective-permute-done | bytes 393248 | tf_op jit(solution)/shard_map/cond/branch_0_fun/ppermute | solution.py:29
  288.4 15.8 %branch_0_fun.39.refs_8_ = bf16[1,4194304]{1,0:T(2,128)(2,1)} custom-call(s32[2]{0:T(128)} %pad_add_fusion.zs, bf16[1536,128]{1,0:T(8,128)(2,1)} %get-tuple-element.66.refs_0_, bf16[1536,128]{1,0:T(8,128)(2,1)} %get-tuple-element.67.refs_1_, bf16[1536,128]{1,0:T(8,128)(2,1)} %copy-done.12, bf16[1536,128]{1,0:T(8,128)(2,1)} %copy-done.21, ...), custom_call_target="tpu_custom_call" | custom-call | flops 9437184 | bytes 9437184 | tf_op jit(solution)/shard_map/cond/branch_0_fun/pallas_call | solution.py:59
  304.2 15.8 %branch_0_fun.40.refs_8_ = bf16[1,4194304]{1,0:T(2,128)(2,1)} custom-call(s32[2]{0:T(128)} %pad_add_fusion.zs, bf16[1536,128]{1,0:T(8,128)(2,1)} %get-tuple-element.64.refs_0_, bf16[1536,128]{1,0:T(8,128)(2,1)} %get-tuple-element.65.refs_1_, bf16[1536,128]{1,0:T(8,128)(2,1)} %collective-permute-done.27.refs_2_, ...), custom_call_target="tpu_custom_call", output_to_operand_aliasing={{}: (9, {})} | custom-call | flops 9437184 | bytes 9437184 | tf_op jit(solution)/shard_map/cond/branch_0_fun/pallas_call | solution.py:59
  320.0 6.0 %branch_0_fun.41 = bf16[1,4194304]{1,0:T(2,128)(2,1)} custom-call(s32[2]{0:T(128)} %pad_add_fusion.zs, bf16[1024,128]{1,0:T(8,128)(2,1)} %get-tuple-element.62.refs_0_, bf16[1024,128]{1,0:T(8,128)(2,1)} %get-tuple-element.63.refs_1_, bf16[1024,128]{1,0:T(8,128)(2,1)} %collective-permute-done.21.refs_2_, ...), custom_call_target="tpu_custom_call", output_to_operand_aliasing={{}: (9, {})} | custom-call | flops 6291456 | bytes 6291456 | tf_op jit(solution)/shard_map/cond/branch_0_fun/pallas_call | solution.py:59
  (70 shorter events, 13.4 us)
Async XLA Ops:
  5.7 23.3 %collective-permute-start.14 = (bf16[3072,128]{1,0:T(8,128)(2,1)}, bf16[3072,128]{1,0:T(8,128)(2,1)}, u32[]{:S(2)}, u32[]{:S(2)}) collective-permute-start(bf16[3072,128]{1,0:T(8,128)(2,1)} %branch_0_fun.30), channel_id=1, source_target_pairs={{0,1},{3,2},{4,5},{7,6},{8,9},{11,10},{12,13},{15,14},{16,17},{19,... | collective-permute-start | bytes 2359304 | tf_op jit(solution)/shard_map/cond/branch_0_fun/ppermute | solution.py:194
  15.3 31.0 %collective-permute-start.8 = (bf16[3072,128]{1,0:T(8,128)(2,1)}, bf16[3072,128]{1,0:T(8,128)(2,1)}, u32[]{:S(2)}, u32[]{:S(2)}) collective-permute-start(bf16[3072,128]{1,0:T(8,128)(2,1)} %branch_0_fun.26), channel_id=1, source_target_pairs={{0,1},{3,2},{4,5},{7,6},{8,9},{11,10},{12,13},{15,14},{16,17},{19,... | collective-permute-start | bytes 2359304 | tf_op jit(solution)/shard_map/cond/branch_0_fun/ppermute | solution.py:194
  22.0 60.2 %collective-permute-start.13 = (bf16[3072,128]{1,0:T(8,128)(2,1)}, bf16[3072,128]{1,0:T(8,128)(2,1)}, u32[]{:S(2)}, u32[]{:S(2)}) collective-permute-start(bf16[3072,128]{1,0:T(8,128)(2,1)} %get-tuple-element.44), channel_id=1, source_target_pairs={{0,1},{3,2},{4,5},{7,6},{8,9},{11,10},{12,13},{15,14},{16,17},{19,... | collective-permute-start | bytes 2359304 | tf_op jit(solution)/shard_map/cond/branch_0_fun/ppermute | solution.py:194
  26.9 46.9 %collective-permute-start.2 = (bf16[2048,128]{1,0:T(8,128)(2,1)}, bf16[2048,128]{1,0:T(8,128)(2,1)}, u32[]{:S(2)}, u32[]{:S(2)}) collective-permute-start(bf16[2048,128]{1,0:T(8,128)(2,1)} %branch_0_fun.22), channel_id=1, source_target_pairs={{0,1},{3,2},{4,5},{7,6},{8,9},{11,10},{12,13},{15,14},{16,17},{19,... | collective-permute-start | bytes 1572872 | tf_op jit(solution)/shard_map/cond/branch_0_fun/ppermute | solution.py:194
  33.2 54.1 %collective-permute-start.15 = (bf16[3072,128]{1,0:T(8,128)(2,1)}, bf16[3072,128]{1,0:T(8,128)(2,1)}, u32[]{:S(2)}, u32[]{:S(2)}) collective-permute-start(bf16[3072,128]{1,0:T(8,128)(2,1)} %branch_0_fun.31), channel_id=1, source_target_pairs={{1,2},{2,1},{5,6},{6,5},{9,10},{10,9},{13,14},{14,13},{17,18},{18,... | collective-permute-start | bytes 2359304 | tf_op jit(solution)/shard_map/cond/branch_0_fun/ppermute | solution.py:194
  39.2 83.7 %collective-permute-start.7 = (bf16[3072,128]{1,0:T(8,128)(2,1)}, bf16[3072,128]{1,0:T(8,128)(2,1)}, u32[]{:S(2)}, u32[]{:S(2)}) collective-permute-start(bf16[3072,128]{1,0:T(8,128)(2,1)} %get-tuple-element.40), channel_id=1, source_target_pairs={{0,1},{3,2},{4,5},{7,6},{8,9},{11,10},{12,13},{15,14},{16,17},{19,... | collective-permute-start | bytes 2359304 | tf_op jit(solution)/shard_map/cond/branch_0_fun/ppermute | solution.py:194
  50.6 73.9 %collective-permute-start.9 = (bf16[3072,128]{1,0:T(8,128)(2,1)}, bf16[3072,128]{1,0:T(8,128)(2,1)}, u32[]{:S(2)}, u32[]{:S(2)}) collective-permute-start(bf16[3072,128]{1,0:T(8,128)(2,1)} %branch_0_fun.27), channel_id=1, source_target_pairs={{1,2},{2,1},{5,6},{6,5},{9,10},{10,9},{13,14},{14,13},{17,18},{18,... | collective-permute-start | bytes 2359304 | tf_op jit(solution)/shard_map/cond/branch_0_fun/ppermute | solution.py:194
  73.8 57.2 %collective-permute-start.12 = (bf16[3072,128]{1,0:T(8,128)(2,1)}, bf16[3072,128]{1,0:T(8,128)(2,1)}, u32[]{:S(2)}, u32[]{:S(2)}) collective-permute-start(bf16[3072,128]{1,0:T(8,128)(2,1)} %get-tuple-element.43), channel_id=1, source_target_pairs={{0,1},{3,2},{4,5},{7,6},{8,9},{11,10},{12,13},{15,14},{16,17},{19,... | collective-permute-start | bytes 2359304 | tf_op jit(solution)/shard_map/cond/branch_0_fun/ppermute | solution.py:194
  82.2 35.4 %collective-permute-start.1 = (bf16[2048,128]{1,0:T(8,128)(2,1)}, bf16[2048,128]{1,0:T(8,128)(2,1)}, u32[]{:S(2)}, u32[]{:S(2)}) collective-permute-start(bf16[2048,128]{1,0:T(8,128)(2,1)} %get-tuple-element.32), channel_id=1, source_target_pairs={{0,1},{3,2},{4,5},{7,6},{8,9},{11,10},{12,13},{15,14},{16,17},{19,... | collective-permute-start | bytes 1572872 | tf_op jit(solution)/shard_map/cond/branch_0_fun/ppermute | solution.py:194
  87.3 45.3 %collective-permute-start.3 = (bf16[2048,128]{1,0:T(8,128)(2,1)}, bf16[2048,128]{1,0:T(8,128)(2,1)}, u32[]{:S(2)}, u32[]{:S(2)}) collective-permute-start(bf16[2048,128]{1,0:T(8,128)(2,1)} %branch_0_fun.23), channel_id=1, source_target_pairs={{1,2},{2,1},{5,6},{6,5},{9,10},{10,9},{13,14},{14,13},{17,18},{18,... | collective-permute-start | bytes 1572872 | tf_op jit(solution)/shard_map/cond/branch_0_fun/ppermute | solution.py:194
  117.6 20.6 %collective-permute-start.6 = (bf16[3072,128]{1,0:T(8,128)(2,1)}, bf16[3072,128]{1,0:T(8,128)(2,1)}, u32[]{:S(2)}, u32[]{:S(2)}) collective-permute-start(bf16[3072,128]{1,0:T(8,128)(2,1)} %get-tuple-element.39), channel_id=1, source_target_pairs={{0,1},{3,2},{4,5},{7,6},{8,9},{11,10},{12,13},{15,14},{16,17},{19,... | collective-permute-start | bytes 2359304 | tf_op jit(solution)/shard_map/cond/branch_0_fun/ppermute | solution.py:194
  122.9 23.6 %collective-permute-start.16 = (bf16[3072,128]{1,0:T(8,128)(2,1)}, bf16[3072,128]{1,0:T(8,128)(2,1)}, u32[]{:S(2)}, u32[]{:S(2)}) collective-permute-start(bf16[3072,128]{1,0:T(8,128)(2,1)} %get-tuple-element.45), channel_id=1, source_target_pairs={{1,2},{2,1},{5,6},{6,5},{9,10},{10,9},{13,14},{14,13},{17,18},{18,... | collective-permute-start | bytes 2359304 | tf_op jit(solution)/shard_map/cond/branch_0_fun/ppermute | solution.py:194
  124.5 23.6 %collective-permute-start.17 = (bf16[3072,128]{1,0:T(8,128)(2,1)}, bf16[3072,128]{1,0:T(8,128)(2,1)}, u32[]{:S(2)}, u32[]{:S(2)}) collective-permute-start(bf16[3072,128]{1,0:T(8,128)(2,1)} %get-tuple-element.46), channel_id=1, source_target_pairs={{1,0},{2,3},{5,4},{6,7},{9,8},{10,11},{13,12},{14,15},{17,16},{18,... | collective-permute-start | bytes 2359304 | tf_op jit(solution)/shard_map/cond/branch_0_fun/ppermute | solution.py:194
  131.0 28.1 %collective-permute-start.10 = (bf16[3072,128]{1,0:T(8,128)(2,1)}, bf16[3072,128]{1,0:T(8,128)(2,1)}, u32[]{:S(2)}, u32[]{:S(2)}) collective-permute-start(bf16[3072,128]{1,0:T(8,128)(2,1)} %get-tuple-element.41), channel_id=1, source_target_pairs={{1,2},{2,1},{5,6},{6,5},{9,10},{10,9},{13,14},{14,13},{17,18},{18,... | collective-permute-start | bytes 2359304 | tf_op jit(solution)/shard_map/cond/branch_0_fun/ppermute | solution.py:194
  132.6 31.4 %collective-permute-start.11 = (bf16[3072,128]{1,0:T(8,128)(2,1)}, bf16[3072,128]{1,0:T(8,128)(2,1)}, u32[]{:S(2)}, u32[]{:S(2)}) collective-permute-start(bf16[3072,128]{1,0:T(8,128)(2,1)} %get-tuple-element.42), channel_id=1, source_target_pairs={{1,0},{2,3},{5,4},{6,7},{9,8},{10,11},{13,12},{14,15},{17,16},{18,... | collective-permute-start | bytes 2359304 | tf_op jit(solution)/shard_map/cond/branch_0_fun/ppermute | solution.py:194
  138.3 34.1 %collective-permute-start = (bf16[2048,128]{1,0:T(8,128)(2,1)}, bf16[2048,128]{1,0:T(8,128)(2,1)}, u32[]{:S(2)}, u32[]{:S(2)}) collective-permute-start(bf16[2048,128]{1,0:T(8,128)(2,1)} %get-tuple-element.31), channel_id=1, source_target_pairs={{0,1},{3,2},{4,5},{7,6},{8,9},{11,10},{12,13},{15,14},{16,17},{19,... | collective-permute-start | bytes 1572872 | tf_op jit(solution)/shard_map/cond/branch_0_fun/ppermute | solution.py:194
  146.6 25.8 %collective-permute-start.4 = (bf16[2048,128]{1,0:T(8,128)(2,1)}, bf16[2048,128]{1,0:T(8,128)(2,1)}, u32[]{:S(2)}, u32[]{:S(2)}) collective-permute-start(bf16[2048,128]{1,0:T(8,128)(2,1)} %get-tuple-element.33), channel_id=1, source_target_pairs={{1,2},{2,1},{5,6},{6,5},{9,10},{10,9},{13,14},{14,13},{17,18},{18,... | collective-permute-start | bytes 1572872 | tf_op jit(solution)/shard_map/cond/branch_0_fun/ppermute | solution.py:194
  148.1 24.8 %collective-permute-start.5 = (bf16[2048,128]{1,0:T(8,128)(2,1)}, bf16[2048,128]{1,0:T(8,128)(2,1)}, u32[]{:S(2)}, u32[]{:S(2)}) collective-permute-start(bf16[2048,128]{1,0:T(8,128)(2,1)} %get-tuple-element.34), channel_id=1, source_target_pairs={{1,0},{2,3},{5,4},{6,7},{9,8},{10,11},{13,12},{14,15},{17,16},{18,... | collective-permute-start | bytes 1572872 | tf_op jit(solution)/shard_map/cond/branch_0_fun/ppermute | solution.py:194
  159.1 19.3 %collective-permute-start.20 = (bf16[3072,128]{1,0:T(8,128)(2,1)}, bf16[3072,128]{1,0:T(8,128)(2,1)}, u32[]{:S(2)}, u32[]{:S(2)}) collective-permute-start(bf16[3072,128]{1,0:T(8,128)(2,1)} %get-tuple-element.56), channel_id=1, source_target_pairs={{0,4},{4,0},{8,12},{12,8},{16,20},{20,16},{24,28},{28,24},{1,5},{5... | collective-permute-start | bytes 2359304 | tf_op jit(solution)/shard_map/cond/branch_0_fun/ppermute | solution.py:25
  172.3 11.8 %collective-permute-start.19 = (bf16[3072,128]{1,0:T(8,128)(2,1)}, bf16[3072,128]{1,0:T(8,128)(2,1)}, u32[]{:S(2)}, u32[]{:S(2)}) collective-permute-start(bf16[3072,128]{1,0:T(8,128)(2,1)} %get-tuple-element.54), channel_id=1, source_target_pairs={{0,4},{4,0},{8,12},{12,8},{16,20},{20,16},{24,28},{28,24},{1,5},{5... | collective-permute-start | bytes 2359304 | tf_op jit(solution)/shard_map/cond/branch_0_fun/ppermute | solution.py:25
  178.3 11.5 %collective-permute-start.18 = (bf16[2048,128]{1,0:T(8,128)(2,1)}, bf16[2048,128]{1,0:T(8,128)(2,1)}, u32[]{:S(2)}, u32[]{:S(2)}) collective-permute-start(bf16[2048,128]{1,0:T(8,128)(2,1)} %get-tuple-element.52), channel_id=1, source_target_pairs={{0,4},{4,0},{8,12},{12,8},{16,20},{20,16},{24,28},{28,24},{1,5},{5... | collective-permute-start | bytes 1572872 | tf_op jit(solution)/shard_map/cond/branch_0_fun/ppermute | solution.py:25
  192.9 11.4 %collective-permute-start.25 = (bf16[1024,128]{1,0:T(8,128)(2,1)}, bf16[1024,128]{1,0:T(8,128)(2,1)}, u32[]{:S(2)}, u32[]{:S(2)}) collective-permute-start(bf16[1024,128]{1,0:T(8,128)(2,1)} %get-tuple-element.62.refs_0_), channel_id=1, source_target_pairs={{0,3},{1,2},{2,1},{3,0},{4,7},{5,6},{6,5},{7,4},{8,11},{9,10},{10,... | collective-permute-start | bytes 786440 | tf_op jit(solution)/shard_map/cond/branch_0_fun/ppermute | solution.py:29
  195.4 48.0 %collective-permute-start.23 = (bf16[1024,128]{1,0:T(8,128)(2,1)}, bf16[1024,128]{1,0:T(8,128)(2,1)}, u32[]{:S(2)}, u32[]{:S(2)}) collective-permute-start(bf16[1024,128]{1,0:T(8,128)(2,1)} %get-tuple-element.62.refs_0_), channel_id=1, source_target_pairs={{0,2},{1,3},{2,0},{3,1},{4,6},{5,7},{6,4},{7,5},{8,10},{9,11},{10,... | collective-permute-start | bytes 786440 | tf_op jit(solution)/shard_map/cond/branch_0_fun/ppermute | solution.py:29
  195.4 48.0 %collective-permute-start.21 = (bf16[1024,128]{1,0:T(8,128)(2,1)}, bf16[1024,128]{1,0:T(8,128)(2,1)}, u32[]{:S(2)}, u32[]{:S(2)}) collective-permute-start(bf16[1024,128]{1,0:T(8,128)(2,1)} %get-tuple-element.62.refs_0_), channel_id=1, source_target_pairs={{0,1},{1,0},{2,3},{3,2},{4,5},{5,4},{6,7},{7,6},{8,9},{9,8},{10,11... | collective-permute-start | bytes 786440 | tf_op jit(solution)/shard_map/cond/branch_0_fun/ppermute | solution.py:29
  197.3 49.2 %collective-permute-start.31 = (bf16[1536,128]{1,0:T(8,128)(2,1)}, bf16[1536,128]{1,0:T(8,128)(2,1)S(1)}, u32[]{:S(2)}, u32[]{:S(2)}) collective-permute-start(bf16[1536,128]{1,0:T(8,128)(2,1)} %get-tuple-element.64.refs_0_), channel_id=1, source_target_pairs={{0,3},{1,2},{2,1},{3,0},{4,7},{5,6},{6,5},{7,4},{8,11},{9,10},{10,... | collective-permute-start | bytes 1179656 | tf_op jit(solution)/shard_map/cond/branch_0_fun/ppermute | solution.py:29
  199.8 69.0 %collective-permute-start.29 = (bf16[1536,128]{1,0:T(8,128)(2,1)}, bf16[1536,128]{1,0:T(8,128)(2,1)}, u32[]{:S(2)}, u32[]{:S(2)}) collective-permute-start(bf16[1536,128]{1,0:T(8,128)(2,1)} %get-tuple-element.64.refs_0_), channel_id=1, source_target_pairs={{0,2},{1,3},{2,0},{3,1},{4,6},{5,7},{6,4},{7,5},{8,10},{9,11},{10,... | collective-permute-start | bytes 1179656 | tf_op jit(solution)/shard_map/cond/branch_0_fun/ppermute | solution.py:29
  204.4 64.4 %collective-permute-start.37 = (bf16[1536,128]{1,0:T(8,128)(2,1)}, bf16[1536,128]{1,0:T(8,128)(2,1)S(1)}, u32[]{:S(2)}, u32[]{:S(2)}) collective-permute-start(bf16[1536,128]{1,0:T(8,128)(2,1)} %get-tuple-element.66.refs_0_), channel_id=1, source_target_pairs={{0,3},{1,2},{2,1},{3,0},{4,7},{5,6},{6,5},{7,4},{8,11},{9,10},{10,... | collective-permute-start | bytes 1179656 | tf_op jit(solution)/shard_map/cond/branch_0_fun/ppermute | solution.py:29
  243.5 41.6 %collective-permute-start.35 = (bf16[1536,128]{1,0:T(8,128)(2,1)}, bf16[1536,128]{1,0:T(8,128)(2,1)S(1)}, u32[]{:S(2)}, u32[]{:S(2)}) collective-permute-start(bf16[1536,128]{1,0:T(8,128)(2,1)} %get-tuple-element.66.refs_0_), channel_id=1, source_target_pairs={{0,2},{1,3},{2,0},{3,1},{4,6},{5,7},{6,4},{7,5},{8,10},{9,11},{10,... | collective-permute-start | bytes 1179656 | tf_op jit(solution)/shard_map/cond/branch_0_fun/ppermute | solution.py:29
  243.5 41.6 %collective-permute-start.33 = (bf16[1536,128]{1,0:T(8,128)(2,1)}, bf16[1536,128]{1,0:T(8,128)(2,1)S(1)}, u32[]{:S(2)}, u32[]{:S(2)}) collective-permute-start(bf16[1536,128]{1,0:T(8,128)(2,1)} %get-tuple-element.66.refs_0_), channel_id=1, source_target_pairs={{0,1},{1,0},{2,3},{3,2},{4,5},{5,4},{6,7},{7,6},{8,9},{9,8},{10,11... | collective-permute-start | bytes 1179656 | tf_op jit(solution)/shard_map/cond/branch_0_fun/ppermute | solution.py:29
  246.5 22.3 %copy-start = (bf16[1536,128]{1,0:T(8,128)(2,1)}, bf16[1536,128]{1,0:T(8,128)(2,1)S(1)}, u32[]{:S(2)}) copy-start(bf16[1536,128]{1,0:T(8,128)(2,1)S(1)} %collective-permute-done.31.refs_6_) | copy-start | bytes 1179652 | tf_op jit(solution)/shard_map/cond
  246.5 39.1 %collective-permute-start.27 = (bf16[1536,128]{1,0:T(8,128)(2,1)}, bf16[1536,128]{1,0:T(8,128)(2,1)}, u32[]{:S(2)}, u32[]{:S(2)}) collective-permute-start(bf16[1536,128]{1,0:T(8,128)(2,1)} %get-tuple-element.64.refs_0_), channel_id=1, source_target_pairs={{0,1},{1,0},{2,3},{3,2},{4,5},{5,4},{6,7},{7,6},{8,9},{9,8},{10,11... | collective-permute-start | bytes 1179656 | tf_op jit(solution)/shard_map/cond/branch_0_fun/ppermute | solution.py:29
  268.8 16.9 %collective-permute-start.32 = (bf16[1536,128]{1,0:T(8,128)(2,1)S(1)}, bf16[1536,128]{1,0:T(8,128)(2,1)S(1)}, u32[]{:S(2)}, u32[]{:S(2)}) collective-permute-start(bf16[1536,128]{1,0:T(8,128)(2,1)S(1)} %collective-permute-done.31.refs_6_), channel_id=1, source_target_pairs={{0,4},{4,0},{8,12},{12,8},{16,20},{20,16},{24,28},{28,24},{1,5},{5... | collective-permute-start | bytes 1179656 | tf_op jit(solution)/shard_map/cond/branch_0_fun/ppermute | solution.py:25
  268.8 18.1 %copy-start.6 = (bf16[1536,128]{1,0:T(8,128)(2,1)}, bf16[1536,128]{1,0:T(8,128)(2,1)S(1)}, u32[]{:S(2)}) copy-start(bf16[1536,128]{1,0:T(8,128)(2,1)S(1)} %collective-permute-done.37.refs_6_) | copy-start | bytes 1179652 | tf_op jit(solution)/shard_map/cond
  268.8 18.0 %collective-permute-start.38 = (bf16[1536,128]{1,0:T(8,128)(2,1)S(1)}, bf16[1536,128]{1,0:T(8,128)(2,1)S(1)}, u32[]{:S(2)}, u32[]{:S(2)}) collective-permute-start(bf16[1536,128]{1,0:T(8,128)(2,1)S(1)} %collective-permute-done.37.refs_6_), channel_id=1, source_target_pairs={{0,4},{4,0},{8,12},{12,8},{16,20},{20,16},{24,28},{28,24},{1,5},{5... | collective-permute-start | bytes 1179656 | tf_op jit(solution)/shard_map/cond/branch_0_fun/ppermute | solution.py:25
  285.1 1.8 copy-start.9
  285.1 2.0 collective-permute-start.36
  285.1 2.0 copy-start.12
  285.1 2.4 collective-permute-start.34
  285.6 18.6 %collective-permute-start.30 = (bf16[1536,128]{1,0:T(8,128)(2,1)}, bf16[1536,128]{1,0:T(8,128)(2,1)}, u32[]{:S(2)}, u32[]{:S(2)}) collective-permute-start(bf16[1536,128]{1,0:T(8,128)(2,1)} %collective-permute-done.29.refs_4_), channel_id=1, source_target_pairs={{0,4},{4,0},{8,12},{12,8},{16,20},{20,16},{24,28},{28,24},{1,5},{5... | collective-permute-start | bytes 1179656 | tf_op jit(solution)/shard_map/cond/branch_0_fun/ppermute | solution.py:25
  285.7 0.8 copy-start.3
  286.4 17.7 %collective-permute-start.28 = (bf16[1536,128]{1,0:T(8,128)(2,1)}, bf16[1536,128]{1,0:T(8,128)(2,1)}, u32[]{:S(2)}, u32[]{:S(2)}) collective-permute-start(bf16[1536,128]{1,0:T(8,128)(2,1)} %collective-permute-done.27.refs_2_), channel_id=1, source_target_pairs={{0,4},{4,0},{8,12},{12,8},{16,20},{20,16},{24,28},{28,24},{1,5},{5... | collective-permute-start | bytes 1179656 | tf_op jit(solution)/shard_map/cond/branch_0_fun/ppermute | solution.py:25
  286.9 0.7 copy-start.15
  286.9 33.1 %collective-permute-start.26 = (bf16[1024,128]{1,0:T(8,128)(2,1)}, bf16[1024,128]{1,0:T(8,128)(2,1)}, u32[]{:S(2)}, u32[]{:S(2)}) collective-permute-start(bf16[1024,128]{1,0:T(8,128)(2,1)} %collective-permute-done.25.refs_6_), channel_id=1, source_target_pairs={{0,4},{4,0},{8,12},{12,8},{16,20},{20,16},{24,28},{28,24},{1,5},{5... | collective-permute-start | bytes 786440 | tf_op jit(solution)/shard_map/cond/branch_0_fun/ppermute | solution.py:25
  287.0 0.8 copy-start.18
  287.0 32.9 %collective-permute-start.24 = (bf16[1024,128]{1,0:T(8,128)(2,1)}, bf16[1024,128]{1,0:T(8,128)(2,1)}, u32[]{:S(2)}, u32[]{:S(2)}) collective-permute-start(bf16[1024,128]{1,0:T(8,128)(2,1)} %collective-permute-done.23.refs_4_), channel_id=1, source_target_pairs={{0,4},{4,0},{8,12},{12,8},{16,20},{20,16},{24,28},{28,24},{1,5},{5... | collective-permute-start | bytes 786440 | tf_op jit(solution)/shard_map/cond/branch_0_fun/ppermute | solution.py:25
  287.6 0.8 copy-start.21
  287.6 32.4 %collective-permute-start.22 = (bf16[1024,128]{1,0:T(8,128)(2,1)}, bf16[1024,128]{1,0:T(8,128)(2,1)}, u32[]{:S(2)}, u32[]{:S(2)}) collective-permute-start(bf16[1024,128]{1,0:T(8,128)(2,1)} %collective-permute-done.21.refs_2_), channel_id=1, source_target_pairs={{0,4},{4,0},{8,12},{12,8},{16,20},{20,16},{24,28},{28,24},{1,5},{5... | collective-permute-start | bytes 786440 | tf_op jit(solution)/shard_map/cond/branch_0_fun/ppermute | solution.py:25

commit v3 on v2

v3 whole, which is shorter than its diff:
```python
import functools

import jax
import jax.numpy as jnp
from jax import lax
from jax.experimental import pallas as pl
from jax.experimental.pallas import tpu as pltpu
from jax.sharding import PartitionSpec as P


LANES = 128
VMEM = 67043328
CUTS = (3, 3, 2)
UNITS = 8
OUTER = ((0, 1), (3, 2))
MIDDLE = ((1, 2), (2, 1))
INNER = ((1, 0), (2, 3))
bf16 = jnp.bfloat16
f32 = jnp.float32
ANY = pl.BlockSpec(memory_space=pl.ANY)


def swapped(value, level):
    pairs = [(r, r ^ 2**level) for r in range(lax.axis_size("rep"))]
    return lax.ppermute(value, "rep", pairs)


def crossed(value, mask):
    return lax.ppermute(value, "zero", [(i, i ^ mask) for i in range(lax.axis_size("zero"))])


def far(z, p):
    return jnp.where(z < 2, 3 - p, p)


def pieces(rows, most):
    step = most
    while rows % step:
        step //= 2

    def run(body):
        def one(i, carry):
            at = pl.multiple_of(i * step, step)
            flat = pl.ds(pl.multiple_of(i * (step * LANES), step * LANES), step * LANES)
            body(pl.ds(at, step), flat, step)
            return carry

        lax.fori_loop(0, rows // step, one, 0)

    return run


def pack_body(sc, reads, writes):
    (g,), (o,) = reads, writes

    @pieces(o.shape[0], 256)
    def _(row, flat, step):
        o[row, :] = g[0, :, flat].reshape(step, LANES)


def sum_body(sc, reads, writes):
    (r, g), (o,) = reads, writes

    @pieces(o.shape[0], 128)
    def _(row, flat, step):
        own = g[0, :, flat].astype(f32).reshape(step, LANES)
        o[row, :] = (r[row, :].astype(f32) + own).astype(bf16)


def adam_body(sc, reads, writes):
    g, ra, rb, rc, m, v, w = reads
    mo, vo, fr, fb = writes
    one, two = sc[0], sc[1]

    @pieces(fr.shape[0], 64)
    def _(row, flat, step):
        shape = (step, LANES)
        total = g[0, :, flat].astype(f32).reshape(shape)
        total = total + ra[row, :].astype(f32) + rb[row, :].astype(f32) + rc[row, :].astype(f32)
        grad = total * 0.25
        m_new = 0.9 * m[:, flat].reshape(shape) + 0.1 * grad
        v_new = 0.999 * v[:, flat].reshape(shape) + 0.001 * grad * grad
        mo[:, flat] = m_new.reshape(1, step * LANES)
        vo[:, flat] = v_new.reshape(1, step * LANES)
        old = w[:, flat].reshape(shape)
        root = jnp.sqrt(v_new * two) + 1e-08
        fresh = old - 0.02 * (m_new * one / root + 0.1 * old)
        fr[row, :] = fresh
        fb[row, :] = fresh.astype(bf16)


def mean_body(sc, reads, writes):
    (fr, other), (wo, ab) = reads, writes

    @pieces(fr.shape[0], 64)
    def _(row, flat, step):
        avg = 0.5 * (fr[row, :] + other[row, :].astype(f32))
        wo[:, flat] = avg.reshape(1, step * LANES)
        ab[row, :] = avg.astype(bf16)


def spread_body(sc, reads, writes):
    (src,), (o,) = reads, writes

    @pieces(src.shape[0], 256)
    def _(row, flat, step):
        o[:, flat] = src[row, :].reshape(1, step * LANES)


def staged(body, scalars, ins, outs, plan, alias=(), scale=None, cost=0):
    count = len(ins)
    buffers = [(shape, kind) for reads, writes in plan for _, _, shape, kind in reads + writes]

    def kernel(zs, *refs):
        if scale is not None:
            sc, refs = refs[0], refs[1:]
        else:
            sc = None
        sources, sinks = refs[:count], refs[count : count + len(outs)]
        scratch, sems = refs[count + len(outs) : -1], refs[-1]
        at, work = 0, []
        for reads, writes in plan:
            loads, stores = [], []
            for i, where, _, _ in reads:
                copy = pltpu.make_async_copy(sources[i].at[where(zs)], scratch[at], sems.at[at])
                loads.append((copy, scratch[at]))
                at += 1
            for i, where, _, _ in writes:
                copy = pltpu.make_async_copy(scratch[at], sinks[i].at[where(zs)], sems.at[at])
                stores.append((copy, scratch[at]))
                at += 1
            work.append((loads, stores))
        for loads, _ in work:
            for copy, _ in loads:
                copy.start()
        for loads, stores in work:
            for copy, _ in loads:
                copy.wait()
            body(sc, [ref for _, ref in loads], [ref for _, ref in stores])
            for copy, _ in stores:
                copy.start()
        for _, stores in work:
            for copy, _ in stores:
                copy.wait()

    first = [] if scale is None else [scale]
    shift = 1 + len(first)
    return pl.pallas_call(
        kernel,
        out_shape=outs,
        grid_spec=pltpu.PrefetchScalarGridSpec(
            num_scalar_prefetch=1,
            grid=(),
            in_specs=[pl.BlockSpec(memory_space=pltpu.SMEM)] * len(first) + [ANY] * count,
            out_specs=[ANY] * len(outs),
            scratch_shapes=[pltpu.VMEM(shape, kind) for shape, kind in buffers]
            + [pltpu.SemaphoreType.DMA((len(buffers),))],
        ),
        input_output_aliases={a + shift: b for a, b in alias},
        cost_estimate=pl.CostEstimate(flops=cost, bytes_accessed=cost, transcendentals=0),
        compiler_params=pltpu.CompilerParams(vmem_limit_bytes=VMEM),
    )(scalars, *first, *ins)


def line_branch(level, grads, master, moment_one, moment_two, step_index):
    size = master.shape[1]
    rows = size // LANES
    z = lax.axis_index("zero").astype(jnp.int32)
    half = (lax.axis_index("rep").astype(jnp.int32) // 2**level) % 2
    count = (step_index[0] + 1).astype(f32)
    scale = jnp.stack(
        [1.0 / (1.0 - jnp.power(f32(0.9), count)), 1.0 / (1.0 - jnp.power(f32(0.999), count))]
    )
    scalars = jnp.stack([z, half])
    unit = rows // UNITS
    kept = {}
    whole = jax.ShapeDtypeStruct((1, size), f32)
    compact = lambda n: jax.ShapeDtypeStruct((n, LANES), bf16)

    def cuts(n, most):
        parts = max(1, n // most)
        return [(i * (n // parts), n // parts) for i in range(parts)]

    def rows_at(i, at, n, kind=bf16):
        return (i, lambda zs: pl.ds(at, n), (n, LANES), kind)

    def flat_at(i, at, n):
        return (i, lambda zs: (slice(None), pl.ds(at * LANES, n * LANES)), (1, n * LANES), f32)

    def grad_at(i, shard, at, n):
        def where(zs):
            first = pl.multiple_of((shard(zs[0]) * rows + at) * LANES, 8 * LANES)
            return (slice(None), slice(None), pl.ds(first, n * LANES))

        return (i, where, (1, 1, n * LANES), bf16)

    def pack(part, places):
        _, start, n = part
        plan = [
            ([grad_at(0, functools.partial(far, p=p), start + at, r)], [rows_at(q, at, r)])
            for q, p in enumerate(places)
            for at, r in cuts(n, 1024)
        ]
        return staged(
            pack_body, scalars, [grads], [compact(n)] * len(places), plan,
            cost=n * LANES * 6 * len(places),
        )

    def add(part, received, places):
        _, start, n = part
        plan = [
            (
                [rows_at(1 + q, at, r), grad_at(0, functools.partial(far, p=p), start + at, r)],
                [rows_at(q, at, r)],
            )
            for q, p in enumerate(places)
            for at, r in cuts(n, 1024)
        ]
        return staged(
            sum_body, scalars, [grads, *received], [compact(n)] * len(places), plan,
            cost=n * LANES * 8 * len(places),
        )

    def send(value, pairs):
        return lax.ppermute(value, "zero", list(pairs))

    def keep(names, ins):
        if names[0] not in kept:
            return ()
        ins += [kept[name] for name in names]
        return tuple((len(ins) - len(names) + i, i) for i in range(len(names)))

    def adam(part, received):
        _, start, n = part
        ins = [grads, *received, moment_one, moment_two, master]
        alias = keep(("m", "v"), ins)
        plan = [
            (
                [grad_at(0, lambda z: z, start + at, r)]
                + [rows_at(i, at, r) for i in (1, 2, 3)]
                + [flat_at(i, start + at, r) for i in (4, 5, 6)],
                [flat_at(0, start + at, r), flat_at(1, start + at, r)]
                + [rows_at(2, at, r, f32), rows_at(3, at, r)],
            )
            for at, r in cuts(n, 512)
        ]
        kept["m"], kept["v"], fresh, fresh16 = staged(
            adam_body, scalars, ins,
            [whole, whole, jax.ShapeDtypeStruct((n, LANES), f32), compact(n)],
            plan, alias, scale, cost=n * LANES * 40,
        )
        return fresh, fresh16

    def side(zs, p):
        return zs[1] if p == 0 else 1 - zs[1]

    def mean(part, fresh, other):
        _, start, n = part
        ins = [fresh, other]
        alias = keep(("w",), ins)
        plan = []
        for p in (0, 1):
            for at, r in cuts(n // 2, 512):
                row = lambda zs, p=p, at=at: pl.multiple_of(side(zs, p) * (n // 2) + at, 8)
                here = lambda zs, row=row, r=r: pl.ds(row(zs), r)
                flat = lambda zs, row=row, r=r: (
                    slice(None),
                    pl.ds(pl.multiple_of((start + row(zs)) * LANES, 8 * LANES), r * LANES),
                )
                plan.append(
                    (
                        [(0, here, (r, LANES), f32), (1, here, (r, LANES), bf16)],
                        [(0, flat, (1, r * LANES), f32), rows_at(1 + p, at, r)],
                    )
                )
        kept["w"], mine, yours = staged(
            mean_body, scalars, ins, [whole, compact(n // 2), compact(n // 2)],
            plan, alias, cost=n * LANES * 14,
        )
        return mine, yours

    def spread(part, mine, yours):
        _, start, n = part
        nh = n // 2
        ins = [mine, yours]
        for mask in (1, 2, 3):
            got = crossed(mine, mask)
            ins += [got, swapped(got, level)]
        plan = []
        for q in range(8):

            def where(zs, q=q):
                shard = jnp.bitwise_xor(zs[0], q // 2)
                first = shard * rows + start + side(zs, q % 2) * nh
                return (slice(None), pl.ds(pl.multiple_of(first * LANES, 8 * LANES), nh * LANES))

            plan.append(([rows_at(q, 0, nh)], [(0, where, (1, nh * LANES), bf16)]))
        alias = keep(("p",), ins)
        (kept["p"],) = staged(
            spread_body, scalars, ins,
            [jax.ShapeDtypeStruct((1, 4 * size), bf16)], plan, alias, cost=n * LANES * 24,
        )

    parts, start = [], 0
    for k, cut in enumerate(CUTS):
        parts.append((k, start, cut * unit))
        start += cut * unit
    for part in parts:
        k = part[0]
        (e,) = pack(part, (0,))
        f, g = pack(part, (1, 2))
        re = send(e, OUTER)
        rf = send(f, OUTER)
        rg = send(g, OUTER)
        (sm,) = add(part, (re,), (0,))
        rm = send(sm, MIDDLE)
        sn, si = add(part, (rf, rm), (1, 3))
        rn = send(sn, MIDDLE)
        ri = send(si, INNER)
        fresh, fresh16 = adam(part, (rg, rn, ri))
        other = swapped(fresh16, level)
        mine, yours = mean(part, fresh, other)
        spread(part, mine, yours)
    return kept["w"], kept["m"], kept["v"], kept["p"]


def line_step(*args):
    nbits = lax.axis_size("rep").bit_length() - 1

    def branch(level, *args):
        return line_branch(level, *args)

    bit = args[-1][0] % nbits
    return lax.switch(bit, [functools.partial(branch, b) for b in range(nbits)], *args)


def plain_step(grads, master, moment_one, moment_two, step_index):
    loop_size = lax.axis_size("zero")
    nbits = lax.axis_size("rep").bit_length() - 1
    tstep = step_index[0]
    count = (tstep + 1).astype(f32)
    terms = grads.reshape(-1, LANES)
    g = lax.psum_scatter(terms, "zero", scatter_dimension=0, tiled=True).astype(f32)
    g = g.reshape(master.shape) / loop_size
    m_new = 0.9 * moment_one + 0.1 * g
    v_new = 0.999 * moment_two + 0.001 * g * g
    corr_one = 1.0 - jnp.power(f32(0.9), count)
    corr_two = 1.0 - jnp.power(f32(0.999), count)
    fresh = master - 0.02 * (m_new / corr_one / (jnp.sqrt(v_new / corr_two) + 1e-08) + 0.1 * master)
    other = jnp.zeros_like(fresh)
    for level in range(nbits):
        other = jnp.where(tstep % nbits == level, swapped(fresh, level), other)
    averaged = 0.5 * (fresh + other)
    whole = lax.all_gather(averaged.astype(bf16).reshape(-1, LANES), "zero", axis=0, tiled=True)
    return (averaged, m_new, v_new, whole.reshape(1, -1))


def shards(*args):
    if lax.axis_size("zero") == 4:
        return line_step(*args)
    return plain_step(*args)


def solution(mesh):
    return jax.shard_map(
        shards,
        mesh=mesh,
        in_specs=(
            P("rep", "zero", None),
            P("rep", "zero"),
            P("rep", "zero"),
            P("rep", "zero"),
            P(),
        ),
        out_specs=(P("rep", "zero"), P("rep", "zero"), P("rep", "zero"), P("rep", None)),
        check_vma=False,
    )
```

time: 328 us -> 298 us (0.909)
  Pallas kernels: 122 us -> 83.3 us
  waiting for transfers between devices: 117 us -> 126 us
    pallas_call x21, Pallas kernels: 122 us -> 83.3 us  [staged(): pl.pallas_call(kernel, out_shape=outs, grid_spec=pltpu.PrefetchScalarGrid...]
    ppermute x18, waiting for transfers between devices: 51.6 us -> 60.9 us  [send(): return lax.ppermute(value, 'zero', list(pairs))]
  transfers between devices with their start and end apart: 39 -> 39, of which waited for: 9 -> 12; matrix products, arithmetic and copies ran while one was open for 0% -> 0% of each run, Pallas kernels for 33% -> 25%
where the time goes in v3:
time: 298 us; the launch traced here: 297 us
  waiting for transfers between devices  126 us (42%)
  Pallas kernels  83.3 us (28%)
  starting transfers between devices  81.6 us (27%)
    pallas_call x21, Pallas kernels, staged(): pl.pallas_call(kernel, out_shape=outs, grid_spec=pltpu.PrefetchScalarGrid...  83.3 us
    ppermute x9, waiting for transfers between devices, crossed(): lax.ppermute(value, 'zero', [(i, i ^ mask) for i in range(lax.axis_size('...  65 us
    ppermute x18, waiting for transfers between devices, send(): return lax.ppermute(value, 'zero', list(pairs))  60.9 us
    ppermute x18, starting transfers between devices, send(): return lax.ppermute(value, 'zero', list(pairs))  52.5 us
    ppermute x9, starting transfers between devices, crossed(): lax.ppermute(value, 'zero', [(i, i ^ mask) for i in range(lax.axis_size('...  26.7 us
  transfers between devices with their start and end apart: 39, of which 12 were waited for; matrix products, arithmetic and copies ran while one was open for 0% of the time, Pallas kernels for 25%

profile of v3, /device:TPU:0, one launch (start us, length us, event | category | flops | bytes accessed | tf_op | source)
XLA Modules:
  0.0 296.5 jit_solution(13683923299931911035)
XLA Ops:
  1.3 295.1 %conditional.1 = (f32[1,1048576]{1,0:T(1,128)}, f32[1,1048576]{1,0:T(1,128)}, f32[1,1048576]{1,0:T(1,128)}, bf16[1,4194304]{1,0:T(2,128)(2,1)}) conditional(s32[]{:T(128)} %clamp.3, (s32[1]{0:T(128)}, bf16[1,1,4194304]{2,1,0:T(2,128)(2,1)}, f32[1,1048576]{1,0:T(1,128)}, f32[1,1048576]{1,0:T(1,128)}, ...), branch_computations={%region_0.1_spmd, %region_1.2_spmd, %region_2.3_spmd} | conditional | flops 125829160 | bytes 222300224 | solution.py:334
  1.9 2.8 branch_0_fun.30
  4.8 5.8 %collective-permute-start.14 = (bf16[3072,128]{1,0:T(8,128)(2,1)}, bf16[3072,128]{1,0:T(8,128)(2,1)}, u32[]{:S(2)}, u32[]{:S(2)}) collective-permute-start(bf16[3072,128]{1,0:T(8,128)(2,1)} %branch_0_fun.30), channel_id=1, source_target_pairs={{0,1},{3,2},{4,5},{7,6},{8,9},{11,10},{12,13},{15,14},{16,17},{19,... | collective-permute-start | bytes 2359304 | tf_op jit(solution)/shard_map/cond/branch_0_fun/ppermute | solution.py:225
  10.6 2.8 branch_0_fun.26
  13.4 2.2 collective-permute-start.8
  15.6 3.4 %branch_0_fun.29 = (bf16[3072,128]{1,0:T(8,128)(2,1)}, bf16[3072,128]{1,0:T(8,128)(2,1)}) custom-call(s32[2]{0:T(128)} %pad_add_fusion.zs, bf16[1,1,4194304]{2,1,0:T(2,128)(2,1)} %get-tuple-element.161.refs_0_.refs_1_), custom_call_target="tpu_custom_call" | custom-call | flops 4718592 | bytes 4718592 | tf_op jit(solution)/shard_map/cond/branch_0_fun/pallas_call | solution.py:148
  19.0 2.2 collective-permute-start.13
  21.2 2.7 branch_0_fun.22
  23.9 2.1 collective-permute-start.2
  26.0 1.9 collective-permute-done.14.refs_1_
  27.9 3.2 %branch_0_fun.31 = bf16[3072,128]{1,0:T(8,128)(2,1)} custom-call(s32[2]{0:T(128)} %pad_add_fusion.zs, bf16[1,1,4194304]{2,1,0:T(2,128)(2,1)} %get-tuple-element.161.refs_0_.refs_1_, bf16[3072,128]{1,0:T(8,128)(2,1)} %collective-permute-done.14.refs_1_), custom_call_target="tpu_custom_call" | custom-call | flops 3145728 | bytes 3145728 | tf_op jit(solution)/shard_map/cond/branch_0_fun/pallas_call | solution.py:148
  32.7 3.4 %branch_0_fun.25 = (bf16[3072,128]{1,0:T(8,128)(2,1)}, bf16[3072,128]{1,0:T(8,128)(2,1)}) custom-call(s32[2]{0:T(128)} %pad_add_fusion.zs, bf16[1,1,4194304]{2,1,0:T(2,128)(2,1)} %get-tuple-element.161.refs_0_.refs_1_), custom_call_target="tpu_custom_call" | custom-call | flops 4718592 | bytes 4718592 | tf_op jit(solution)/shard_map/cond/branch_0_fun/pallas_call | solution.py:148
  36.1 7.3 %collective-permute-start.7 = (bf16[3072,128]{1,0:T(8,128)(2,1)}, bf16[3072,128]{1,0:T(8,128)(2,1)}, u32[]{:S(2)}, u32[]{:S(2)}) collective-permute-start(bf16[3072,128]{1,0:T(8,128)(2,1)} %get-tuple-element.40), channel_id=1, source_target_pairs={{0,1},{3,2},{4,5},{7,6},{8,9},{11,10},{12,13},{15,14},{16,17},{19,... | collective-permute-start | bytes 2359304 | tf_op jit(solution)/shard_map/cond/branch_0_fun/ppermute | solution.py:225
  44.8 3.2 %branch_0_fun.27 = bf16[3072,128]{1,0:T(8,128)(2,1)} custom-call(s32[2]{0:T(128)} %pad_add_fusion.zs, bf16[1,1,4194304]{2,1,0:T(2,128)(2,1)} %get-tuple-element.161.refs_0_.refs_1_, bf16[3072,128]{1,0:T(8,128)(2,1)} %collective-permute-done.8.refs_1_), custom_call_target="tpu_custom_call" | custom-call | flops 3145728 | bytes 3145728 | tf_op jit(solution)/shard_map/cond/branch_0_fun/pallas_call | solution.py:148
  48.0 1.6 collective-permute-start.9
  49.6 23.3 %collective-permute-done.2.refs_1_ = bf16[2048,128]{1,0:T(8,128)(2,1)} collective-permute-done((bf16[2048,128]{1,0:T(8,128)(2,1)}, bf16[2048,128]{1,0:T(8,128)(2,1)}, u32[]{:S(2)}, u32[]{:S(2)}) %collective-permute-start.2) | collective-permute-done | bytes 524320 | tf_op jit(solution)/shard_map/cond/branch_0_fun/ppermute | solution.py:225
  72.9 5.3 %collective-permute-start.12 = (bf16[3072,128]{1,0:T(8,128)(2,1)}, bf16[3072,128]{1,0:T(8,128)(2,1)}, u32[]{:S(2)}, u32[]{:S(2)}) collective-permute-start(bf16[3072,128]{1,0:T(8,128)(2,1)} %get-tuple-element.43), channel_id=1, source_target_pairs={{0,1},{3,2},{4,5},{7,6},{8,9},{11,10},{12,13},{15,14},{16,17},{19,... | collective-permute-start | bytes 2359304 | tf_op jit(solution)/shard_map/cond/branch_0_fun/ppermute | solution.py:225
  78.2 3.0 %branch_0_fun.21 = (bf16[2048,128]{1,0:T(8,128)(2,1)}, bf16[2048,128]{1,0:T(8,128)(2,1)}) custom-call(s32[2]{0:T(128)} %pad_add_fusion.zs, bf16[1,1,4194304]{2,1,0:T(2,128)(2,1)} %get-tuple-element.161.refs_0_.refs_1_), custom_call_target="tpu_custom_call" | custom-call | flops 3145728 | bytes 3145728 | tf_op jit(solution)/shard_map/cond/branch_0_fun/pallas_call | solution.py:148
  81.2 2.1 collective-permute-start.1
  83.3 2.9 branch_0_fun.23
  87.8 4.1 %branch_0_fun.32 = (bf16[3072,128]{1,0:T(8,128)(2,1)}, bf16[3072,128]{1,0:T(8,128)(2,1)}) custom-call(s32[2]{0:T(128)} %pad_add_fusion.zs, bf16[1,1,4194304]{2,1,0:T(2,128)(2,1)} %get-tuple-element.161.refs_0_.refs_1_, bf16[3072,128]{1,0:T(8,128)(2,1)} %collective-permute-done.13.refs_1_, bf16[3072,128]{1,0:T(8,128)(2,1)} %collective-permute-done.15.refs_2_), custom_call_target="tpu_custom_call" | custom-call | flops 6291456 | bytes 6291456 | tf_op jit(solution)/shard_map/cond/branch_0_fun/pallas_call | solution.py:148
  91.9 24.8 %collective-permute-done.1.refs_1_ = bf16[2048,128]{1,0:T(8,128)(2,1)} collective-permute-done((bf16[2048,128]{1,0:T(8,128)(2,1)}, bf16[2048,128]{1,0:T(8,128)(2,1)}, u32[]{:S(2)}, u32[]{:S(2)}) %collective-permute-start.1) | collective-permute-done | bytes 524320 | tf_op jit(solution)/shard_map/cond/branch_0_fun/ppermute | solution.py:225
  116.7 5.3 %collective-permute-start.6 = (bf16[3072,128]{1,0:T(8,128)(2,1)}, bf16[3072,128]{1,0:T(8,128)(2,1)}, u32[]{:S(2)}, u32[]{:S(2)}) collective-permute-start(bf16[3072,128]{1,0:T(8,128)(2,1)} %get-tuple-element.39), channel_id=1, source_target_pairs={{0,1},{3,2},{4,5},{7,6},{8,9},{11,10},{12,13},{15,14},{16,17},{19,... | collective-permute-start | bytes 2359304 | tf_op jit(solution)/shard_map/cond/branch_0_fun/ppermute | solution.py:225
  122.0 1.6 collective-permute-start.16
  124.8 4.1 %branch_0_fun.28 = (bf16[3072,128]{1,0:T(8,128)(2,1)}, bf16[3072,128]{1,0:T(8,128)(2,1)}) custom-call(s32[2]{0:T(128)} %pad_add_fusion.zs, bf16[1,1,4194304]{2,1,0:T(2,128)(2,1)} %get-tuple-element.161.refs_0_.refs_1_, bf16[3072,128]{1,0:T(8,128)(2,1)} %collective-permute-done.7.refs_1_, bf16[3072,128]{1,0:T(8,128)(2,1)} %collective-permute-done.9.refs_2_), custom_call_target="tpu_custom_call" | custom-call | flops 6291456 | bytes 6291456 | tf_op jit(solution)/shard_map/cond/branch_0_fun/pallas_call | solution.py:148
  131.8 3.5 %branch_0_fun.24 = (bf16[2048,128]{1,0:T(8,128)(2,1)}, bf16[2048,128]{1,0:T(8,128)(2,1)}) custom-call(s32[2]{0:T(128)} %pad_add_fusion.zs, bf16[1,1,4194304]{2,1,0:T(2,128)(2,1)} %get-tuple-element.161.refs_0_.refs_1_, bf16[2048,128]{1,0:T(8,128)(2,1)} %collective-permute-done.1.refs_1_, bf16[2048,128]{1,0:T(8,128)(2,1)} %collective-permute-done.3.refs_2_), custom_call_target="tpu_custom_call" | custom-call | flops 4194304 | bytes 4194304 | tf_op jit(solution)/shard_map/cond/branch_0_fun/pallas_call | solution.py:148
  135.3 2.0 collective-permute-done.6.refs_2_
  137.3 7.0 %collective-permute-start = (bf16[2048,128]{1,0:T(8,128)(2,1)}, bf16[2048,128]{1,0:T(8,128)(2,1)}, u32[]{:S(2)}, u32[]{:S(2)}) collective-permute-start(bf16[2048,128]{1,0:T(8,128)(2,1)} %get-tuple-element.32), channel_id=1, source_target_pairs={{0,1},{3,2},{4,5},{7,6},{8,9},{11,10},{12,13},{15,14},{16,17},{19,... | collective-permute-start | bytes 1572872 | tf_op jit(solution)/shard_map/cond/branch_0_fun/ppermute | solution.py:225
  148.9 8.0 %branch_0_fun.33 = (f32[1,1048576]{1,0:T(1,128)}, f32[1,1048576]{1,0:T(1,128)}, f32[3072,128]{1,0:T(8,128)}, bf16[3072,128]{1,0:T(8,128)(2,1)}) custom-call(s32[2]{0:T(128)} %pad_add_fusion.zs, f32[2]{0:T(128)} %pad_maximum_fusion.refs_0_, bf16[1,1,4194304]{2,1,0:T(2,128)(2,1)} %get-tuple-element.161.refs_0_.refs_1_, ...), custom_call_target="tpu_custom_call" | custom-call | flops 15728640 | bytes 15728640 | tf_op jit(solution)/shard_map/cond/branch_0_fun/pallas_call | solution.py:148
  156.9 6.1 %collective-permute-done.11.refs_4_ = bf16[3072,128]{1,0:T(8,128)(2,1)} collective-permute-done((bf16[3072,128]{1,0:T(8,128)(2,1)}, bf16[3072,128]{1,0:T(8,128)(2,1)}, u32[]{:S(2)}, u32[]{:S(2)}) %collective-permute-start.11) | collective-permute-done | bytes 786464 | tf_op jit(solution)/shard_map/cond/branch_0_fun/ppermute | solution.py:225
  163.0 8.0 %branch_0_fun.34 = (f32[1,1048576]{1,0:T(1,128)}, f32[1,1048576]{1,0:T(1,128)}, f32[3072,128]{1,0:T(8,128)}, bf16[3072,128]{1,0:T(8,128)(2,1)}) custom-call(s32[2]{0:T(128)} %pad_add_fusion.zs, f32[2]{0:T(128)} %pad_maximum_fusion.refs_0_, bf16[1,1,4194304]{2,1,0:T(2,128)(2,1)} %get-tuple-element.161.refs_0_.refs_1_, ...), custom_call_target="tpu_custom_call", output_to_operand_aliasing={{0}: (9, {}), {1}: (10, {})} | custom-call | flops 15728640 | bytes 15728640 | tf_op jit(solution)/shard_map/cond/branch_0_fun/pallas_call | solution.py:148
  172.0 5.7 %branch_0_fun.35 = (f32[1,1048576]{1,0:T(1,128)}, f32[1,1048576]{1,0:T(1,128)}, f32[2048,128]{1,0:T(8,128)}, bf16[2048,128]{1,0:T(8,128)(2,1)}) custom-call(s32[2]{0:T(128)} %pad_add_fusion.zs, f32[2]{0:T(128)} %pad_maximum_fusion.refs_0_, bf16[1,1,4194304]{2,1,0:T(2,128)(2,1)} %get-tuple-element.161.refs_0_.refs_1_, ...), custom_call_target="tpu_custom_call", output_to_operand_aliasing={{0}: (9, {}), {1}: (10, {})} | custom-call | flops 10485760 | bytes 10485760 | tf_op jit(solution)/shard_map/cond/branch_0_fun/pallas_call | solution.py:148
  177.8 3.3 %branch_0_fun.36 = (f32[1,1048576]{1,0:T(1,128)}, bf16[1536,128]{1,0:T(8,128)(2,1)}, bf16[1536,128]{1,0:T(8,128)(2,1)}) custom-call(s32[2]{0:T(128)} %pad_add_fusion.zs, f32[3072,128]{1,0:T(8,128)} %get-tuple-element.55.refs_0_, bf16[3072,128]{1,0:T(8,128)(2,1)} %collective-permute-done.20.refs_1_), custom_call_target="tpu_custom_call" | custom-call | flops 5505024 | bytes 5505024 | tf_op jit(solution)/shard_map/cond/branch_0_fun/pallas_call | solution.py:148
  181.2 3.3 %branch_0_fun.37 = (f32[1,1048576]{1,0:T(1,128)}, bf16[1536,128]{1,0:T(8,128)(2,1)}, bf16[1536,128]{1,0:T(8,128)(2,1)}) custom-call(s32[2]{0:T(128)} %pad_add_fusion.zs, f32[3072,128]{1,0:T(8,128)} %get-tuple-element.53.refs_0_, bf16[3072,128]{1,0:T(8,128)(2,1)} %collective-permute-done.19.refs_1_, ...), custom_call_target="tpu_custom_call", output_to_operand_aliasing={{0}: (3, {})} | custom-call | flops 5505024 | bytes 5505024 | tf_op jit(solution)/shard_map/cond/branch_0_fun/pallas_call | solution.py:148
  184.5 3.0 %branch_0_fun.38 = (f32[1,1048576]{1,0:T(1,128)}, bf16[1024,128]{1,0:T(8,128)(2,1)}, bf16[1024,128]{1,0:T(8,128)(2,1)}) custom-call(s32[2]{0:T(128)} %pad_add_fusion.zs, f32[2048,128]{1,0:T(8,128)} %get-tuple-element.51.refs_0_, bf16[2048,128]{1,0:T(8,128)(2,1)} %collective-permute-done.18.refs_1_, ...), custom_call_target="tpu_custom_call", output_to_operand_aliasing={{0}: (3, {})} | custom-call | flops 3670016 | bytes 3670016 | tf_op jit(solution)/shard_map/cond/branch_0_fun/pallas_call | solution.py:148
  187.5 2.5 collective-permute-start.25
  190.0 1.9 collective-permute-start.21
  191.9 2.5 collective-permute-start.31
  194.4 4.6 %collective-permute-done.25.refs_6_ = bf16[1024,128]{1,0:T(8,128)(2,1)} collective-permute-done((bf16[1024,128]{1,0:T(8,128)(2,1)}, bf16[1024,128]{1,0:T(8,128)(2,1)}, u32[]{:S(2)}, u32[]{:S(2)}) %collective-permute-start.25) | collective-permute-done | bytes 262176 | tf_op jit(solution)/shard_map/cond/branch_0_fun/ppermute | solution.py:29
  199.0 2.5 collective-permute-start.37
  201.5 36.7 %collective-permute-done.23.refs_4_ = bf16[1024,128]{1,0:T(8,128)(2,1)} collective-permute-done((bf16[1024,128]{1,0:T(8,128)(2,1)}, bf16[1024,128]{1,0:T(8,128)(2,1)}, u32[]{:S(2)}, u32[]{:S(2)}) %collective-permute-start.23) | collective-permute-done | bytes 262176 | tf_op jit(solution)/shard_map/cond/branch_0_fun/ppermute | solution.py:29
  238.2 3.0 %collective-permute-start.33 = (bf16[1536,128]{1,0:T(8,128)(2,1)}, bf16[1536,128]{1,0:T(8,128)(2,1)S(1)}, u32[]{:S(2)}, u32[]{:S(2)}) collective-permute-start(bf16[1536,128]{1,0:T(8,128)(2,1)} %get-tuple-element.66.refs_0_), channel_id=1, source_target_pairs={{0,1},{1,0},{2,3},{3,2},{4,5},{5,4},{6,7},{7,6},{8,9},{9,8},{10,11... | collective-permute-start | bytes 1179656 | tf_op jit(solution)/shard_map/cond/branch_0_fun/ppermute | solution.py:29
  241.2 14.3 %collective-permute-start.27 = (bf16[1536,128]{1,0:T(8,128)(2,1)}, bf16[1536,128]{1,0:T(8,128)(2,1)}, u32[]{:S(2)}, u32[]{:S(2)}) collective-permute-start(bf16[1536,128]{1,0:T(8,128)(2,1)} %get-tuple-element.64.refs_0_), channel_id=1, source_target_pairs={{0,1},{1,0},{2,3},{3,2},{4,5},{5,4},{6,7},{7,6},{8,9},{9,8},{10,11... | collective-permute-start | bytes 1179656 | tf_op jit(solution)/shard_map/cond/branch_0_fun/ppermute | solution.py:29
  255.5 8.0 %collective-permute-done.29.refs_4_ = bf16[1536,128]{1,0:T(8,128)(2,1)} collective-permute-done((bf16[1536,128]{1,0:T(8,128)(2,1)}, bf16[1536,128]{1,0:T(8,128)(2,1)}, u32[]{:S(2)}, u32[]{:S(2)}) %collective-permute-start.29) | collective-permute-done | bytes 393248 | tf_op jit(solution)/shard_map/cond/branch_0_fun/ppermute | solution.py:29
  264.0 15.7 %collective-permute-done.35.refs_4_ = bf16[1536,128]{1,0:T(8,128)(2,1)S(1)} collective-permute-done((bf16[1536,128]{1,0:T(8,128)(2,1)}, bf16[1536,128]{1,0:T(8,128)(2,1)S(1)}, u32[]{:S(2)}, u32[]{:S(2)}) %collective-permute-start.35) | collective-permute-done | bytes 393248 | tf_op jit(solution)/shard_map/cond/branch_0_fun/ppermute | solution.py:29
  283.1 4.6 %branch_0_fun.39.refs_8_ = bf16[1,4194304]{1,0:T(2,128)(2,1)} custom-call(s32[2]{0:T(128)} %pad_add_fusion.zs, bf16[1536,128]{1,0:T(8,128)(2,1)} %get-tuple-element.66.refs_0_, bf16[1536,128]{1,0:T(8,128)(2,1)} %get-tuple-element.67.refs_1_, bf16[1536,128]{1,0:T(8,128)(2,1)} %copy-done.12, bf16[1536,128]{1,0:T(8,128)(2,1)} %copy-done.21, ...), custom_call_target="tpu_custom_call" | custom-call | flops 9437184 | bytes 9437184 | tf_op jit(solution)/shard_map/cond/branch_0_fun/pallas_call | solution.py:148
  287.7 4.6 %branch_0_fun.40.refs_8_ = bf16[1,4194304]{1,0:T(2,128)(2,1)} custom-call(s32[2]{0:T(128)} %pad_add_fusion.zs, bf16[1536,128]{1,0:T(8,128)(2,1)} %get-tuple-element.64.refs_0_, bf16[1536,128]{1,0:T(8,128)(2,1)} %get-tuple-element.65.refs_1_, bf16[1536,128]{1,0:T(8,128)(2,1)} %collective-permute-done.27.refs_2_, ...), custom_call_target="tpu_custom_call", output_to_operand_aliasing={{}: (9, {})} | custom-call | flops 9437184 | bytes 9437184 | tf_op jit(solution)/shard_map/cond/branch_0_fun/pallas_call | solution.py:148
  292.3 3.8 %branch_0_fun.41 = bf16[1,4194304]{1,0:T(2,128)(2,1)} custom-call(s32[2]{0:T(128)} %pad_add_fusion.zs, bf16[1024,128]{1,0:T(8,128)(2,1)} %get-tuple-element.62.refs_0_, bf16[1024,128]{1,0:T(8,128)(2,1)} %get-tuple-element.63.refs_1_, bf16[1024,128]{1,0:T(8,128)(2,1)} %collective-permute-done.21.refs_2_, ...), custom_call_target="tpu_custom_call", output_to_operand_aliasing={{}: (9, {})} | custom-call | flops 6291456 | bytes 6291456 | tf_op jit(solution)/shard_map/cond/branch_0_fun/pallas_call | solution.py:148
  (70 shorter events, 17.8 us)
Async XLA Ops:
  4.8 23.2 %collective-permute-start.14 = (bf16[3072,128]{1,0:T(8,128)(2,1)}, bf16[3072,128]{1,0:T(8,128)(2,1)}, u32[]{:S(2)}, u32[]{:S(2)}) collective-permute-start(bf16[3072,128]{1,0:T(8,128)(2,1)} %branch_0_fun.30), channel_id=1, source_target_pairs={{0,1},{3,2},{4,5},{7,6},{8,9},{11,10},{12,13},{15,14},{16,17},{19,... | collective-permute-start | bytes 2359304 | tf_op jit(solution)/shard_map/cond/branch_0_fun/ppermute | solution.py:225
  13.4 31.4 %collective-permute-start.8 = (bf16[3072,128]{1,0:T(8,128)(2,1)}, bf16[3072,128]{1,0:T(8,128)(2,1)}, u32[]{:S(2)}, u32[]{:S(2)}) collective-permute-start(bf16[3072,128]{1,0:T(8,128)(2,1)} %branch_0_fun.26), channel_id=1, source_target_pairs={{0,1},{3,2},{4,5},{7,6},{8,9},{11,10},{12,13},{15,14},{16,17},{19,... | collective-permute-start | bytes 2359304 | tf_op jit(solution)/shard_map/cond/branch_0_fun/ppermute | solution.py:225
  19.0 62.2 %collective-permute-start.13 = (bf16[3072,128]{1,0:T(8,128)(2,1)}, bf16[3072,128]{1,0:T(8,128)(2,1)}, u32[]{:S(2)}, u32[]{:S(2)}) collective-permute-start(bf16[3072,128]{1,0:T(8,128)(2,1)} %get-tuple-element.44), channel_id=1, source_target_pairs={{0,1},{3,2},{4,5},{7,6},{8,9},{11,10},{12,13},{15,14},{16,17},{19,... | collective-permute-start | bytes 2359304 | tf_op jit(solution)/shard_map/cond/branch_0_fun/ppermute | solution.py:225
  23.9 49.0 %collective-permute-start.2 = (bf16[2048,128]{1,0:T(8,128)(2,1)}, bf16[2048,128]{1,0:T(8,128)(2,1)}, u32[]{:S(2)}, u32[]{:S(2)}) collective-permute-start(bf16[2048,128]{1,0:T(8,128)(2,1)} %branch_0_fun.22), channel_id=1, source_target_pairs={{0,1},{3,2},{4,5},{7,6},{8,9},{11,10},{12,13},{15,14},{16,17},{19,... | collective-permute-start | bytes 1572872 | tf_op jit(solution)/shard_map/cond/branch_0_fun/ppermute | solution.py:225
  31.2 55.1 %collective-permute-start.15 = (bf16[3072,128]{1,0:T(8,128)(2,1)}, bf16[3072,128]{1,0:T(8,128)(2,1)}, u32[]{:S(2)}, u32[]{:S(2)}) collective-permute-start(bf16[3072,128]{1,0:T(8,128)(2,1)} %branch_0_fun.31), channel_id=1, source_target_pairs={{1,2},{2,1},{5,6},{6,5},{9,10},{10,9},{13,14},{14,13},{17,18},{18,... | collective-permute-start | bytes 2359304 | tf_op jit(solution)/shard_map/cond/branch_0_fun/ppermute | solution.py:225
  36.1 85.9 %collective-permute-start.7 = (bf16[3072,128]{1,0:T(8,128)(2,1)}, bf16[3072,128]{1,0:T(8,128)(2,1)}, u32[]{:S(2)}, u32[]{:S(2)}) collective-permute-start(bf16[3072,128]{1,0:T(8,128)(2,1)} %get-tuple-element.40), channel_id=1, source_target_pairs={{0,1},{3,2},{4,5},{7,6},{8,9},{11,10},{12,13},{15,14},{16,17},{19,... | collective-permute-start | bytes 2359304 | tf_op jit(solution)/shard_map/cond/branch_0_fun/ppermute | solution.py:225
  48.0 75.5 %collective-permute-start.9 = (bf16[3072,128]{1,0:T(8,128)(2,1)}, bf16[3072,128]{1,0:T(8,128)(2,1)}, u32[]{:S(2)}, u32[]{:S(2)}) collective-permute-start(bf16[3072,128]{1,0:T(8,128)(2,1)} %branch_0_fun.27), channel_id=1, source_target_pairs={{1,2},{2,1},{5,6},{6,5},{9,10},{10,9},{13,14},{14,13},{17,18},{18,... | collective-permute-start | bytes 2359304 | tf_op jit(solution)/shard_map/cond/branch_0_fun/ppermute | solution.py:225
  72.9 56.1 %collective-permute-start.12 = (bf16[3072,128]{1,0:T(8,128)(2,1)}, bf16[3072,128]{1,0:T(8,128)(2,1)}, u32[]{:S(2)}, u32[]{:S(2)}) collective-permute-start(bf16[3072,128]{1,0:T(8,128)(2,1)} %get-tuple-element.43), channel_id=1, source_target_pairs={{0,1},{3,2},{4,5},{7,6},{8,9},{11,10},{12,13},{15,14},{16,17},{19,... | collective-permute-start | bytes 2359304 | tf_op jit(solution)/shard_map/cond/branch_0_fun/ppermute | solution.py:225
  81.2 35.5 %collective-permute-start.1 = (bf16[2048,128]{1,0:T(8,128)(2,1)}, bf16[2048,128]{1,0:T(8,128)(2,1)}, u32[]{:S(2)}, u32[]{:S(2)}) collective-permute-start(bf16[2048,128]{1,0:T(8,128)(2,1)} %get-tuple-element.33), channel_id=1, source_target_pairs={{0,1},{3,2},{4,5},{7,6},{8,9},{11,10},{12,13},{15,14},{16,17},{19,... | collective-permute-start | bytes 1572872 | tf_op jit(solution)/shard_map/cond/branch_0_fun/ppermute | solution.py:225
  86.3 44.2 %collective-permute-start.3 = (bf16[2048,128]{1,0:T(8,128)(2,1)}, bf16[2048,128]{1,0:T(8,128)(2,1)}, u32[]{:S(2)}, u32[]{:S(2)}) collective-permute-start(bf16[2048,128]{1,0:T(8,128)(2,1)} %branch_0_fun.23), channel_id=1, source_target_pairs={{1,2},{2,1},{5,6},{6,5},{9,10},{10,9},{13,14},{14,13},{17,18},{18,... | collective-permute-start | bytes 1572872 | tf_op jit(solution)/shard_map/cond/branch_0_fun/ppermute | solution.py:225
  116.7 20.6 %collective-permute-start.6 = (bf16[3072,128]{1,0:T(8,128)(2,1)}, bf16[3072,128]{1,0:T(8,128)(2,1)}, u32[]{:S(2)}, u32[]{:S(2)}) collective-permute-start(bf16[3072,128]{1,0:T(8,128)(2,1)} %get-tuple-element.39), channel_id=1, source_target_pairs={{0,1},{3,2},{4,5},{7,6},{8,9},{11,10},{12,13},{15,14},{16,17},{19,... | collective-permute-start | bytes 2359304 | tf_op jit(solution)/shard_map/cond/branch_0_fun/ppermute | solution.py:225
  122.0 22.4 %collective-permute-start.16 = (bf16[3072,128]{1,0:T(8,128)(2,1)}, bf16[3072,128]{1,0:T(8,128)(2,1)}, u32[]{:S(2)}, u32[]{:S(2)}) collective-permute-start(bf16[3072,128]{1,0:T(8,128)(2,1)} %get-tuple-element.45), channel_id=1, source_target_pairs={{1,2},{2,1},{5,6},{6,5},{9,10},{10,9},{13,14},{14,13},{17,18},{18,... | collective-permute-start | bytes 2359304 | tf_op jit(solution)/shard_map/cond/branch_0_fun/ppermute | solution.py:225
  123.6 22.6 %collective-permute-start.17 = (bf16[3072,128]{1,0:T(8,128)(2,1)}, bf16[3072,128]{1,0:T(8,128)(2,1)}, u32[]{:S(2)}, u32[]{:S(2)}) collective-permute-start(bf16[3072,128]{1,0:T(8,128)(2,1)} %get-tuple-element.46), channel_id=1, source_target_pairs={{1,0},{2,3},{5,4},{6,7},{9,8},{10,11},{13,12},{14,15},{17,16},{18,... | collective-permute-start | bytes 2359304 | tf_op jit(solution)/shard_map/cond/branch_0_fun/ppermute | solution.py:225
  129.0 27.9 %collective-permute-start.10 = (bf16[3072,128]{1,0:T(8,128)(2,1)}, bf16[3072,128]{1,0:T(8,128)(2,1)}, u32[]{:S(2)}, u32[]{:S(2)}) collective-permute-start(bf16[3072,128]{1,0:T(8,128)(2,1)} %get-tuple-element.41), channel_id=1, source_target_pairs={{1,2},{2,1},{5,6},{6,5},{9,10},{10,9},{13,14},{14,13},{17,18},{18,... | collective-permute-start | bytes 2359304 | tf_op jit(solution)/shard_map/cond/branch_0_fun/ppermute | solution.py:225
  130.5 32.5 %collective-permute-start.11 = (bf16[3072,128]{1,0:T(8,128)(2,1)}, bf16[3072,128]{1,0:T(8,128)(2,1)}, u32[]{:S(2)}, u32[]{:S(2)}) collective-permute-start(bf16[3072,128]{1,0:T(8,128)(2,1)} %get-tuple-element.42), channel_id=1, source_target_pairs={{1,0},{2,3},{5,4},{6,7},{9,8},{10,11},{13,12},{14,15},{17,16},{18,... | collective-permute-start | bytes 2359304 | tf_op jit(solution)/shard_map/cond/branch_0_fun/ppermute | solution.py:225
  137.3 33.8 %collective-permute-start = (bf16[2048,128]{1,0:T(8,128)(2,1)}, bf16[2048,128]{1,0:T(8,128)(2,1)}, u32[]{:S(2)}, u32[]{:S(2)}) collective-permute-start(bf16[2048,128]{1,0:T(8,128)(2,1)} %get-tuple-element.32), channel_id=1, source_target_pairs={{0,1},{3,2},{4,5},{7,6},{8,9},{11,10},{12,13},{15,14},{16,17},{19,... | collective-permute-start | bytes 1572872 | tf_op jit(solution)/shard_map/cond/branch_0_fun/ppermute | solution.py:225
  144.4 26.7 %collective-permute-start.4 = (bf16[2048,128]{1,0:T(8,128)(2,1)}, bf16[2048,128]{1,0:T(8,128)(2,1)}, u32[]{:S(2)}, u32[]{:S(2)}) collective-permute-start(bf16[2048,128]{1,0:T(8,128)(2,1)} %get-tuple-element.34), channel_id=1, source_target_pairs={{1,2},{2,1},{5,6},{6,5},{9,10},{10,9},{13,14},{14,13},{17,18},{18,... | collective-permute-start | bytes 1572872 | tf_op jit(solution)/shard_map/cond/branch_0_fun/ppermute | solution.py:225
  146.2 25.8 %collective-permute-start.5 = (bf16[2048,128]{1,0:T(8,128)(2,1)}, bf16[2048,128]{1,0:T(8,128)(2,1)}, u32[]{:S(2)}, u32[]{:S(2)}) collective-permute-start(bf16[2048,128]{1,0:T(8,128)(2,1)} %get-tuple-element.35), channel_id=1, source_target_pairs={{1,0},{2,3},{5,4},{6,7},{9,8},{10,11},{13,12},{14,15},{17,16},{18,... | collective-permute-start | bytes 1572872 | tf_op jit(solution)/shard_map/cond/branch_0_fun/ppermute | solution.py:225
  156.8 21.0 %collective-permute-start.20 = (bf16[3072,128]{1,0:T(8,128)(2,1)}, bf16[3072,128]{1,0:T(8,128)(2,1)}, u32[]{:S(2)}, u32[]{:S(2)}) collective-permute-start(bf16[3072,128]{1,0:T(8,128)(2,1)} %get-tuple-element.56), channel_id=1, source_target_pairs={{0,4},{4,0},{8,12},{12,8},{16,20},{20,16},{24,28},{28,24},{1,5},{5... | collective-permute-start | bytes 2359304 | tf_op jit(solution)/shard_map/cond/branch_0_fun/ppermute | solution.py:25
  171.0 10.1 %collective-permute-start.19 = (bf16[3072,128]{1,0:T(8,128)(2,1)}, bf16[3072,128]{1,0:T(8,128)(2,1)}, u32[]{:S(2)}, u32[]{:S(2)}) collective-permute-start(bf16[3072,128]{1,0:T(8,128)(2,1)} %get-tuple-element.54), channel_id=1, source_target_pairs={{0,4},{4,0},{8,12},{12,8},{16,20},{20,16},{24,28},{28,24},{1,5},{5... | collective-permute-start | bytes 2359304 | tf_op jit(solution)/shard_map/cond/branch_0_fun/ppermute | solution.py:25
  177.7 6.8 %collective-permute-start.18 = (bf16[2048,128]{1,0:T(8,128)(2,1)}, bf16[2048,128]{1,0:T(8,128)(2,1)}, u32[]{:S(2)}, u32[]{:S(2)}) collective-permute-start(bf16[2048,128]{1,0:T(8,128)(2,1)} %get-tuple-element.52), channel_id=1, source_target_pairs={{0,4},{4,0},{8,12},{12,8},{16,20},{20,16},{24,28},{28,24},{1,5},{5... | collective-permute-start | bytes 1572872 | tf_op jit(solution)/shard_map/cond/branch_0_fun/ppermute | solution.py:25
  187.5 11.5 %collective-permute-start.25 = (bf16[1024,128]{1,0:T(8,128)(2,1)}, bf16[1024,128]{1,0:T(8,128)(2,1)}, u32[]{:S(2)}, u32[]{:S(2)}) collective-permute-start(bf16[1024,128]{1,0:T(8,128)(2,1)} %get-tuple-element.62.refs_0_), channel_id=1, source_target_pairs={{0,3},{1,2},{2,1},{3,0},{4,7},{5,6},{6,5},{7,4},{8,11},{9,10},{10,... | collective-permute-start | bytes 786440 | tf_op jit(solution)/shard_map/cond/branch_0_fun/ppermute | solution.py:29
  190.0 48.1 %collective-permute-start.23 = (bf16[1024,128]{1,0:T(8,128)(2,1)}, bf16[1024,128]{1,0:T(8,128)(2,1)}, u32[]{:S(2)}, u32[]{:S(2)}) collective-permute-start(bf16[1024,128]{1,0:T(8,128)(2,1)} %get-tuple-element.62.refs_0_), channel_id=1, source_target_pairs={{0,2},{1,3},{2,0},{3,1},{4,6},{5,7},{6,4},{7,5},{8,10},{9,11},{10,... | collective-permute-start | bytes 786440 | tf_op jit(solution)/shard_map/cond/branch_0_fun/ppermute | solution.py:29
  190.0 48.1 %collective-permute-start.21 = (bf16[1024,128]{1,0:T(8,128)(2,1)}, bf16[1024,128]{1,0:T(8,128)(2,1)}, u32[]{:S(2)}, u32[]{:S(2)}) collective-permute-start(bf16[1024,128]{1,0:T(8,128)(2,1)} %get-tuple-element.62.refs_0_), channel_id=1, source_target_pairs={{0,1},{1,0},{2,3},{3,2},{4,5},{5,4},{6,7},{7,6},{8,9},{9,8},{10,11... | collective-permute-start | bytes 786440 | tf_op jit(solution)/shard_map/cond/branch_0_fun/ppermute | solution.py:29
  191.9 49.3 %collective-permute-start.31 = (bf16[1536,128]{1,0:T(8,128)(2,1)}, bf16[1536,128]{1,0:T(8,128)(2,1)S(1)}, u32[]{:S(2)}, u32[]{:S(2)}) collective-permute-start(bf16[1536,128]{1,0:T(8,128)(2,1)} %get-tuple-element.64.refs_0_), channel_id=1, source_target_pairs={{0,3},{1,2},{2,1},{3,0},{4,7},{5,6},{6,5},{7,4},{8,11},{9,10},{10,... | collective-permute-start | bytes 1179656 | tf_op jit(solution)/shard_map/cond/branch_0_fun/ppermute | solution.py:29
  194.4 69.1 %collective-permute-start.29 = (bf16[1536,128]{1,0:T(8,128)(2,1)}, bf16[1536,128]{1,0:T(8,128)(2,1)}, u32[]{:S(2)}, u32[]{:S(2)}) collective-permute-start(bf16[1536,128]{1,0:T(8,128)(2,1)} %get-tuple-element.64.refs_0_), channel_id=1, source_target_pairs={{0,2},{1,3},{2,0},{3,1},{4,6},{5,7},{6,4},{7,5},{8,10},{9,11},{10,... | collective-permute-start | bytes 1179656 | tf_op jit(solution)/shard_map/cond/branch_0_fun/ppermute | solution.py:29
  199.0 64.5 %collective-permute-start.37 = (bf16[1536,128]{1,0:T(8,128)(2,1)}, bf16[1536,128]{1,0:T(8,128)(2,1)S(1)}, u32[]{:S(2)}, u32[]{:S(2)}) collective-permute-start(bf16[1536,128]{1,0:T(8,128)(2,1)} %get-tuple-element.66.refs_0_), channel_id=1, source_target_pairs={{0,3},{1,2},{2,1},{3,0},{4,7},{5,6},{6,5},{7,4},{8,11},{9,10},{10,... | collective-permute-start | bytes 1179656 | tf_op jit(solution)/shard_map/cond/branch_0_fun/ppermute | solution.py:29
  238.2 41.6 %collective-permute-start.35 = (bf16[1536,128]{1,0:T(8,128)(2,1)}, bf16[1536,128]{1,0:T(8,128)(2,1)S(1)}, u32[]{:S(2)}, u32[]{:S(2)}) collective-permute-start(bf16[1536,128]{1,0:T(8,128)(2,1)} %get-tuple-element.66.refs_0_), channel_id=1, source_target_pairs={{0,2},{1,3},{2,0},{3,1},{4,6},{5,7},{6,4},{7,5},{8,10},{9,11},{10,... | collective-permute-start | bytes 1179656 | tf_op jit(solution)/shard_map/cond/branch_0_fun/ppermute | solution.py:29
  238.2 41.6 %collective-permute-start.33 = (bf16[1536,128]{1,0:T(8,128)(2,1)}, bf16[1536,128]{1,0:T(8,128)(2,1)S(1)}, u32[]{:S(2)}, u32[]{:S(2)}) collective-permute-start(bf16[1536,128]{1,0:T(8,128)(2,1)} %get-tuple-element.66.refs_0_), channel_id=1, source_target_pairs={{0,1},{1,0},{2,3},{3,2},{4,5},{5,4},{6,7},{7,6},{8,9},{9,8},{10,11... | collective-permute-start | bytes 1179656 | tf_op jit(solution)/shard_map/cond/branch_0_fun/ppermute | solution.py:29
  241.2 22.3 %copy-start = (bf16[1536,128]{1,0:T(8,128)(2,1)}, bf16[1536,128]{1,0:T(8,128)(2,1)S(1)}, u32[]{:S(2)}) copy-start(bf16[1536,128]{1,0:T(8,128)(2,1)S(1)} %collective-permute-done.31.refs_6_) | copy-start | bytes 1179652 | tf_op jit(solution)/shard_map/cond
  241.2 39.1 %collective-permute-start.27 = (bf16[1536,128]{1,0:T(8,128)(2,1)}, bf16[1536,128]{1,0:T(8,128)(2,1)}, u32[]{:S(2)}, u32[]{:S(2)}) collective-permute-start(bf16[1536,128]{1,0:T(8,128)(2,1)} %get-tuple-element.64.refs_0_), channel_id=1, source_target_pairs={{0,1},{1,0},{2,3},{3,2},{4,5},{5,4},{6,7},{7,6},{8,9},{9,8},{10,11... | collective-permute-start | bytes 1179656 | tf_op jit(solution)/shard_map/cond/branch_0_fun/ppermute | solution.py:29
  263.5 16.9 %collective-permute-start.32 = (bf16[1536,128]{1,0:T(8,128)(2,1)S(1)}, bf16[1536,128]{1,0:T(8,128)(2,1)S(1)}, u32[]{:S(2)}, u32[]{:S(2)}) collective-permute-start(bf16[1536,128]{1,0:T(8,128)(2,1)S(1)} %collective-permute-done.31.refs_6_), channel_id=1, source_target_pairs={{0,4},{4,0},{8,12},{12,8},{16,20},{20,16},{24,28},{28,24},{1,5},{5... | collective-permute-start | bytes 1179656 | tf_op jit(solution)/shard_map/cond/branch_0_fun/ppermute | solution.py:25
  263.5 18.1 %copy-start.6 = (bf16[1536,128]{1,0:T(8,128)(2,1)}, bf16[1536,128]{1,0:T(8,128)(2,1)S(1)}, u32[]{:S(2)}) copy-start(bf16[1536,128]{1,0:T(8,128)(2,1)S(1)} %collective-permute-done.37.refs_6_) | copy-start | bytes 1179652 | tf_op jit(solution)/shard_map/cond
  263.5 18.0 %collective-permute-start.38 = (bf16[1536,128]{1,0:T(8,128)(2,1)S(1)}, bf16[1536,128]{1,0:T(8,128)(2,1)S(1)}, u32[]{:S(2)}, u32[]{:S(2)}) collective-permute-start(bf16[1536,128]{1,0:T(8,128)(2,1)S(1)} %collective-permute-done.37.refs_6_), channel_id=1, source_target_pairs={{0,4},{4,0},{8,12},{12,8},{16,20},{20,16},{24,28},{28,24},{1,5},{5... | collective-permute-start | bytes 1179656 | tf_op jit(solution)/shard_map/cond/branch_0_fun/ppermute | solution.py:25
  279.8 1.8 copy-start.9
  279.8 2.0 collective-permute-start.36
  279.8 2.0 copy-start.12
  279.8 2.4 collective-permute-start.34
  280.3 7.4 %collective-permute-start.30 = (bf16[1536,128]{1,0:T(8,128)(2,1)}, bf16[1536,128]{1,0:T(8,128)(2,1)}, u32[]{:S(2)}, u32[]{:S(2)}) collective-permute-start(bf16[1536,128]{1,0:T(8,128)(2,1)} %collective-permute-done.29.refs_4_), channel_id=1, source_target_pairs={{0,4},{4,0},{8,12},{12,8},{16,20},{20,16},{24,28},{28,24},{1,5},{5... | collective-permute-start | bytes 1179656 | tf_op jit(solution)/shard_map/cond/branch_0_fun/ppermute | solution.py:25
  280.4 0.8 copy-start.3
  281.1 6.5 %collective-permute-start.28 = (bf16[1536,128]{1,0:T(8,128)(2,1)}, bf16[1536,128]{1,0:T(8,128)(2,1)}, u32[]{:S(2)}, u32[]{:S(2)}) collective-permute-start(bf16[1536,128]{1,0:T(8,128)(2,1)} %collective-permute-done.27.refs_2_), channel_id=1, source_target_pairs={{0,4},{4,0},{8,12},{12,8},{16,20},{20,16},{24,28},{28,24},{1,5},{5... | collective-permute-start | bytes 1179656 | tf_op jit(solution)/shard_map/cond/branch_0_fun/ppermute | solution.py:25
  281.6 0.7 copy-start.15
  281.6 10.7 %collective-permute-start.26 = (bf16[1024,128]{1,0:T(8,128)(2,1)}, bf16[1024,128]{1,0:T(8,128)(2,1)}, u32[]{:S(2)}, u32[]{:S(2)}) collective-permute-start(bf16[1024,128]{1,0:T(8,128)(2,1)} %collective-permute-done.25.refs_6_), channel_id=1, source_target_pairs={{0,4},{4,0},{8,12},{12,8},{16,20},{20,16},{24,28},{28,24},{1,5},{5... | collective-permute-start | bytes 786440 | tf_op jit(solution)/shard_map/cond/branch_0_fun/ppermute | solution.py:25
  281.7 0.8 copy-start.18
  281.7 10.5 %collective-permute-start.24 = (bf16[1024,128]{1,0:T(8,128)(2,1)}, bf16[1024,128]{1,0:T(8,128)(2,1)}, u32[]{:S(2)}, u32[]{:S(2)}) collective-permute-start(bf16[1024,128]{1,0:T(8,128)(2,1)} %collective-permute-done.23.refs_4_), channel_id=1, source_target_pairs={{0,4},{4,0},{8,12},{12,8},{16,20},{20,16},{24,28},{28,24},{1,5},{5... | collective-permute-start | bytes 786440 | tf_op jit(solution)/shard_map/cond/branch_0_fun/ppermute | solution.py:25
  282.3 0.8 copy-start.21
  282.3 10.0 %collective-permute-start.22 = (bf16[1024,128]{1,0:T(8,128)(2,1)}, bf16[1024,128]{1,0:T(8,128)(2,1)}, u32[]{:S(2)}, u32[]{:S(2)}) collective-permute-start(bf16[1024,128]{1,0:T(8,128)(2,1)} %collective-permute-done.21.refs_2_), channel_id=1, source_target_pairs={{0,4},{4,0},{8,12},{12,8},{16,20},{20,16},{24,28},{28,24},{1,5},{5... | collective-permute-start | bytes 786440 | tf_op jit(solution)/shard_map/cond/branch_0_fun/ppermute | solution.py:25

commit v4 on v3

--- a/solution.py
+++ b/solution.py
@@ -10,8 +10,9 @@
 
 LANES = 128
 VMEM = 67043328
-CUTS = (3, 3, 2)
-UNITS = 8
+CUTS = (5, 7, 4)
+UNITS = 16
+CHAIN = "ccd"
 OUTER = ((0, 1), (3, 2))
 MIDDLE = ((1, 2), (2, 1))
 INNER = ((1, 0), (2, 3))
@@ -25,6 +26,14 @@
     return lax.ppermute(value, "rep", pairs)
 
 
+def swapped_among(value, level, places):
+    n = lax.axis_size("zero")
+    pairs = [
+        (r * n + i, (r ^ 2**level) * n + i) for r in range(lax.axis_size("rep")) for i in places
+    ]
+    return lax.ppermute(value, ("rep", "zero"), pairs)
+
+
 def crossed(value, mask):
     return lax.ppermute(value, "zero", [(i, i ^ mask) for i in range(lax.axis_size("zero"))])
 
@@ -53,7 +62,7 @@
 def pack_body(sc, reads, writes):
     (g,), (o,) = reads, writes
 
-    @pieces(o.shape[0], 256)
+    @pieces(o.shape[0], 64)
     def _(row, flat, step):
         o[row, :] = g[0, :, flat].reshape(step, LANES)
 
@@ -61,7 +70,7 @@
 def sum_body(sc, reads, writes):
     (r, g), (o,) = reads, writes
 
-    @pieces(o.shape[0], 128)
+    @pieces(o.shape[0], 64)
     def _(row, flat, step):
         own = g[0, :, flat].astype(f32).reshape(step, LANES)
         o[row, :] = (r[row, :].astype(f32) + own).astype(bf16)
@@ -102,14 +111,14 @@
 def spread_body(sc, reads, writes):
     (src,), (o,) = reads, writes
 
-    @pieces(src.shape[0], 256)
+    @pieces(src.shape[0], 64)
     def _(row, flat, step):
         o[:, flat] = src[row, :].reshape(1, step * LANES)
 
 
 def staged(body, scalars, ins, outs, plan, alias=(), scale=None, cost=0):
     count = len(ins)
-    buffers = [(shape, kind) for reads, writes in plan for _, _, shape, kind in reads + writes]
+    buffers = [(shape, kind) for reads, writes in plan for _, _, shape, kind, *_ in reads + writes]
 
     def kernel(zs, *refs):
         if scale is not None:
@@ -121,22 +130,29 @@
         at, work = 0, []
         for reads, writes in plan:
             loads, stores = [], []
-            for i, where, _, _ in reads:
-                copy = pltpu.make_async_copy(sources[i].at[where(zs)], scratch[at], sems.at[at])
-                loads.append((copy, scratch[at]))
+            for i, where, _, _, *choice in reads:
+                def load(i, at=at, where=where):
+                    return pltpu.make_async_copy(sources[i].at[where(zs)], scratch[at], sems.at[at])
+
+                loads.append((load, choice[0] if choice else (i, i), scratch[at]))
                 at += 1
             for i, where, _, _ in writes:
                 copy = pltpu.make_async_copy(scratch[at], sinks[i].at[where(zs)], sems.at[at])
                 stores.append((copy, scratch[at]))
                 at += 1
             work.append((loads, stores))
+        middle = (zs[0] == 1) | (zs[0] == 2)
         for loads, _ in work:
-            for copy, _ in loads:
-                copy.start()
+            for load, (i, j), _ in loads:
+                if i == j:
+                    load(i).start()
+                    continue
+                pl.when(middle)(lambda load=load, i=i: load(i).start())
+                pl.when(~middle)(lambda load=load, j=j: load(j).start())
         for loads, stores in work:
-            for copy, _ in loads:
-                copy.wait()
-            body(sc, [ref for _, ref in loads], [ref for _, ref in stores])
+            for load, (i, _), _ in loads:
+                load(i).wait()
+            body(sc, [ref for _, _, ref in loads], [ref for _, ref in stores])
             for copy, _ in stores:
                 copy.start()
         for _, stores in work:
@@ -179,6 +195,8 @@
 
     def cuts(n, most):
         parts = max(1, n // most)
+        while n % (64 * parts):
+            parts += 1
         return [(i * (n // parts), n // parts) for i in range(parts)]
 
     def rows_at(i, at, n, kind=bf16):
@@ -242,7 +260,7 @@
                 [flat_at(0, start + at, r), flat_at(1, start + at, r)]
                 + [rows_at(2, at, r, f32), rows_at(3, at, r)],
             )
-            for at, r in cuts(n, 512)
+            for at, r in cuts(n, 1024)
         ]
         kept["m"], kept["v"], fresh, fresh16 = staged(
             adam_body, scalars, ins,
@@ -260,7 +278,7 @@
         alias = keep(("w",), ins)
         plan = []
         for p in (0, 1):
-            for at, r in cuts(n // 2, 512):
+            for at, r in cuts(n // 2, 768):
                 row = lambda zs, p=p, at=at: pl.multiple_of(side(zs, p) * (n // 2) + at, 8)
                 here = lambda zs, row=row, r=r: pl.ds(row(zs), r)
                 flat = lambda zs, row=row, r=r: (
@@ -280,12 +298,30 @@
         return mine, yours
 
     def spread(part, mine, yours):
-        _, start, n = part
+        k, start, n = part
         nh = n // 2
-        ins = [mine, yours]
-        for mask in (1, 2, 3):
-            got = crossed(mine, mask)
-            ins += [got, swapped(got, level)]
+        ins, slots = [mine, yours], [(0, 1)]
+
+        def swap_halves(got, among):
+            return swapped_among(got, level, among)
+
+        got = crossed(mine, 1)
+        ins += [got, swap_halves(got, range(4))]
+        slots.append((2, 3))
+        if CHAIN[k] == "d":
+            for mask in (2, 3):
+                got = crossed(mine, mask)
+                slots.append((len(ins), len(ins) + 1))
+                ins += [got, swap_halves(got, range(4))]
+        else:
+            m1 = send(mine, MIDDLE)
+            m2 = send(got, MIDDLE)
+            a2 = send(m1, INNER)
+            a3 = send(m2, INNER)
+            for mid, end in ((m2, a2), (m1, a3)):
+                slots.append(tuple((len(ins) + i, len(ins) + 2 + i) for i in (0, 1)))
+                ins += [mid, swap_halves(mid, (1, 2))]
+                ins += [end, swap_halves(end, (0, 3))]
         plan = []
         for q in range(8):
 
@@ -294,7 +330,10 @@
                 first = shard * rows + start + side(zs, q % 2) * nh
                 return (slice(None), pl.ds(pl.multiple_of(first * LANES, 8 * LANES), nh * LANES))
 
-            plan.append(([rows_at(q, 0, nh)], [(0, where, (1, nh * LANES), bf16)]))
+            source = slots[q // 2][q % 2]
+            read = rows_at(source[0] if isinstance(source, tuple) else source, 0, nh)
+            plan.append(([read + ((source,) if isinstance(source, tuple) else ())],
+                         [(0, where, (1, nh * LANES), bf16)]))
         alias = keep(("p",), ins)
         (kept["p"],) = staged(
             spread_body, scalars, ins,

time: 298 us -> 269 us (0.903)
  waiting for transfers between devices: 126 us -> 87.9 us
  starting transfers between devices: 81.6 us -> 89.8 us
    ppermute x9 -> x5, waiting for transfers between devices: 65 us -> 15.4 us  [crossed(): lax.ppermute(value, 'zero', [(i, i ^ mask) for i in range(lax.axis_size('...]
    ppermute x9 -> x5, starting transfers between devices: 26.7 us -> 8.51 us  [crossed(): lax.ppermute(value, 'zero', [(i, i ^ mask) for i in range(lax.axis_size('...]
    ppermute x0 -> x13, starting transfers between devices: none -> 14.9 us  [swapped_among(): return lax.ppermute(value, ('rep', 'zero'), pairs)]
    ppermute x18 -> x26, starting transfers between devices: 52.5 us -> 65.7 us  [send(): return lax.ppermute(value, 'zero', list(pairs))]
    ppermute x18 -> x26, waiting for transfers between devices: 60.9 us -> 72.5 us  [send(): return lax.ppermute(value, 'zero', list(pairs))]
  transfers between devices with their start and end apart: 39 -> 47, of which waited for: 12 -> 12; matrix products, arithmetic and copies ran while one was open for 0% -> 0% of each run, Pallas kernels for 25% -> 29%
where the time goes in v4:
time: 269 us; the launch traced here: 267 us
  starting transfers between devices  89.8 us (33%)
  waiting for transfers between devices  87.9 us (33%)
  Pallas kernels  85.6 us (32%)
    pallas_call x21, Pallas kernels, staged(): pl.pallas_call(kernel, out_shape=outs, grid_spec=pltpu.PrefetchScalarGrid...  85.6 us
    ppermute x26, waiting for transfers between devices, send(): return lax.ppermute(value, 'zero', list(pairs))  72.5 us
    ppermute x26, starting transfers between devices, send(): return lax.ppermute(value, 'zero', list(pairs))  65.7 us
    ppermute x5, waiting for transfers between devices, crossed(): lax.ppermute(value, 'zero', [(i, i ^ mask) for i in range(lax.axis_size('...  15.4 us
    ppermute x13, starting transfers between devices, swapped_among(): return lax.ppermute(value, ('rep', 'zero'), pairs)  14.9 us
    ppermute x5, starting transfers between devices, crossed(): lax.ppermute(value, 'zero', [(i, i ^ mask) for i in range(lax.axis_size('...  8.51 us
  transfers between devices with their start and end apart: 47, of which 12 were waited for; matrix products, arithmetic and copies ran while one was open for 0% of the time, Pallas kernels for 29%

profile of v4, /device:TPU:0, one launch (start us, length us, event | category | flops | bytes accessed | tf_op | source)
XLA Modules:
  0.0 267.4 jit_solution(972135297455032791)
XLA Ops:
  1.3 266.0 %conditional.1 = (f32[1,1048576]{1,0:T(1,128)}, f32[1,1048576]{1,0:T(1,128)}, f32[1,1048576]{1,0:T(1,128)}, bf16[1,4194304]{1,0:T(2,128)(2,1)}) conditional(s32[]{:T(128)} %clamp.3, (s32[1]{0:T(128)}, bf16[1,1,4194304]{2,1,0:T(2,128)(2,1)}, f32[1,1048576]{1,0:T(1,128)}, f32[1,1048576]{1,0:T(1,128)}, ...), branch_computations={%region_0.1_spmd, %region_1.2_spmd, %region_2.3_spmd} | conditional | flops 125829160 | bytes 222300224 | solution.py:373
  1.9 2.9 %branch_0_fun.26 = bf16[3584,128]{1,0:T(8,128)(2,1)} custom-call(s32[2]{0:T(128)} %pad_add_fusion.zs, bf16[1,1,4194304]{2,1,0:T(2,128)(2,1)} %get-tuple-element.161.refs_0_.refs_1_), custom_call_target="tpu_custom_call" | custom-call | flops 2752512 | bytes 2752512 | tf_op jit(solution)/shard_map/cond/branch_0_fun/pallas_call | solution.py:164
  4.9 5.9 %collective-permute-start.8 = (bf16[3584,128]{1,0:T(8,128)(2,1)}, bf16[3584,128]{1,0:T(8,128)(2,1)}, u32[]{:S(2)}, u32[]{:S(2)}) collective-permute-start(bf16[3584,128]{1,0:T(8,128)(2,1)} %branch_0_fun.26), channel_id=1, source_target_pairs={{0,1},{3,2},{4,5},{7,6},{8,9},{11,10},{12,13},{15,14},{16,17},{19,... | collective-permute-start | bytes 2752520 | tf_op jit(solution)/shard_map/cond/branch_0_fun/ppermute | solution.py:243
  10.8 2.9 %branch_0_fun.30 = bf16[2560,128]{1,0:T(8,128)(2,1)} custom-call(s32[2]{0:T(128)} %pad_add_fusion.zs, bf16[1,1,4194304]{2,1,0:T(2,128)(2,1)} %get-tuple-element.161.refs_0_.refs_1_), custom_call_target="tpu_custom_call" | custom-call | flops 1966080 | bytes 1966080 | tf_op jit(solution)/shard_map/cond/branch_0_fun/pallas_call | solution.py:164
  13.7 2.1 collective-permute-start.14
  15.8 3.3 %branch_0_fun.29 = (bf16[2560,128]{1,0:T(8,128)(2,1)}, bf16[2560,128]{1,0:T(8,128)(2,1)}) custom-call(s32[2]{0:T(128)} %pad_add_fusion.zs, bf16[1,1,4194304]{2,1,0:T(2,128)(2,1)} %get-tuple-element.161.refs_0_.refs_1_), custom_call_target="tpu_custom_call" | custom-call | flops 3932160 | bytes 3932160 | tf_op jit(solution)/shard_map/cond/branch_0_fun/pallas_call | solution.py:164
  19.1 2.1 collective-permute-start.13
  21.2 3.6 %branch_0_fun.25 = (bf16[3584,128]{1,0:T(8,128)(2,1)}, bf16[3584,128]{1,0:T(8,128)(2,1)}) custom-call(s32[2]{0:T(128)} %pad_add_fusion.zs, bf16[1,1,4194304]{2,1,0:T(2,128)(2,1)} %get-tuple-element.161.refs_0_.refs_1_), custom_call_target="tpu_custom_call" | custom-call | flops 5505024 | bytes 5505024 | tf_op jit(solution)/shard_map/cond/branch_0_fun/pallas_call | solution.py:164
  24.8 2.2 collective-permute-start.7
  27.1 3.8 %collective-permute-done.8.refs_1_ = bf16[3584,128]{1,0:T(8,128)(2,1)} collective-permute-done((bf16[3584,128]{1,0:T(8,128)(2,1)}, bf16[3584,128]{1,0:T(8,128)(2,1)}, u32[]{:S(2)}, u32[]{:S(2)}) %collective-permute-start.8) | collective-permute-done | bytes 917536 | tf_op jit(solution)/shard_map/cond/branch_0_fun/ppermute | solution.py:243
  30.9 3.4 %branch_0_fun.27 = bf16[3584,128]{1,0:T(8,128)(2,1)} custom-call(s32[2]{0:T(128)} %pad_add_fusion.zs, bf16[1,1,4194304]{2,1,0:T(2,128)(2,1)} %get-tuple-element.161.refs_0_.refs_1_, bf16[3584,128]{1,0:T(8,128)(2,1)} %collective-permute-done.8.refs_1_), custom_call_target="tpu_custom_call" | custom-call | flops 3670016 | bytes 3670016 | tf_op jit(solution)/shard_map/cond/branch_0_fun/pallas_call | solution.py:164
  35.9 9.0 %collective-permute-done.14.refs_1_ = bf16[2560,128]{1,0:T(8,128)(2,1)} collective-permute-done((bf16[2560,128]{1,0:T(8,128)(2,1)}, bf16[2560,128]{1,0:T(8,128)(2,1)}, u32[]{:S(2)}, u32[]{:S(2)}) %collective-permute-start.14) | collective-permute-done | bytes 655392 | tf_op jit(solution)/shard_map/cond/branch_0_fun/ppermute | solution.py:243
  44.9 3.2 %branch_0_fun.31 = bf16[2560,128]{1,0:T(8,128)(2,1)} custom-call(s32[2]{0:T(128)} %pad_add_fusion.zs, bf16[1,1,4194304]{2,1,0:T(2,128)(2,1)} %get-tuple-element.161.refs_0_.refs_1_, bf16[2560,128]{1,0:T(8,128)(2,1)} %collective-permute-done.14.refs_1_), custom_call_target="tpu_custom_call" | custom-call | flops 2621440 | bytes 2621440 | tf_op jit(solution)/shard_map/cond/branch_0_fun/pallas_call | solution.py:164
  49.7 7.2 %collective-permute-start.12 = (bf16[2560,128]{1,0:T(8,128)(2,1)}, bf16[2560,128]{1,0:T(8,128)(2,1)}, u32[]{:S(2)}, u32[]{:S(2)}) collective-permute-start(bf16[2560,128]{1,0:T(8,128)(2,1)} %get-tuple-element.43), channel_id=1, source_target_pairs={{0,1},{3,2},{4,5},{7,6},{8,9},{11,10},{12,13},{15,14},{16,17},{19,... | collective-permute-start | bytes 1966088 | tf_op jit(solution)/shard_map/cond/branch_0_fun/ppermute | solution.py:243
  56.9 2.7 %branch_0_fun.22 = bf16[2048,128]{1,0:T(8,128)(2,1)} custom-call(s32[2]{0:T(128)} %pad_add_fusion.zs, bf16[1,1,4194304]{2,1,0:T(2,128)(2,1)} %get-tuple-element.161.refs_0_.refs_1_), custom_call_target="tpu_custom_call" | custom-call | flops 1572864 | bytes 1572864 | tf_op jit(solution)/shard_map/cond/branch_0_fun/pallas_call | solution.py:164
  59.6 4.5 %collective-permute-start.2 = (bf16[2048,128]{1,0:T(8,128)(2,1)}, bf16[2048,128]{1,0:T(8,128)(2,1)}, u32[]{:S(2)}, u32[]{:S(2)}) collective-permute-start(bf16[2048,128]{1,0:T(8,128)(2,1)} %branch_0_fun.22), channel_id=1, source_target_pairs={{0,1},{3,2},{4,5},{7,6},{8,9},{11,10},{12,13},{15,14},{16,17},{19,... | collective-permute-start | bytes 1572872 | tf_op jit(solution)/shard_map/cond/branch_0_fun/ppermute | solution.py:243
  64.2 3.9 %branch_0_fun.32 = (bf16[2560,128]{1,0:T(8,128)(2,1)}, bf16[2560,128]{1,0:T(8,128)(2,1)}) custom-call(s32[2]{0:T(128)} %pad_add_fusion.zs, bf16[1,1,4194304]{2,1,0:T(2,128)(2,1)} %get-tuple-element.161.refs_0_.refs_1_, bf16[2560,128]{1,0:T(8,128)(2,1)} %collective-permute-done.13.refs_1_, bf16[2560,128]{1,0:T(8,128)(2,1)} %collective-permute-done.15.refs_2_), custom_call_target="tpu_custom_call" | custom-call | flops 5242880 | bytes 5242880 | tf_op jit(solution)/shard_map/cond/branch_0_fun/pallas_call | solution.py:164
  69.6 9.1 %collective-permute-done.7.refs_1_ = bf16[3584,128]{1,0:T(8,128)(2,1)} collective-permute-done((bf16[3584,128]{1,0:T(8,128)(2,1)}, bf16[3584,128]{1,0:T(8,128)(2,1)}, u32[]{:S(2)}, u32[]{:S(2)}) %collective-permute-start.7) | collective-permute-done | bytes 917536 | tf_op jit(solution)/shard_map/cond/branch_0_fun/ppermute | solution.py:243
  79.9 6.4 %collective-permute-start.6 = (bf16[3584,128]{1,0:T(8,128)(2,1)}, bf16[3584,128]{1,0:T(8,128)(2,1)}, u32[]{:S(2)}, u32[]{:S(2)}) collective-permute-start(bf16[3584,128]{1,0:T(8,128)(2,1)} %get-tuple-element.39), channel_id=1, source_target_pairs={{0,1},{3,2},{4,5},{7,6},{8,9},{11,10},{12,13},{15,14},{16,17},{19,... | collective-permute-start | bytes 2752520 | tf_op jit(solution)/shard_map/cond/branch_0_fun/ppermute | solution.py:243
  86.3 4.6 %branch_0_fun.28 = (bf16[3584,128]{1,0:T(8,128)(2,1)}, bf16[3584,128]{1,0:T(8,128)(2,1)}) custom-call(s32[2]{0:T(128)} %pad_add_fusion.zs, bf16[1,1,4194304]{2,1,0:T(2,128)(2,1)} %get-tuple-element.161.refs_0_.refs_1_, bf16[3584,128]{1,0:T(8,128)(2,1)} %collective-permute-done.7.refs_1_, bf16[3584,128]{1,0:T(8,128)(2,1)} %collective-permute-done.9.refs_2_), custom_call_target="tpu_custom_call" | custom-call | flops 7340032 | bytes 7340032 | tf_op jit(solution)/shard_map/cond/branch_0_fun/pallas_call | solution.py:164
  90.9 13.0 %collective-permute-done.2.refs_1_ = bf16[2048,128]{1,0:T(8,128)(2,1)} collective-permute-done((bf16[2048,128]{1,0:T(8,128)(2,1)}, bf16[2048,128]{1,0:T(8,128)(2,1)}, u32[]{:S(2)}, u32[]{:S(2)}) %collective-permute-start.2) | collective-permute-done | bytes 524320 | tf_op jit(solution)/shard_map/cond/branch_0_fun/ppermute | solution.py:243
  106.8 3.0 %branch_0_fun.21 = (bf16[2048,128]{1,0:T(8,128)(2,1)}, bf16[2048,128]{1,0:T(8,128)(2,1)}) custom-call(s32[2]{0:T(128)} %pad_add_fusion.zs, bf16[1,1,4194304]{2,1,0:T(2,128)(2,1)} %get-tuple-element.161.refs_0_.refs_1_), custom_call_target="tpu_custom_call" | custom-call | flops 3145728 | bytes 3145728 | tf_op jit(solution)/shard_map/cond/branch_0_fun/pallas_call | solution.py:164
  109.8 3.0 %branch_0_fun.23 = bf16[2048,128]{1,0:T(8,128)(2,1)} custom-call(s32[2]{0:T(128)} %pad_add_fusion.zs, bf16[1,1,4194304]{2,1,0:T(2,128)(2,1)} %get-tuple-element.161.refs_0_.refs_1_, bf16[2048,128]{1,0:T(8,128)(2,1)} %collective-permute-done.2.refs_1_), custom_call_target="tpu_custom_call" | custom-call | flops 2097152 | bytes 2097152 | tf_op jit(solution)/shard_map/cond/branch_0_fun/pallas_call | solution.py:164
  112.9 8.1 %collective-permute-start.1 = (bf16[2048,128]{1,0:T(8,128)(2,1)}, bf16[2048,128]{1,0:T(8,128)(2,1)}, u32[]{:S(2)}, u32[]{:S(2)}) collective-permute-start(bf16[2048,128]{1,0:T(8,128)(2,1)} %get-tuple-element.33), channel_id=1, source_target_pairs={{0,1},{3,2},{4,5},{7,6},{8,9},{11,10},{12,13},{15,14},{16,17},{19,... | collective-permute-start | bytes 1572872 | tf_op jit(solution)/shard_map/cond/branch_0_fun/ppermute | solution.py:243
  123.9 6.9 %branch_0_fun.33 = (f32[1,1048576]{1,0:T(1,128)}, f32[1,1048576]{1,0:T(1,128)}, f32[2560,128]{1,0:T(8,128)}, bf16[2560,128]{1,0:T(8,128)(2,1)}) custom-call(s32[2]{0:T(128)} %pad_add_fusion.zs, f32[2]{0:T(128)} %pad_maximum_fusion.refs_0_, bf16[1,1,4194304]{2,1,0:T(2,128)(2,1)} %get-tuple-element.161.refs_0_.refs_1_, ...), custom_call_target="tpu_custom_call" | custom-call | flops 13107200 | bytes 13107200 | tf_op jit(solution)/shard_map/cond/branch_0_fun/pallas_call | solution.py:164
  130.9 9.0 %branch_0_fun.34 = (f32[1,1048576]{1,0:T(1,128)}, f32[1,1048576]{1,0:T(1,128)}, f32[3584,128]{1,0:T(8,128)}, bf16[3584,128]{1,0:T(8,128)(2,1)}) custom-call(s32[2]{0:T(128)} %pad_add_fusion.zs, f32[2]{0:T(128)} %pad_maximum_fusion.refs_0_, bf16[1,1,4194304]{2,1,0:T(2,128)(2,1)} %get-tuple-element.161.refs_0_.refs_1_, ...), custom_call_target="tpu_custom_call", output_to_operand_aliasing={{0}: (9, {}), {1}: (10, {})} | custom-call | flops 18350080 | bytes 18350080 | tf_op jit(solution)/shard_map/cond/branch_0_fun/pallas_call | solution.py:164
  140.4 3.2 %collective-permute-start = (bf16[2048,128]{1,0:T(8,128)(2,1)}, bf16[2048,128]{1,0:T(8,128)(2,1)}, u32[]{:S(2)}, u32[]{:S(2)}) collective-permute-start(bf16[2048,128]{1,0:T(8,128)(2,1)} %get-tuple-element.32), channel_id=1, source_target_pairs={{0,1},{3,2},{4,5},{7,6},{8,9},{11,10},{12,13},{15,14},{16,17},{19,... | collective-permute-start | bytes 1572872 | tf_op jit(solution)/shard_map/cond/branch_0_fun/ppermute | solution.py:243
  143.6 3.5 %branch_0_fun.24 = (bf16[2048,128]{1,0:T(8,128)(2,1)}, bf16[2048,128]{1,0:T(8,128)(2,1)}) custom-call(s32[2]{0:T(128)} %pad_add_fusion.zs, bf16[1,1,4194304]{2,1,0:T(2,128)(2,1)} %get-tuple-element.161.refs_0_.refs_1_, bf16[2048,128]{1,0:T(8,128)(2,1)} %collective-permute-done.1.refs_1_, bf16[2048,128]{1,0:T(8,128)(2,1)} %collective-permute-done.3.refs_2_), custom_call_target="tpu_custom_call" | custom-call | flops 4194304 | bytes 4194304 | tf_op jit(solution)/shard_map/cond/branch_0_fun/pallas_call | solution.py:164
  149.9 3.4 %branch_0_fun.36 = (f32[1,1048576]{1,0:T(1,128)}, bf16[1280,128]{1,0:T(8,128)(2,1)}, bf16[1280,128]{1,0:T(8,128)(2,1)}) custom-call(s32[2]{0:T(128)} %pad_add_fusion.zs, f32[2560,128]{1,0:T(8,128)} %get-tuple-element.55.refs_0_, bf16[2560,128]{1,0:T(8,128)(2,1)} %collective-permute-done.20.refs_1_), custom_call_target="tpu_custom_call" | custom-call | flops 4587520 | bytes 4587520 | tf_op jit(solution)/shard_map/cond/branch_0_fun/pallas_call | solution.py:164
  155.0 9.9 %collective-permute-done.5.refs_4_ = bf16[2048,128]{1,0:T(8,128)(2,1)} collective-permute-done((bf16[2048,128]{1,0:T(8,128)(2,1)}, bf16[2048,128]{1,0:T(8,128)(2,1)}, u32[]{:S(2)}, u32[]{:S(2)}) %collective-permute-start.5) | collective-permute-done | bytes 524320 | tf_op jit(solution)/shard_map/cond/branch_0_fun/ppermute | solution.py:243
  164.9 6.1 %branch_0_fun.35 = (f32[1,1048576]{1,0:T(1,128)}, f32[1,1048576]{1,0:T(1,128)}, f32[2048,128]{1,0:T(8,128)}, bf16[2048,128]{1,0:T(8,128)(2,1)}) custom-call(s32[2]{0:T(128)} %pad_add_fusion.zs, f32[2]{0:T(128)} %pad_maximum_fusion.refs_0_, bf16[1,1,4194304]{2,1,0:T(2,128)(2,1)} %get-tuple-element.161.refs_0_.refs_1_, ...), custom_call_target="tpu_custom_call", output_to_operand_aliasing={{0}: (9, {}), {1}: (10, {})} | custom-call | flops 10485760 | bytes 10485760 | tf_op jit(solution)/shard_map/cond/branch_0_fun/pallas_call | solution.py:164
  172.6 3.6 %branch_0_fun.37 = (f32[1,1048576]{1,0:T(1,128)}, bf16[1792,128]{1,0:T(8,128)(2,1)}, bf16[1792,128]{1,0:T(8,128)(2,1)}) custom-call(s32[2]{0:T(128)} %pad_add_fusion.zs, f32[3584,128]{1,0:T(8,128)} %get-tuple-element.53.refs_0_, bf16[3584,128]{1,0:T(8,128)(2,1)} %collective-permute-done.19.refs_1_, ...), custom_call_target="tpu_custom_call", output_to_operand_aliasing={{0}: (3, {})} | custom-call | flops 6422528 | bytes 6422528 | tf_op jit(solution)/shard_map/cond/branch_0_fun/pallas_call | solution.py:164
  176.1 2.7 %collective-permute-start.27 = (bf16[1792,128]{1,0:T(8,128)(2,1)}, bf16[1792,128]{1,0:T(8,128)(2,1)}, u32[]{:S(2)}, u32[]{:S(2)}) collective-permute-start(bf16[1792,128]{1,0:T(8,128)(2,1)} %get-tuple-element.64.refs_0_), channel_id=1, source_target_pairs={{0,1},{1,0},{2,3},{3,2},{4,5},{5,4},{6,7},{7,6},{8,9},{9,8},{10,11... | collective-permute-start | bytes 1376264 | tf_op jit(solution)/shard_map/cond/branch_0_fun/ppermute | solution.py:38
  184.9 13.5 %collective-permute-done.42.refs_6_ = bf16[1280,128]{1,0:T(8,128)(2,1)} collective-permute-done((bf16[1280,128]{1,0:T(8,128)(2,1)}, bf16[1280,128]{1,0:T(8,128)(2,1)}, u32[]{:S(2)}, u32[]{:S(2)}) %collective-permute-start.42) | collective-permute-done | bytes 327712 | tf_op jit(solution)/shard_map/cond/branch_0_fun/ppermute | solution.py:243
  198.3 1.9 collective-permute-start.43
  205.7 3.1 %branch_0_fun.38 = (f32[1,1048576]{1,0:T(1,128)}, bf16[1024,128]{1,0:T(8,128)(2,1)}, bf16[1024,128]{1,0:T(8,128)(2,1)}) custom-call(s32[2]{0:T(128)} %pad_add_fusion.zs, f32[2048,128]{1,0:T(8,128)} %get-tuple-element.51.refs_0_, bf16[2048,128]{1,0:T(8,128)(2,1)} %collective-permute-done.18.refs_1_, ...), custom_call_target="tpu_custom_call", output_to_operand_aliasing={{0}: (3, {})} | custom-call | flops 3670016 | bytes 3670016 | tf_op jit(solution)/shard_map/cond/branch_0_fun/pallas_call | solution.py:164
  208.9 2.6 collective-permute-start.25
  211.5 8.4 %collective-permute-done.45.refs_10_ = bf16[1280,128]{1,0:T(8,128)(2,1)} collective-permute-done((bf16[1280,128]{1,0:T(8,128)(2,1)}, bf16[1280,128]{1,0:T(8,128)(2,1)}, u32[]{:S(2)}, u32[]{:S(2)}) %collective-permute-start.45) | collective-permute-done | bytes 327712 | tf_op jit(solution)/shard_map/cond/branch_0_fun/ppermute | solution.py:243
  219.9 3.1 %collective-permute-start.21 = (bf16[1024,128]{1,0:T(8,128)(2,1)}, bf16[1024,128]{1,0:T(8,128)(2,1)}, u32[]{:S(2)}, u32[]{:S(2)}) collective-permute-start(bf16[1024,128]{1,0:T(8,128)(2,1)} %get-tuple-element.62.refs_0_), channel_id=1, source_target_pairs={{0,1},{1,0},{2,3},{3,2},{4,5},{5,4},{6,7},{7,6},{8,9},{9,8},{10,11... | collective-permute-start | bytes 786440 | tf_op jit(solution)/shard_map/cond/branch_0_fun/ppermute | solution.py:38
  224.3 1.9 collective-permute-start.46
  226.2 10.6 %collective-permute-done.23.refs_4_ = bf16[1024,128]{1,0:T(8,128)(2,1)} collective-permute-done((bf16[1024,128]{1,0:T(8,128)(2,1)}, bf16[1024,128]{1,0:T(8,128)(2,1)}, u32[]{:S(2)}, u32[]{:S(2)}) %collective-permute-start.23) | collective-permute-done | bytes 262176 | tf_op jit(solution)/shard_map/cond/branch_0_fun/ppermute | solution.py:38
  238.3 2.9 %collective-permute-done.21.refs_2_ = bf16[1024,128]{1,0:T(8,128)(2,1)} collective-permute-done((bf16[1024,128]{1,0:T(8,128)(2,1)}, bf16[1024,128]{1,0:T(8,128)(2,1)}, u32[]{:S(2)}, u32[]{:S(2)}) %collective-permute-start.21) | collective-permute-done | bytes 262176 | tf_op jit(solution)/shard_map/cond/branch_0_fun/ppermute | solution.py:38
  241.2 2.4 collective-permute-start.33
  245.1 5.5 %collective-permute-done.35.refs_10_ = bf16[1792,128]{1,0:T(8,128)(2,1)} collective-permute-done((bf16[1792,128]{1,0:T(8,128)(2,1)}, bf16[1792,128]{1,0:T(8,128)(2,1)}, u32[]{:S(2)}, u32[]{:S(2)}) %collective-permute-start.35) | collective-permute-done | bytes 458784 | tf_op jit(solution)/shard_map/cond/branch_0_fun/ppermute | solution.py:243
  250.5 1.9 collective-permute-start.36
  253.6 4.3 %branch_0_fun.39.refs_12_ = bf16[1,4194304]{1,0:T(2,128)(2,1)} custom-call(s32[2]{0:T(128)} %pad_add_fusion.zs, bf16[1280,128]{1,0:T(8,128)(2,1)} %get-tuple-element.66.refs_0_, bf16[1280,128]{1,0:T(8,128)(2,1)} %get-tuple-element.67.refs_1_, bf16[1280,128]{1,0:T(8,128)(2,1)} %collective-permute-done.37.refs_2_, ...), custom_call_target="tpu_custom_call" | custom-call | flops 7864320 | bytes 7864320 | tf_op jit(solution)/shard_map/cond/branch_0_fun/pallas_call | solution.py:164
  257.9 5.1 %branch_0_fun.40.refs_8_ = bf16[1,4194304]{1,0:T(2,128)(2,1)} custom-call(s32[2]{0:T(128)} %pad_add_fusion.zs, bf16[1792,128]{1,0:T(8,128)(2,1)} %get-tuple-element.64.refs_0_, bf16[1792,128]{1,0:T(8,128)(2,1)} %get-tuple-element.65.refs_1_, bf16[1792,128]{1,0:T(8,128)(2,1)} %collective-permute-done.27.refs_2_, ...), custom_call_target="tpu_custom_call", output_to_operand_aliasing={{}: (13, {})} | custom-call | flops 11010048 | bytes 11010048 | tf_op jit(solution)/shard_map/cond/branch_0_fun/pallas_call | solution.py:164
  263.1 3.9 %branch_0_fun.41 = bf16[1,4194304]{1,0:T(2,128)(2,1)} custom-call(s32[2]{0:T(128)} %pad_add_fusion.zs, bf16[1024,128]{1,0:T(8,128)(2,1)} %get-tuple-element.62.refs_0_, bf16[1024,128]{1,0:T(8,128)(2,1)} %get-tuple-element.63.refs_1_, bf16[1024,128]{1,0:T(8,128)(2,1)} %collective-permute-done.21.refs_2_, ...), custom_call_target="tpu_custom_call", output_to_operand_aliasing={{}: (9, {})} | custom-call | flops 6291456 | bytes 6291456 | tf_op jit(solution)/shard_map/cond/branch_0_fun/pallas_call | solution.py:164
  (70 shorter events, 34.8 us)
Async XLA Ops:
  4.9 26.0 %collective-permute-start.8 = (bf16[3584,128]{1,0:T(8,128)(2,1)}, bf16[3584,128]{1,0:T(8,128)(2,1)}, u32[]{:S(2)}, u32[]{:S(2)}) collective-permute-start(bf16[3584,128]{1,0:T(8,128)(2,1)} %branch_0_fun.26), channel_id=1, source_target_pairs={{0,1},{3,2},{4,5},{7,6},{8,9},{11,10},{12,13},{15,14},{16,17},{19,... | collective-permute-start | bytes 2752520 | tf_op jit(solution)/shard_map/cond/branch_0_fun/ppermute | solution.py:243
  13.7 31.3 %collective-permute-start.14 = (bf16[2560,128]{1,0:T(8,128)(2,1)}, bf16[2560,128]{1,0:T(8,128)(2,1)}, u32[]{:S(2)}, u32[]{:S(2)}) collective-permute-start(bf16[2560,128]{1,0:T(8,128)(2,1)} %branch_0_fun.30), channel_id=1, source_target_pairs={{0,1},{3,2},{4,5},{7,6},{8,9},{11,10},{12,13},{15,14},{16,17},{19,... | collective-permute-start | bytes 1966088 | tf_op jit(solution)/shard_map/cond/branch_0_fun/ppermute | solution.py:243
  19.1 40.5 %collective-permute-start.13 = (bf16[2560,128]{1,0:T(8,128)(2,1)}, bf16[2560,128]{1,0:T(8,128)(2,1)}, u32[]{:S(2)}, u32[]{:S(2)}) collective-permute-start(bf16[2560,128]{1,0:T(8,128)(2,1)} %get-tuple-element.44), channel_id=1, source_target_pairs={{0,1},{3,2},{4,5},{7,6},{8,9},{11,10},{12,13},{15,14},{16,17},{19,... | collective-permute-start | bytes 1966088 | tf_op jit(solution)/shard_map/cond/branch_0_fun/ppermute | solution.py:243
  24.8 53.8 %collective-permute-start.7 = (bf16[3584,128]{1,0:T(8,128)(2,1)}, bf16[3584,128]{1,0:T(8,128)(2,1)}, u32[]{:S(2)}, u32[]{:S(2)}) collective-permute-start(bf16[3584,128]{1,0:T(8,128)(2,1)} %get-tuple-element.40), channel_id=1, source_target_pairs={{0,1},{3,2},{4,5},{7,6},{8,9},{11,10},{12,13},{15,14},{16,17},{19,... | collective-permute-start | bytes 2752520 | tf_op jit(solution)/shard_map/cond/branch_0_fun/ppermute | solution.py:243
  34.3 45.6 %collective-permute-start.9 = (bf16[3584,128]{1,0:T(8,128)(2,1)}, bf16[3584,128]{1,0:T(8,128)(2,1)}, u32[]{:S(2)}, u32[]{:S(2)}) collective-permute-start(bf16[3584,128]{1,0:T(8,128)(2,1)} %branch_0_fun.27), channel_id=1, source_target_pairs={{1,2},{2,1},{5,6},{6,5},{9,10},{10,9},{13,14},{14,13},{17,18},{18,... | collective-permute-start | bytes 2752520 | tf_op jit(solution)/shard_map/cond/branch_0_fun/ppermute | solution.py:243
  48.2 16.0 %collective-permute-start.15 = (bf16[2560,128]{1,0:T(8,128)(2,1)}, bf16[2560,128]{1,0:T(8,128)(2,1)}, u32[]{:S(2)}, u32[]{:S(2)}) collective-permute-start(bf16[2560,128]{1,0:T(8,128)(2,1)} %branch_0_fun.31), channel_id=1, source_target_pairs={{1,2},{2,1},{5,6},{6,5},{9,10},{10,9},{13,14},{14,13},{17,18},{18,... | collective-permute-start | bytes 1966088 | tf_op jit(solution)/shard_map/cond/branch_0_fun/ppermute | solution.py:243
  49.7 55.8 %collective-permute-start.12 = (bf16[2560,128]{1,0:T(8,128)(2,1)}, bf16[2560,128]{1,0:T(8,128)(2,1)}, u32[]{:S(2)}, u32[]{:S(2)}) collective-permute-start(bf16[2560,128]{1,0:T(8,128)(2,1)} %get-tuple-element.43), channel_id=1, source_target_pairs={{0,1},{3,2},{4,5},{7,6},{8,9},{11,10},{12,13},{15,14},{16,17},{19,... | collective-permute-start | bytes 1966088 | tf_op jit(solution)/shard_map/cond/branch_0_fun/ppermute | solution.py:243
  59.6 44.3 %collective-permute-start.2 = (bf16[2048,128]{1,0:T(8,128)(2,1)}, bf16[2048,128]{1,0:T(8,128)(2,1)}, u32[]{:S(2)}, u32[]{:S(2)}) collective-permute-start(bf16[2048,128]{1,0:T(8,128)(2,1)} %branch_0_fun.22), channel_id=1, source_target_pairs={{0,1},{3,2},{4,5},{7,6},{8,9},{11,10},{12,13},{15,14},{16,17},{19,... | collective-permute-start | bytes 1572872 | tf_op jit(solution)/shard_map/cond/branch_0_fun/ppermute | solution.py:243
  68.1 44.8 %collective-permute-start.16 = (bf16[2560,128]{1,0:T(8,128)(2,1)}, bf16[2560,128]{1,0:T(8,128)(2,1)}, u32[]{:S(2)}, u32[]{:S(2)}) collective-permute-start(bf16[2560,128]{1,0:T(8,128)(2,1)} %get-tuple-element.45), channel_id=1, source_target_pairs={{1,2},{2,1},{5,6},{6,5},{9,10},{10,9},{13,14},{14,13},{17,18},{18,... | collective-permute-start | bytes 1966088 | tf_op jit(solution)/shard_map/cond/branch_0_fun/ppermute | solution.py:243
  78.6 42.3 %collective-permute-start.17 = (bf16[2560,128]{1,0:T(8,128)(2,1)}, bf16[2560,128]{1,0:T(8,128)(2,1)}, u32[]{:S(2)}, u32[]{:S(2)}) collective-permute-start(bf16[2560,128]{1,0:T(8,128)(2,1)} %get-tuple-element.46), channel_id=1, source_target_pairs={{1,0},{2,3},{5,4},{6,7},{9,8},{10,11},{13,12},{14,15},{17,16},{18,... | collective-permute-start | bytes 1966088 | tf_op jit(solution)/shard_map/cond/branch_0_fun/ppermute | solution.py:243
  79.9 50.8 %collective-permute-start.6 = (bf16[3584,128]{1,0:T(8,128)(2,1)}, bf16[3584,128]{1,0:T(8,128)(2,1)}, u32[]{:S(2)}, u32[]{:S(2)}) collective-permute-start(bf16[3584,128]{1,0:T(8,128)(2,1)} %get-tuple-element.39), channel_id=1, source_target_pairs={{0,1},{3,2},{4,5},{7,6},{8,9},{11,10},{12,13},{15,14},{16,17},{19,... | collective-permute-start | bytes 2752520 | tf_op jit(solution)/shard_map/cond/branch_0_fun/ppermute | solution.py:243
  103.9 26.9 %collective-permute-start.10 = (bf16[3584,128]{1,0:T(8,128)(2,1)}, bf16[3584,128]{1,0:T(8,128)(2,1)}, u32[]{:S(2)}, u32[]{:S(2)}) collective-permute-start(bf16[3584,128]{1,0:T(8,128)(2,1)} %get-tuple-element.41), channel_id=1, source_target_pairs={{1,2},{2,1},{5,6},{6,5},{9,10},{10,9},{13,14},{14,13},{17,18},{18,... | collective-permute-start | bytes 2752520 | tf_op jit(solution)/shard_map/cond/branch_0_fun/ppermute | solution.py:243
  105.5 25.4 %collective-permute-start.11 = (bf16[3584,128]{1,0:T(8,128)(2,1)}, bf16[3584,128]{1,0:T(8,128)(2,1)}, u32[]{:S(2)}, u32[]{:S(2)}) collective-permute-start(bf16[3584,128]{1,0:T(8,128)(2,1)} %get-tuple-element.42), channel_id=1, source_target_pairs={{1,0},{2,3},{5,4},{6,7},{9,8},{10,11},{13,12},{14,15},{17,16},{18,... | collective-permute-start | bytes 2752520 | tf_op jit(solution)/shard_map/cond/branch_0_fun/ppermute | solution.py:243
  112.9 30.8 %collective-permute-start.1 = (bf16[2048,128]{1,0:T(8,128)(2,1)}, bf16[2048,128]{1,0:T(8,128)(2,1)}, u32[]{:S(2)}, u32[]{:S(2)}) collective-permute-start(bf16[2048,128]{1,0:T(8,128)(2,1)} %get-tuple-element.33), channel_id=1, source_target_pairs={{0,1},{3,2},{4,5},{7,6},{8,9},{11,10},{12,13},{15,14},{16,17},{19,... | collective-permute-start | bytes 1572872 | tf_op jit(solution)/shard_map/cond/branch_0_fun/ppermute | solution.py:243
  121.0 22.7 %collective-permute-start.3 = (bf16[2048,128]{1,0:T(8,128)(2,1)}, bf16[2048,128]{1,0:T(8,128)(2,1)}, u32[]{:S(2)}, u32[]{:S(2)}) collective-permute-start(bf16[2048,128]{1,0:T(8,128)(2,1)} %branch_0_fun.23), channel_id=1, source_target_pairs={{1,2},{2,1},{5,6},{6,5},{9,10},{10,9},{13,14},{14,13},{17,18},{18,... | collective-permute-start | bytes 1572872 | tf_op jit(solution)/shard_map/cond/branch_0_fun/ppermute | solution.py:243
  130.8 19.2 %collective-permute-start.20 = (bf16[2560,128]{1,0:T(8,128)(2,1)}, bf16[2560,128]{1,0:T(8,128)(2,1)}, u32[]{:S(2)}, u32[]{:S(2)}) collective-permute-start(bf16[2560,128]{1,0:T(8,128)(2,1)} %get-tuple-element.56), channel_id=1, source_target_pairs={{0,4},{4,0},{8,12},{12,8},{16,20},{20,16},{24,28},{28,24},{1,5},{5... | collective-permute-start | bytes 1966088 | tf_op jit(solution)/shard_map/cond/branch_0_fun/ppermute | solution.py:26
  139.9 32.7 %collective-permute-start.19 = (bf16[3584,128]{1,0:T(8,128)(2,1)}, bf16[3584,128]{1,0:T(8,128)(2,1)}, u32[]{:S(2)}, u32[]{:S(2)}) collective-permute-start(bf16[3584,128]{1,0:T(8,128)(2,1)} %get-tuple-element.54), channel_id=1, source_target_pairs={{0,4},{4,0},{8,12},{12,8},{16,20},{20,16},{24,28},{28,24},{1,5},{5... | collective-permute-start | bytes 2752520 | tf_op jit(solution)/shard_map/cond/branch_0_fun/ppermute | solution.py:26
  140.4 14.5 %collective-permute-start = (bf16[2048,128]{1,0:T(8,128)(2,1)}, bf16[2048,128]{1,0:T(8,128)(2,1)}, u32[]{:S(2)}, u32[]{:S(2)}) collective-permute-start(bf16[2048,128]{1,0:T(8,128)(2,1)} %get-tuple-element.32), channel_id=1, source_target_pairs={{0,1},{3,2},{4,5},{7,6},{8,9},{11,10},{12,13},{15,14},{16,17},{19,... | collective-permute-start | bytes 1572872 | tf_op jit(solution)/shard_map/cond/branch_0_fun/ppermute | solution.py:243
  147.2 7.8 %collective-permute-start.4 = (bf16[2048,128]{1,0:T(8,128)(2,1)}, bf16[2048,128]{1,0:T(8,128)(2,1)}, u32[]{:S(2)}, u32[]{:S(2)}) collective-permute-start(bf16[2048,128]{1,0:T(8,128)(2,1)} %get-tuple-element.34), channel_id=1, source_target_pairs={{1,2},{2,1},{5,6},{6,5},{9,10},{10,9},{13,14},{14,13},{17,18},{18,... | collective-permute-start | bytes 1572872 | tf_op jit(solution)/shard_map/cond/branch_0_fun/ppermute | solution.py:243
  148.6 16.2 %collective-permute-start.5 = (bf16[2048,128]{1,0:T(8,128)(2,1)}, bf16[2048,128]{1,0:T(8,128)(2,1)}, u32[]{:S(2)}, u32[]{:S(2)}) collective-permute-start(bf16[2048,128]{1,0:T(8,128)(2,1)} %get-tuple-element.35), channel_id=1, source_target_pairs={{1,0},{2,3},{5,4},{6,7},{9,8},{10,11},{13,12},{14,15},{17,16},{18,... | collective-permute-start | bytes 1572872 | tf_op jit(solution)/shard_map/cond/branch_0_fun/ppermute | solution.py:243
  153.3 17.9 %collective-permute-start.41 = (bf16[1280,128]{1,0:T(8,128)(2,1)}, bf16[1280,128]{1,0:T(8,128)(2,1)}, u32[]{:S(2)}, u32[]{:S(2)}) collective-permute-start(bf16[1280,128]{1,0:T(8,128)(2,1)} %get-tuple-element.66.refs_0_), channel_id=1, source_target_pairs={{1,2},{2,1},{5,6},{6,5},{9,10},{10,9},{13,14},{14,13},{17,18},{18,... | collective-permute-start | bytes 983048 | tf_op jit(solution)/shard_map/cond/branch_0_fun/ppermute | solution.py:243
  171.0 12.4 %collective-permute-start.18 = (bf16[2048,128]{1,0:T(8,128)(2,1)}, bf16[2048,128]{1,0:T(8,128)(2,1)}, u32[]{:S(2)}, u32[]{:S(2)}) collective-permute-start(bf16[2048,128]{1,0:T(8,128)(2,1)} %get-tuple-element.52), channel_id=1, source_target_pairs={{0,4},{4,0},{8,12},{12,8},{16,20},{20,16},{24,28},{28,24},{1,5},{5... | collective-permute-start | bytes 1572872 | tf_op jit(solution)/shard_map/cond/branch_0_fun/ppermute | solution.py:26
  171.1 11.0 %collective-permute-start.37 = (bf16[1280,128]{1,0:T(8,128)(2,1)}, bf16[1280,128]{1,0:T(8,128)(2,1)}, u32[]{:S(2)}, u32[]{:S(2)}) collective-permute-start(bf16[1280,128]{1,0:T(8,128)(2,1)} %get-tuple-element.66.refs_0_), channel_id=1, source_target_pairs={{0,1},{1,0},{2,3},{3,2},{4,5},{5,4},{6,7},{7,6},{8,9},{9,8},{10,11... | collective-permute-start | bytes 983048 | tf_op jit(solution)/shard_map/cond/branch_0_fun/ppermute | solution.py:38
  171.2 12.3 %collective-permute-start.44 = (bf16[1280,128]{1,0:T(8,128)(2,1)}, bf16[1280,128]{1,0:T(8,128)(2,1)}, u32[]{:S(2)}, u32[]{:S(2)}) collective-permute-start(bf16[1280,128]{1,0:T(8,128)(2,1)} %collective-permute-done.41.refs_8_), channel_id=1, source_target_pairs={{1,5},{2,6},{5,1},{6,2},{9,13},{10,14},{13,9},{14,10},{17,21},{18,... | collective-permute-start | bytes 983048 | tf_op jit(solution)/shard_map/cond/branch_0_fun/ppermute | solution.py:34
  176.1 24.1 %collective-permute-start.27 = (bf16[1792,128]{1,0:T(8,128)(2,1)}, bf16[1792,128]{1,0:T(8,128)(2,1)}, u32[]{:S(2)}, u32[]{:S(2)}) collective-permute-start(bf16[1792,128]{1,0:T(8,128)(2,1)} %get-tuple-element.64.refs_0_), channel_id=1, source_target_pairs={{0,1},{1,0},{2,3},{3,2},{4,5},{5,4},{6,7},{7,6},{8,9},{9,8},{10,11... | collective-permute-start | bytes 1376264 | tf_op jit(solution)/shard_map/cond/branch_0_fun/ppermute | solution.py:38
  178.9 19.5 %collective-permute-start.42 = (bf16[1280,128]{1,0:T(8,128)(2,1)}, bf16[1280,128]{1,0:T(8,128)(2,1)}, u32[]{:S(2)}, u32[]{:S(2)}) collective-permute-start(bf16[1280,128]{1,0:T(8,128)(2,1)} %collective-permute-done.41.refs_8_), channel_id=1, source_target_pairs={{1,0},{2,3},{5,4},{6,7},{9,8},{10,11},{13,12},{14,15},{17,16},{18,... | collective-permute-start | bytes 983048 | tf_op jit(solution)/shard_map/cond/branch_0_fun/ppermute | solution.py:243
  182.0 19.7 %collective-permute-start.39 = (bf16[1280,128]{1,0:T(8,128)(2,1)}, bf16[1280,128]{1,0:T(8,128)(2,1)}, u32[]{:S(2)}, u32[]{:S(2)}) collective-permute-start(bf16[1280,128]{1,0:T(8,128)(2,1)} %collective-permute-done.37.refs_2_), channel_id=1, source_target_pairs={{1,2},{2,1},{5,6},{6,5},{9,10},{10,9},{13,14},{14,13},{17,18},{18,... | collective-permute-start | bytes 983048 | tf_op jit(solution)/shard_map/cond/branch_0_fun/ppermute | solution.py:243
  183.4 19.6 %collective-permute-start.38 = (bf16[1280,128]{1,0:T(8,128)(2,1)}, bf16[1280,128]{1,0:T(8,128)(2,1)}, u32[]{:S(2)}, u32[]{:S(2)}) collective-permute-start(bf16[1280,128]{1,0:T(8,128)(2,1)} %collective-permute-done.37.refs_2_), channel_id=1, source_target_pairs={{0,4},{1,5},{2,6},{3,7},{4,0},{5,1},{6,2},{7,3},{8,12},{9,13},{10,... | collective-permute-start | bytes 983048 | tf_op jit(solution)/shard_map/cond/branch_0_fun/ppermute | solution.py:34
  183.4 21.0 %collective-permute-start.31 = (bf16[1792,128]{1,0:T(8,128)(2,1)}, bf16[1792,128]{1,0:T(8,128)(2,1)}, u32[]{:S(2)}, u32[]{:S(2)}) collective-permute-start(bf16[1792,128]{1,0:T(8,128)(2,1)} %get-tuple-element.64.refs_0_), channel_id=1, source_target_pairs={{1,2},{2,1},{5,6},{6,5},{9,10},{10,9},{13,14},{14,13},{17,18},{18,... | collective-permute-start | bytes 1376264 | tf_op jit(solution)/shard_map/cond/branch_0_fun/ppermute | solution.py:243
  198.3 10.5 %collective-permute-start.43 = (bf16[1280,128]{1,0:T(8,128)(2,1)}, bf16[1280,128]{1,0:T(8,128)(2,1)}, u32[]{:S(2)}, u32[]{:S(2)}) collective-permute-start(bf16[1280,128]{1,0:T(8,128)(2,1)} %collective-permute-done.42.refs_6_), channel_id=1, source_target_pairs={{0,4},{3,7},{4,0},{7,3},{8,12},{11,15},{12,8},{15,11},{16,20},{19,... | collective-permute-start | bytes 983048 | tf_op jit(solution)/shard_map/cond/branch_0_fun/ppermute | solution.py:34
  200.3 22.7 %collective-permute-start.29 = (bf16[1792,128]{1,0:T(8,128)(2,1)}, bf16[1792,128]{1,0:T(8,128)(2,1)}, u32[]{:S(2)}, u32[]{:S(2)}) collective-permute-start(bf16[1792,128]{1,0:T(8,128)(2,1)} %collective-permute-done.27.refs_2_), channel_id=1, source_target_pairs={{1,2},{2,1},{5,6},{6,5},{9,10},{10,9},{13,14},{14,13},{17,18},{18,... | collective-permute-start | bytes 1376264 | tf_op jit(solution)/shard_map/cond/branch_0_fun/ppermute | solution.py:243
  201.7 18.2 %collective-permute-start.45 = (bf16[1280,128]{1,0:T(8,128)(2,1)}, bf16[1280,128]{1,0:T(8,128)(2,1)}, u32[]{:S(2)}, u32[]{:S(2)}) collective-permute-start(bf16[1280,128]{1,0:T(8,128)(2,1)} %collective-permute-done.39.refs_4_), channel_id=1, source_target_pairs={{1,0},{2,3},{5,4},{6,7},{9,8},{10,11},{13,12},{14,15},{17,16},{18,... | collective-permute-start | bytes 983048 | tf_op jit(solution)/shard_map/cond/branch_0_fun/ppermute | solution.py:243
  203.0 16.9 %collective-permute-start.40 = (bf16[1280,128]{1,0:T(8,128)(2,1)}, bf16[1280,128]{1,0:T(8,128)(2,1)}, u32[]{:S(2)}, u32[]{:S(2)}) collective-permute-start(bf16[1280,128]{1,0:T(8,128)(2,1)} %collective-permute-done.39.refs_4_), channel_id=1, source_target_pairs={{1,5},{2,6},{5,1},{6,2},{9,13},{10,14},{13,9},{14,10},{17,21},{18,... | collective-permute-start | bytes 983048 | tf_op jit(solution)/shard_map/cond/branch_0_fun/ppermute | solution.py:34
  204.4 36.8 %collective-permute-start.32 = (bf16[1792,128]{1,0:T(8,128)(2,1)}, bf16[1792,128]{1,0:T(8,128)(2,1)}, u32[]{:S(2)}, u32[]{:S(2)}) collective-permute-start(bf16[1792,128]{1,0:T(8,128)(2,1)} %collective-permute-done.31.refs_8_), channel_id=1, source_target_pairs={{1,0},{2,3},{5,4},{6,7},{9,8},{10,11},{13,12},{14,15},{17,16},{18,... | collective-permute-start | bytes 1376264 | tf_op jit(solution)/shard_map/cond/branch_0_fun/ppermute | solution.py:243
  208.9 15.4 %collective-permute-start.25 = (bf16[1024,128]{1,0:T(8,128)(2,1)}, bf16[1024,128]{1,0:T(8,128)(2,1)}, u32[]{:S(2)}, u32[]{:S(2)}) collective-permute-start(bf16[1024,128]{1,0:T(8,128)(2,1)} %get-tuple-element.62.refs_0_), channel_id=1, source_target_pairs={{0,3},{1,2},{2,1},{3,0},{4,7},{5,6},{6,5},{7,4},{8,11},{9,10},{10,... | collective-permute-start | bytes 786440 | tf_op jit(solution)/shard_map/cond/branch_0_fun/ppermute | solution.py:38
  219.9 16.9 %collective-permute-start.23 = (bf16[1024,128]{1,0:T(8,128)(2,1)}, bf16[1024,128]{1,0:T(8,128)(2,1)}, u32[]{:S(2)}, u32[]{:S(2)}) collective-permute-start(bf16[1024,128]{1,0:T(8,128)(2,1)} %get-tuple-element.62.refs_0_), channel_id=1, source_target_pairs={{0,2},{1,3},{2,0},{3,1},{4,6},{5,7},{6,4},{7,5},{8,10},{9,11},{10,... | collective-permute-start | bytes 786440 | tf_op jit(solution)/shard_map/cond/branch_0_fun/ppermute | solution.py:38
  219.9 21.3 %collective-permute-start.21 = (bf16[1024,128]{1,0:T(8,128)(2,1)}, bf16[1024,128]{1,0:T(8,128)(2,1)}, u32[]{:S(2)}, u32[]{:S(2)}) collective-permute-start(bf16[1024,128]{1,0:T(8,128)(2,1)} %get-tuple-element.62.refs_0_), channel_id=1, source_target_pairs={{0,1},{1,0},{2,3},{3,2},{4,5},{5,4},{6,7},{7,6},{8,9},{9,8},{10,11... | collective-permute-start | bytes 786440 | tf_op jit(solution)/shard_map/cond/branch_0_fun/ppermute | solution.py:38
  223.0 27.5 %collective-permute-start.35 = (bf16[1792,128]{1,0:T(8,128)(2,1)}, bf16[1792,128]{1,0:T(8,128)(2,1)}, u32[]{:S(2)}, u32[]{:S(2)}) collective-permute-start(bf16[1792,128]{1,0:T(8,128)(2,1)} %collective-permute-done.29.refs_4_), channel_id=1, source_target_pairs={{1,0},{2,3},{5,4},{6,7},{9,8},{10,11},{13,12},{14,15},{17,16},{18,... | collective-permute-start | bytes 1376264 | tf_op jit(solution)/shard_map/cond/branch_0_fun/ppermute | solution.py:243
  224.3 19.3 %collective-permute-start.46 = (bf16[1280,128]{1,0:T(8,128)(2,1)}, bf16[1280,128]{1,0:T(8,128)(2,1)}, u32[]{:S(2)}, u32[]{:S(2)}) collective-permute-start(bf16[1280,128]{1,0:T(8,128)(2,1)} %collective-permute-done.45.refs_10_), channel_id=1, source_target_pairs={{0,4},{3,7},{4,0},{7,3},{8,12},{11,15},{12,8},{15,11},{16,20},{19,... | collective-permute-start | bytes 983048 | tf_op jit(solution)/shard_map/cond/branch_0_fun/ppermute | solution.py:34
  236.8 15.7 %collective-permute-start.34 = (bf16[1792,128]{1,0:T(8,128)(2,1)}, bf16[1792,128]{1,0:T(8,128)(2,1)}, u32[]{:S(2)}, u32[]{:S(2)}) collective-permute-start(bf16[1792,128]{1,0:T(8,128)(2,1)} %collective-permute-done.31.refs_8_), channel_id=1, source_target_pairs={{1,5},{2,6},{5,1},{6,2},{9,13},{10,14},{13,9},{14,10},{17,21},{18,... | collective-permute-start | bytes 1376264 | tf_op jit(solution)/shard_map/cond/branch_0_fun/ppermute | solution.py:34
  241.2 11.9 %collective-permute-start.28 = (bf16[1792,128]{1,0:T(8,128)(2,1)}, bf16[1792,128]{1,0:T(8,128)(2,1)}, u32[]{:S(2)}, u32[]{:S(2)}) collective-permute-start(bf16[1792,128]{1,0:T(8,128)(2,1)} %collective-permute-done.27.refs_2_), channel_id=1, source_target_pairs={{0,4},{1,5},{2,6},{3,7},{4,0},{5,1},{6,2},{7,3},{8,12},{9,13},{10,... | collective-permute-start | bytes 1376264 | tf_op jit(solution)/shard_map/cond/branch_0_fun/ppermute | solution.py:34
  241.2 11.9 %collective-permute-start.33 = (bf16[1792,128]{1,0:T(8,128)(2,1)}, bf16[1792,128]{1,0:T(8,128)(2,1)}, u32[]{:S(2)}, u32[]{:S(2)}) collective-permute-start(bf16[1792,128]{1,0:T(8,128)(2,1)} %collective-permute-done.32.refs_6_), channel_id=1, source_target_pairs={{0,4},{3,7},{4,0},{7,3},{8,12},{11,15},{12,8},{15,11},{16,20},{19,... | collective-permute-start | bytes 1376264 | tf_op jit(solution)/shard_map/cond/branch_0_fun/ppermute | solution.py:34
  243.6 14.3 %collective-permute-start.30 = (bf16[1792,128]{1,0:T(8,128)(2,1)}, bf16[1792,128]{1,0:T(8,128)(2,1)}, u32[]{:S(2)}, u32[]{:S(2)}) collective-permute-start(bf16[1792,128]{1,0:T(8,128)(2,1)} %collective-permute-done.29.refs_4_), channel_id=1, source_target_pairs={{1,5},{2,6},{5,1},{6,2},{9,13},{10,14},{13,9},{14,10},{17,21},{18,... | collective-permute-start | bytes 1376264 | tf_op jit(solution)/shard_map/cond/branch_0_fun/ppermute | solution.py:34
  250.5 7.4 %collective-permute-start.36 = (bf16[1792,128]{1,0:T(8,128)(2,1)}, bf16[1792,128]{1,0:T(8,128)(2,1)}, u32[]{:S(2)}, u32[]{:S(2)}) collective-permute-start(bf16[1792,128]{1,0:T(8,128)(2,1)} %collective-permute-done.35.refs_10_), channel_id=1, source_target_pairs={{0,4},{3,7},{4,0},{7,3},{8,12},{11,15},{12,8},{15,11},{16,20},{19,... | collective-permute-start | bytes 1376264 | tf_op jit(solution)/shard_map/cond/branch_0_fun/ppermute | solution.py:34
  252.5 10.6 %collective-permute-start.26 = (bf16[1024,128]{1,0:T(8,128)(2,1)}, bf16[1024,128]{1,0:T(8,128)(2,1)}, u32[]{:S(2)}, u32[]{:S(2)}) collective-permute-start(bf16[1024,128]{1,0:T(8,128)(2,1)} %collective-permute-done.25.refs_6_), channel_id=1, source_target_pairs={{0,4},{1,5},{2,6},{3,7},{4,0},{5,1},{6,2},{7,3},{8,12},{9,13},{10,... | collective-permute-start | bytes 786440 | tf_op jit(solution)/shard_map/cond/branch_0_fun/ppermute | solution.py:34
  253.0 10.0 %collective-permute-start.24 = (bf16[1024,128]{1,0:T(8,128)(2,1)}, bf16[1024,128]{1,0:T(8,128)(2,1)}, u32[]{:S(2)}, u32[]{:S(2)}) collective-permute-start(bf16[1024,128]{1,0:T(8,128)(2,1)} %collective-permute-done.23.refs_4_), channel_id=1, source_target_pairs={{0,4},{1,5},{2,6},{3,7},{4,0},{5,1},{6,2},{7,3},{8,12},{9,13},{10,... | collective-permute-start | bytes 786440 | tf_op jit(solution)/shard_map/cond/branch_0_fun/ppermute | solution.py:34
  253.1 10.0 %collective-permute-start.22 = (bf16[1024,128]{1,0:T(8,128)(2,1)}, bf16[1024,128]{1,0:T(8,128)(2,1)}, u32[]{:S(2)}, u32[]{:S(2)}) collective-permute-start(bf16[1024,128]{1,0:T(8,128)(2,1)} %collective-permute-done.21.refs_2_), channel_id=1, source_target_pairs={{0,4},{1,5},{2,6},{3,7},{4,0},{5,1},{6,2},{7,3},{8,12},{9,13},{10,... | collective-permute-start | bytes 786440 | tf_op jit(solution)/shard_map/cond/branch_0_fun/ppermute | solution.py:34
